TPU v7x, 32 devices: a whole 2x2x4 slice. The times are simulated.
32 devices in a mesh: row: 8 (over y, x, core), col: 4 (over z).
Axes of the slice: x: 2, y: 2, z: 4, core: 2. Of those that a mesh axis runs over, the one named last changes fastest.
Arguments:
- frames: bfloat16 [8192, 1536], P(('row', 'col')), may hold values from -6 to 6
- text_states: bfloat16 [8, 64, 1536], P(None, 'row', 'col'), may hold values from -6 to 6
- clip_ids: int32 [8192], P('row'), may hold values from 0 to 7, never falling along the last dimension, each value on 1 to 1500 neighbouring positions
- valid_mask: int32 [8192], P('row'), may hold values from 0 to 1, as said below
- teacher_states: bfloat16 [8192, 1536], P(('row', 'col')), may hold values from -6 to 6
- self_norm_gain: float32 [1536], replicated, may hold values from 0.5 to 1.5
- self_norm_bias: float32 [1536], replicated, may hold values from -3 to 3
- cross_norm_gain: float32 [1536], replicated, may hold values from 0.5 to 1.5
- cross_norm_bias: float32 [1536], replicated, may hold values from -3 to 3
- final_norm_gain: float32 [1536], replicated, may hold values from 0.5 to 1.5
- final_norm_bias: float32 [1536], replicated, may hold values from -3 to 3
- self_query: bfloat16 [1536, 1536], P('row', 'col'), may hold values from -0.15625 to 0.15625
- self_key: bfloat16 [1536, 1536], P('row', 'col'), may hold values from -0.15625 to 0.15625
- self_value: bfloat16 [1536, 1536], P('row', 'col'), may hold values from -0.15625 to 0.15625
- self_output: bfloat16 [1536, 1536], P('col', 'row'), may hold values from -1.25 to 1.25
- cross_query: bfloat16 [1536, 1536], P('row', 'col'), may hold values from -0.15625 to 0.15625
- cross_key: bfloat16 [1536, 1536], P('row', 'col'), may hold values from -0.15625 to 0.15625
- cross_value: bfloat16 [1536, 1536], P('row', 'col'), may hold values from -0.15625 to 0.15625
- cross_output: bfloat16 [1536, 1536], P('col', 'row'), may hold values from -0.625 to 0.625
- expand_weight: bfloat16 [1536, 6144], P('row', 'col'), may hold values from -0.15625 to 0.15625
- reduce_weight: bfloat16 [6144, 1536], P('col', 'row'), may hold values from -0.078125 to 0.078125
Outputs:
- layer_out: bfloat16 [8192, 1536], P(('row', 'col'))
- loss: float32 [], replicated
- grad_input: float32 [8192, 1536], P(('row', 'col'))
- grad_text: float32 [8, 64, 1536], P(None, 'row', 'col')
- grad_self_norm_gain: float32 [1536], replicated
- grad_self_norm_bias: float32 [1536], replicated
- grad_cross_norm_gain: float32 [1536], replicated
- grad_cross_norm_bias: float32 [1536], replicated
- grad_final_norm_gain: float32 [1536], replicated
- grad_final_norm_bias: float32 [1536], replicated
- grad_self_query: float32 [1536, 1536], P('row', 'col')
- grad_self_key: float32 [1536, 1536], P('row', 'col')
- grad_self_value: float32 [1536, 1536], P('row', 'col')
- grad_self_output: float32 [1536, 1536], P('col', 'row')
- grad_cross_query: float32 [1536, 1536], P('row', 'col')
- grad_cross_key: float32 [1536, 1536], P('row', 'col')
- grad_cross_value: float32 [1536, 1536], P('row', 'col')
- grad_cross_output: float32 [1536, 1536], P('col', 'row')
- grad_expand_weight: float32 [1536, 6144], P('row', 'col')
- grad_reduce_weight: float32 [6144, 1536], P('col', 'row')
Inputs may be any that keep to these rules, and one draw needn't show every extreme that they name: `clip_ids`: clip numbers never fall along the tokens; each clip holds 1 to 1500 tokens, one exactly 1500. `valid_mask`: the first token is valid.
All inputs are finite; a program needn't handle non-finite values.
Results may differ from a plain program's by a relative error of at most 0.014.
Values may be sent and summed in bfloat16 or wider, within the bound.
A program may use at most 256 MiB of HBM per device.

v0:
```python
from functools import partial

import jax
import jax.numpy as jnp
from jax import lax
from jax.experimental import pallas as pl
from jax.experimental.pallas import tpu as pltpu
from jax.sharding import PartitionSpec as P

HD = 64
CLIP = 1500
LANES = 128
TILE = 256
MESH = pl.DeviceIdType.MESH

eps_norm = 1e-05
masked_score = -1e30
scale = HD**-0.5
f32 = jnp.float32
bf16 = jnp.bfloat16
ANY = pl.BlockSpec(memory_space=pl.ANY)
VMEM = pl.BlockSpec(memory_space=pltpu.VMEM)
CHEAP = pl.CostEstimate(flops=1 << 20, bytes_accessed=1 << 20, transcendentals=0)


def matmul(left, right):
    return jnp.dot(left, right, preferred_element_type=f32)


def against(left, right):
    return lax.dot_general(left, right, (((1,), (1,)), ((), ())), preferred_element_type=f32)


def transposed(left, right):
    return lax.dot_general(left, right, (((0,), (0,)), ((), ())), preferred_element_type=f32)


def normalize(hidden, gain, shift):
    values = hidden.astype(f32)
    centre = values - jnp.mean(values, axis=1, keepdims=True)
    inverse = lax.rsqrt(jnp.mean(centre * centre, axis=1, keepdims=True) + eps_norm)
    unit = centre * inverse
    return ((unit * gain + shift).astype(bf16), unit, inverse)


def normalize_back(grad_normed, unit, inverse, gain):
    scaled = grad_normed * gain
    inner = (
        scaled
        - jnp.mean(scaled, axis=1, keepdims=True)
        - unit * jnp.mean(scaled * unit, axis=1, keepdims=True)
    )
    return (inner * inverse, jnp.sum(grad_normed * unit, axis=0), jnp.sum(grad_normed, axis=0))


def reach_parts(tokens, halo):
    parts, left = [], halo
    while left > 0:
        parts.append(min(tokens, left))
        left -= tokens
    return parts


def place():
    return lax.axis_index("row"), lax.axis_index("col")


def greet(barrier, row, col):
    pl.semaphore_signal(barrier, inc=1, device_id=(row, col), device_id_type=MESH)


def push(src, dst, send, recv, row, col):
    return pltpu.make_async_remote_copy(
        src, dst, send, recv, device_id=(row, col), device_id_type=MESH
    )


def dma(count):
    return pltpu.SemaphoreType.DMA((count,))


def shape_of(x, shape):
    return jax.ShapeDtypeStruct(shape, x.dtype)


class LineGather:
    def __init__(self, x, n):
        self.n = n
        self.ins, self.in_specs = [x], [ANY]
        self.outs, self.out_specs = [shape_of(x, (n,) + x.shape)], [ANY]
        self.scratch = [pltpu.VMEM(x.shape, x.dtype)] + [dma(1)] + [dma(n)] * 4

    def greet(self, barrier):
        (row, me), n = place(), self.n

        @pl.when(me < n - 1)
        def _():
            greet(barrier, row, lax.rem(me + 1, n))

        @pl.when(me > 0)
        def _():
            greet(barrier, row, lax.rem(me + n - 1, n))

        return jnp.minimum(me, 1) + jnp.minimum(n - 1 - me, 1)

    def copies(self, refs):
        x, out, held, load, send_r, recv_r, send_l, recv_l = refs
        (row, me), n = place(), self.n

        def right(src, owner, step):
            to = lax.rem(me + 1, n)
            return push(src, out.at[owner], send_r.at[step], recv_r.at[step], row, to)

        def left(src, owner, step):
            to = lax.rem(me + n - 1, n)
            return push(src, out.at[owner], send_l.at[step], recv_l.at[step], row, to)

        return right, left

    def begin(self, refs):
        x, out, held, load = refs[:4]
        me, n = place()[1], self.n
        right, left = self.copies(refs)

        @pl.when(me < n - 1)
        def _():
            right(x, me, 0).start()

        @pl.when(me > 0)
        def _():
            left(x, me, 0).start()

        own = pltpu.make_async_copy(x, held, load.at[0])
        own.start()
        own.wait()
        pltpu.make_async_copy(held, out.at[me], load.at[0]).start()

    def run(self, refs):
        x, out = refs[:2]
        me, n = place()[1], self.n
        right, left = self.copies(refs)
        for step in range(n - 1):
            before, later = me - 1 - step, me + 1 + step

            @pl.when(before >= 0)
            def _():
                right(x, me, step).wait_recv()

            @pl.when((before >= 0) & (me < n - 1))
            def _():
                owner = jnp.maximum(before, 0)
                right(out.at[owner], owner, step + 1).start()

            @pl.when(later < n)
            def _():
                left(x, me, step).wait_recv()

            @pl.when((later < n) & (me > 0))
            def _():
                owner = jnp.minimum(later, n - 1)
                left(out.at[owner], owner, step + 1).start()

    def end(self, refs):
        x, out, held, load = refs[:4]
        me, n = place()[1], self.n
        right, left = self.copies(refs)
        for step in range(n):

            @pl.when((me < n - 1) & (me - step >= 0))
            def _():
                right(x, me, step).wait_send()

            @pl.when((me > 0) & (me + step < n))
            def _():
                left(x, me, step).wait_send()

        pltpu.make_async_copy(held, out.at[me], load.at[0]).wait()


class LineScatter:
    def __init__(self, x, n):
        rows, width = x.shape
        block = rows // n
        self.n = n
        self.ins, self.in_specs = [x.reshape(n, block, width)], [ANY]
        self.outs = [jax.ShapeDtypeStruct((block, width), f32)]
        self.out_specs = [VMEM]
        self.scratch = [pltpu.VMEM((n, block, width), bf16)] * 3 + [dma(n)] * 5

    greet = LineGather.greet

    def copies(self, refs):
        x, out, mine, from_l, from_r, loads, send_r, recv_r, send_l, recv_l = refs
        (row, me), n = place(), self.n

        def right(d):
            to = lax.rem(me + 1, n)
            return push(mine.at[d], from_l.at[d], send_r.at[d], recv_r.at[d], row, to)

        def left(d):
            to = lax.rem(me + n - 1, n)
            return push(mine.at[d], from_r.at[d], send_l.at[d], recv_l.at[d], row, to)

        def load(d):
            return pltpu.make_async_copy(x.at[d], mine.at[d], loads.at[d])

        return right, left, load

    def begin(self, refs):
        load = self.copies(refs)[2]
        for d in range(self.n):
            load(d).start()
        for d in range(self.n):
            load(d).wait()

    def run(self, refs):
        out, mine, from_l, from_r = refs[1:5]
        me, n = place()[1], self.n
        right, left = self.copies(refs)[:2]
        for slot in range(2 * n - 3):
            far, near = n - 1 + me - slot, me + slot + 1 - n

            @pl.when((me <= slot) & (me < far) & (me > 0))
            def _():
                right(far).wait_recv()
                mine[far] = (mine[far].astype(f32) + from_l[far].astype(f32)).astype(bf16)

            @pl.when((me <= slot) & (me < far))
            def _():
                right(far).start()

            @pl.when((near >= 0) & (me > near) & (me < n - 1))
            def _():
                left(near).wait_recv()
                mine[near] = (mine[near].astype(f32) + from_r[near].astype(f32)).astype(bf16)

            @pl.when((near >= 0) & (me > near))
            def _():
                left(near).start()

        for d in range(n):

            @pl.when((me == d) & (me > 0))
            def _():
                right(d).wait_recv()

            @pl.when((me == d) & (me < n - 1))
            def _():
                left(d).wait_recv()

            @pl.when(me == d)
            def _():
                total = mine[d].astype(f32)
                if d > 0:
                    total = total + from_l[d].astype(f32)
                if d < n - 1:
                    total = total + from_r[d].astype(f32)
                out[...] = total

    def end(self, refs):
        me, n = place()[1], self.n
        right, left = self.copies(refs)[:2]
        for d in range(n):

            @pl.when(me < d)
            def _():
                right(d).wait_send()

            @pl.when(me > d)
            def _():
                left(d).wait_send()


class HaloGather:
    def __init__(self, x, halo, n):
        tokens, width = x.shape
        self.n, self.halo, self.tokens = n, halo, tokens
        self.parts = reach_parts(tokens, halo)
        self.ins, self.in_specs = [x], [ANY]
        self.outs, self.out_specs = [shape_of(x, (halo, width))], [ANY]
        self.scratch = [dma(len(self.parts))] * 2

    def greet(self, barrier):
        (row, col), n = place(), self.n
        for i in range(len(self.parts)):

            @pl.when(row >= i + 1)
            def _():
                greet(barrier, lax.rem(row + n - i - 1, n), col)

        return jnp.minimum(n - 1 - row, len(self.parts))

    def copy(self, refs, i):
        x, out, send, recv = refs
        (row, col), part = place(), self.parts[i]
        return push(
            x.at[pl.ds(self.tokens - part, part)],
            out.at[pl.ds(self.halo - sum(self.parts[: i + 1]), part)],
            send.at[i],
            recv.at[i],
            lax.rem(row + i + 1, self.n),
            col,
        )

    def begin(self, refs):
        row = place()[0]
        for i in range(len(self.parts)):

            @pl.when(row + i + 1 < self.n)
            def _():
                self.copy(refs, i).start()

    def run(self, refs):
        pass

    def end(self, refs):
        row = place()[0]
        for i in range(len(self.parts)):

            @pl.when(row >= i + 1)
            def _():
                self.copy(refs, i).wait_recv()

            @pl.when(row + i + 1 < self.n)
            def _():
                self.copy(refs, i).wait_send()


class HaloReturn:
    def __init__(self, x, tokens, n):
        halo, width = x.shape
        self.n, self.halo = n, halo
        self.parts = reach_parts(tokens, halo)
        self.ins, self.in_specs = [x], [ANY]
        self.outs = [shape_of(x, (part, width)) for part in self.parts]
        self.out_specs = [ANY] * len(self.parts)
        self.scratch = [dma(len(self.parts))] * 2

    def greet(self, barrier):
        (row, col), n = place(), self.n
        for i in range(len(self.parts)):

            @pl.when(row + i + 1 < n)
            def _():
                greet(barrier, lax.rem(row + i + 1, n), col)

        return jnp.minimum(row, len(self.parts))

    def copy(self, refs, i):
        x, outs, (send, recv) = refs[0], refs[1:-2], refs[-2:]
        (row, col), part = place(), self.parts[i]
        return push(
            x.at[pl.ds(self.halo - sum(self.parts[: i + 1]), part)],
            outs[i],
            send.at[i],
            recv.at[i],
            lax.rem(row + self.n - i - 1, self.n),
            col,
        )

    def begin(self, refs):
        row = place()[0]
        for i in range(len(self.parts)):

            @pl.when(row >= i + 1)
            def _():
                self.copy(refs, i).start()

    def run(self, refs):
        pass

    def end(self, refs):
        row = place()[0]
        for i in range(len(self.parts)):

            @pl.when(row + i + 1 < self.n)
            def _():
                self.copy(refs, i).wait_recv()

            @pl.when(row >= i + 1)
            def _():
                self.copy(refs, i).wait_send()


class AllSum:
    def __init__(self, x, rows, cols):
        self.rows, self.cols = rows, cols
        self.ins, self.in_specs = [x], [VMEM]
        self.outs, self.out_specs = [shape_of(x, x.shape)], [VMEM]
        self.scratch = [
            pltpu.VMEM((rows,) + x.shape, x.dtype),
            pltpu.VMEM((cols,) + x.shape, x.dtype),
            pltpu.VMEM(x.shape, x.dtype),
        ] + [dma(rows - 1), dma(rows - 1), dma(cols - 1), dma(cols - 1)]

    def greet(self, barrier):
        row, col = place()
        for i in range(1, self.rows):
            greet(barrier, lax.rem(row + i, self.rows), col)
        for i in range(1, self.cols):
            greet(barrier, row, lax.rem(col + i, self.cols))
        return self.rows + self.cols - 2

    def first(self, refs, i):
        x, out, by_row, by_col, half, send_a, recv_a, send_b, recv_b = refs
        row, col = place()
        to = lax.rem(row + i, self.rows)
        return push(x, by_row.at[row], send_a.at[i - 1], recv_a.at[i - 1], to, col)

    def second(self, refs, i):
        x, out, by_row, by_col, half, send_a, recv_a, send_b, recv_b = refs
        row, col = place()
        to = lax.rem(col + i, self.cols)
        return push(half, by_col.at[col], send_b.at[i - 1], recv_b.at[i - 1], row, to)

    def begin(self, refs):
        x, out, by_row = refs[:3]
        for i in range(1, self.rows):
            self.first(refs, i).start()
        by_row[place()[0]] = x[...]

    def run(self, refs):
        x, out, by_row, by_col, half = refs[:5]
        for i in range(1, self.rows):
            self.first(refs, i).wait_recv()
        total = by_row[0]
        for i in range(1, self.rows):
            total = total + by_row[i]
        half[...] = total
        for i in range(1, self.cols):
            self.second(refs, i).start()
        by_col[place()[1]] = total
        for i in range(1, self.cols):
            self.second(refs, i).wait_recv()
        total = by_col[0]
        for i in range(1, self.cols):
            total = total + by_col[i]
        out[...] = total

    def end(self, refs):
        for i in range(1, self.rows):
            self.first(refs, i).wait_send()
        for i in range(1, self.cols):
            self.second(refs, i).wait_send()


class RowGatherSmall:
    def __init__(self, x, n):
        self.n = n
        self.ins, self.in_specs = [x], [VMEM]
        self.outs, self.out_specs = [shape_of(x, (n,) + x.shape)], [VMEM]
        self.scratch = [dma(n - 1), dma(n - 1)]

    def greet(self, barrier):
        row, col = place()
        for i in range(1, self.n):
            greet(barrier, lax.rem(row + i, self.n), col)
        return self.n - 1

    def copy(self, refs, i):
        x, out, send, recv = refs
        row, col = place()
        return push(x, out.at[row], send.at[i - 1], recv.at[i - 1], lax.rem(row + i, self.n), col)

    def begin(self, refs):
        for i in range(1, self.n):
            self.copy(refs, i).start()
        refs[1][place()[0]] = refs[0][...]

    def run(self, refs):
        pass

    def end(self, refs):
        for i in range(1, self.n):
            self.copy(refs, i).wait()


class SiblingSwap:
    def __init__(self, *xs):
        self.ins, self.in_specs = list(xs), [ANY] * len(xs)
        self.outs = [shape_of(x, x.shape[:1] + x.shape[2:]) for x in xs]
        self.out_specs = [ANY] * len(xs)
        self.scratch = [dma(len(xs))] * 2

    def greet(self, barrier):
        row, col = place()
        greet(barrier, row + 1 - 2 * lax.rem(row, 2), col)
        return 1

    def copies(self, refs):
        row, col = place()
        other = 1 - lax.rem(row, 2)
        to = row + 2 * other - 1
        send, recv = refs[-2:]
        count = len(self.ins)
        return [
            push(refs[i].at[:, other], refs[count + i], send.at[i], recv.at[i], to, col)
            for i in range(count)
        ]

    def begin(self, refs):
        for copy in self.copies(refs):
            copy.start()

    def run(self, refs):
        pass

    def end(self, refs):
        for copy in self.copies(refs):
            copy.wait()


class ChipExchange:
    def __init__(self, *xs, known=False):
        self.half, self.known = xs[0].shape[0], known
        self.ins, self.in_specs = list(xs), [ANY] * len(xs)
        self.outs = [shape_of(x, x.shape) for x in xs]
        self.out_specs = [ANY] * len(xs)
        self.scratch = [dma(len(xs) * (self.half - 1))] * 2

    def greet(self, barrier):
        if self.known:
            return 0
        row, col = place()
        for i in range(1, self.half):
            greet(barrier, lax.rem(row + 2 * i, 2 * self.half), col)
        return self.half - 1

    def copies(self, refs):
        row, col = place()
        send, recv = refs[-2:]
        count, found = len(self.ins), []
        for i in range(1, self.half):
            to = lax.rem(row + 2 * i, 2 * self.half)
            for j in range(count):
                spot = (i - 1) * count + j
                found.append(
                    push(
                        refs[j].at[to // 2],
                        refs[count + j].at[row // 2],
                        send.at[spot],
                        recv.at[spot],
                        to,
                        col,
                    )
                )
        return found

    begin, run, end = SiblingSwap.begin, SiblingSwap.run, SiblingSwap.end


class RowGather:
    def __init__(self, *xs, n):
        self.n, self.half = n, n // 2
        self.ins, self.in_specs = list(xs), [ANY] * len(xs)
        self.outs = [shape_of(x, (n,) + x.shape) for x in xs]
        self.out_specs = [ANY] * len(xs)
        count = len(xs)
        self.scratch = [pltpu.VMEM(x.shape, x.dtype) for x in xs] + [
            dma(count),
            dma(count * self.half),
            dma(count * self.half),
            dma(count * self.half),
            dma(count * self.half),
        ]

    def greet(self, barrier):
        row, col = place()
        for i in range(1, self.half):
            greet(barrier, lax.rem(row + 2 * i, self.n), col)
        greet(barrier, row + 1 - 2 * lax.rem(row, 2), col)
        return self.half

    def near(self, refs, j, i):
        (row, col), count = place(), len(self.ins)
        send, recv = refs[-4:-2]
        to = row + 1 - 2 * lax.rem(row, 2) if i == 0 else lax.rem(row + 2 * i, self.n)
        spot = i * count + j
        return push(refs[j], refs[count + j].at[row], send.at[spot], recv.at[spot], to, col)

    def relay(self, refs, j, i):
        (row, col), count = place(), len(self.ins)
        send, recv = refs[-2:]
        source = lax.rem(row + self.n - 2 * i, self.n)
        spot = i * count + j
        out = refs[count + j]
        to = row + 1 - 2 * lax.rem(row, 2)
        return push(out.at[source], out.at[source], send.at[spot], recv.at[spot], to, col)

    def own(self, refs, j):
        count = len(self.ins)
        held, sem = refs[2 * count + j], refs[3 * count].at[j]
        return (
            pltpu.make_async_copy(refs[j], held, sem),
            pltpu.make_async_copy(held, refs[count + j].at[place()[0]], sem),
        )

    def begin(self, refs):
        for i in range(self.half):
            for j in range(len(self.ins)):
                self.near(refs, j, i).start()
        for j in range(len(self.ins)):
            load, store = self.own(refs, j)
            load.start()
            load.wait()
            store.start()

    def run(self, refs):
        pass

    def end(self, refs):
        for i in range(1, self.half):
            for j in range(len(self.ins)):
                self.near(refs, j, i).wait_recv()
                self.relay(refs, j, i).start()
        for j in range(len(self.ins)):
            self.near(refs, j, 0).wait_recv()
            self.own(refs, j)[1].wait()
            for i in range(self.half):
                self.near(refs, j, i).wait_send()
            for i in range(1, self.half):
                self.relay(refs, j, i).wait()


class ColWide:
    def __init__(self, *xs, n):
        self.n = n
        self.ins, self.in_specs = list(xs), [ANY] * len(xs)
        self.outs = [shape_of(x, (x.shape[0], n * x.shape[1])) for x in xs]
        self.out_specs = [ANY] * len(xs)
        count = len(xs)
        self.scratch = [pltpu.VMEM(x.shape, x.dtype) for x in xs] + [
            dma(count),
            dma(count * (n - 1)),
            dma(count * (n - 1)),
        ]

    def greet(self, barrier):
        row, col = place()
        for i in range(1, self.n):
            greet(barrier, row, lax.rem(col + i, self.n))
        return self.n - 1

    def spot(self, refs, j):
        width = self.ins[j].shape[1]
        start = pl.multiple_of(place()[1] * width, LANES)
        return refs[len(self.ins) + j].at[:, pl.ds(start, width)]

    def copies(self, refs):
        (row, col), count, found = place(), len(self.ins), []
        send, recv = refs[-2:]
        for i in range(1, self.n):
            for j in range(count):
                at = (i - 1) * count + j
                to = lax.rem(col + i, self.n)
                found.append(
                    push(refs[j], self.spot(refs, j), send.at[at], recv.at[at], row, to)
                )
        return found

    def begin(self, refs):
        count = len(self.ins)
        for copy in self.copies(refs):
            copy.start()
        for j in range(count):
            load = pltpu.make_async_copy(refs[j], refs[2 * count + j], refs[3 * count].at[j])
            load.start()
            load.wait()
            self.store(refs, j).start()

    def store(self, refs, j):
        count = len(self.ins)
        return pltpu.make_async_copy(
            refs[2 * count + j], self.spot(refs, j), refs[3 * count].at[j]
        )

    def run(self, refs):
        pass

    def end(self, refs):
        for copy in self.copies(refs):
            copy.wait()
        for j in range(len(self.ins)):
            self.store(refs, j).wait()


class ColExchange:
    def __init__(self, *xs, n, known=False):
        self.n, self.known = n, known
        self.ins, self.in_specs = list(xs), [ANY] * len(xs)
        self.outs = [shape_of(x, (n, x.shape[0], x.shape[1] // n)) for x in xs]
        self.out_specs = [ANY] * len(xs)
        self.scratch = [dma(len(xs) * (n - 1))] * 2

    def greet(self, barrier):
        return 0 if self.known else ColWide.greet(self, barrier)

    def copies(self, refs):
        (row, col), count, found = place(), len(self.ins), []
        send, recv = refs[-2:]
        for i in range(1, self.n):
            for j in range(count):
                at = (i - 1) * count + j
                to = lax.rem(col + i, self.n)
                width = self.ins[j].shape[1] // self.n
                start = pl.multiple_of(to * width, LANES)
                found.append(
                    push(
                        refs[j].at[:, pl.ds(start, width)],
                        refs[count + j].at[col],
                        send.at[at],
                        recv.at[at],
                        row,
                        to,
                    )
                )
        return found

    begin, run, end = SiblingSwap.begin, SiblingSwap.run, SiblingSwap.end


def exchange(name, collective_id, *jobs):
    def kernel(*refs):
        left = list(refs)

        def take(counts):
            found = []
            for count in counts:
                found.append(left[:count])
                del left[:count]
            return found

        parts = [take([len(getattr(job, kind)) for job in jobs]) for kind in ("ins", "outs", "scratch")]
        held = [a + b + c for a, b, c in zip(*parts)]
        barrier = pltpu.get_barrier_semaphore()
        count = 0
        for job in jobs:
            count = count + job.greet(barrier)

        @pl.when(count > 0)
        def _():
            pl.semaphore_wait(barrier, count)

        for job, own in zip(jobs, held):
            job.begin(own)
        for job, own in zip(jobs, held):
            job.run(own)
        for job, own in zip(jobs, held):
            job.end(own)

    outs = pl.pallas_call(
        kernel,
        out_shape=[out for job in jobs for out in job.outs],
        in_specs=[spec for job in jobs for spec in job.in_specs],
        out_specs=[spec for job in jobs for spec in job.out_specs],
        scratch_shapes=[item for job in jobs for item in job.scratch],
        compiler_params=pltpu.CompilerParams(
            collective_id=collective_id, has_side_effects=True, vmem_limit_bytes=48 << 20
        ),
        cost_estimate=CHEAP,
        name=name,
    )(*[x for job in jobs for x in job.ins])
    outs, found = list(outs), []
    for job in jobs:
        found.append(outs[: len(job.outs)])
        del outs[: len(job.outs)]
    return found


def own_half(x, swapped, parity):
    mine = lax.dynamic_index_in_dim(x, parity, 1, keepdims=False)
    return (mine.astype(f32) + swapped.astype(f32)).astype(bf16)


def total_of(mine, received, index):
    kept = jnp.arange(received.shape[0]).reshape(-1, 1, 1) == index
    return jnp.sum(jnp.where(kept, 0.0, received.astype(f32)), axis=0) + mine.astype(f32)


def lane_groups(width):
    groups = []
    for start in range(0, width, LANES):
        size = min(LANES, width - start)
        groups.append((start, size, range(size // HD)))
    return groups


def only_head(values, head, size):
    if size == HD:
        return values
    lane = lax.broadcasted_iota(jnp.int32, values.shape, 1)
    return jnp.where((lane >= head * HD) & (lane < (head + 1) * HD), values, jnp.zeros_like(values))


def key_bias(bias_ref, key_tags_ref, query_tags, tile, low, halo, index):
    shape = (tile, query_tags.shape[1])

    def fill(t, carry):
        place = pl.multiple_of(t * tile, tile)
        tags = key_tags_ref[pl.ds(place, tile), 0:1]
        key_place = lax.broadcasted_iota(jnp.int32, shape, 0) + (t * tile - halo)
        query_place = lax.broadcasted_iota(jnp.int32, shape, 1) + index * query_tags.shape[1]
        allowed = ((tags == query_tags) & (key_place <= query_place)) | (key_place == query_place)
        bias_ref[pl.ds(place, tile), :] = jnp.where(allowed, 0.0, masked_score)
        return carry

    lax.fori_loop(low, halo // tile + index + 1, fill, 0)


def self_forward(queries, key_values, halo_key_values, query_tags, key_tags, lows):
    tokens, width = queries.shape
    halo = halo_key_values.shape[0]
    tile = min(TILE, tokens)
    blocks = tokens // tile
    window = halo + tokens
    heads = width // HD
    groups = lane_groups(width)

    def kernel(low_ref, q_ref, kv_ref, halo_ref, qt_ref, kt_ref, o_ref, lse_ref, kv_all, v_t, bias):
        index = pl.program_id(0)

        @pl.when(index == 0)
        def _():
            kv_all[pl.ds(0, halo), :] = halo_ref[...]
            kv_all[pl.ds(halo, tokens), :] = kv_ref[...]
            v_t[:, pl.ds(0, halo)] = halo_ref[:, width:].T
            v_t[:, pl.ds(halo, tokens)] = kv_ref[:, width:].T

        low = low_ref[index]
        last = halo // tile + index
        key_bias(bias, kt_ref, qt_ref[0:1, :], tile, low, halo, index)
        parts = []
        for start, size, members in groups:
            q = (q_ref[:, start : start + size].astype(f32) * scale).astype(bf16)
            parts += [only_head(q, h, size) for h in members]

        def step(back, carry):
            t = last - back
            place = pl.multiple_of(t * tile, tile)
            added = bias[pl.ds(place, tile), :]
            new = []
            for start, size, members in groups:
                keys = kv_all[pl.ds(place, tile), start : start + size]
                for h in members:
                    head = start // HD + h
                    peak, total, mixed = carry[head]
                    scores = against(keys, parts[head]) + added
                    top = jnp.maximum(peak, jnp.max(scores, axis=0, keepdims=True))
                    weights = jnp.exp(scores - top)
                    fade = jnp.exp(peak - top)
                    total = total * fade + jnp.sum(weights, axis=0, keepdims=True)
                    values_t = v_t[head * HD : (head + 1) * HD, pl.ds(place, tile)]
                    mixed = mixed * fade + matmul(values_t, weights.astype(bf16))
                    new.append((top, total, mixed))
            return tuple(new)

        empty = tuple(
            (
                jnp.full((1, tile), masked_score, f32),
                jnp.zeros((1, tile), f32),
                jnp.zeros((HD, tile), f32),
            )
            for h in range(heads)
        )
        done = lax.fori_loop(0, last + 1 - low, step, empty)
        mixed = jnp.concatenate([m / l for (_, l, m) in done], axis=0)
        o_ref[...] = mixed.T.astype(bf16)
        for head in range(heads):
            lse_ref[head : head + 1, :] = done[head][0] + jnp.log(done[head][1])

    return pl.pallas_call(
        kernel,
        out_shape=[
            jax.ShapeDtypeStruct((tokens, width), bf16),
            jax.ShapeDtypeStruct((8, tokens), f32),
        ],
        grid_spec=pltpu.PrefetchScalarGridSpec(
            num_scalar_prefetch=1,
            grid=(blocks,),
            in_specs=[
                pl.BlockSpec((tile, width), lambda i, low: (i, 0)),
                pl.BlockSpec((tokens, 2 * width), lambda i, low: (0, 0)),
                pl.BlockSpec((halo, 2 * width), lambda i, low: (0, 0)),
                pl.BlockSpec((8, tile), lambda i, low: (0, i)),
                pl.BlockSpec((window, LANES), lambda i, low: (0, 0)),
            ],
            out_specs=[
                pl.BlockSpec((tile, width), lambda i, low: (i, 0)),
                pl.BlockSpec((8, tile), lambda i, low: (0, i)),
            ],
            scratch_shapes=[
                pltpu.VMEM((window, 2 * width), bf16),
                pltpu.VMEM((width, window), bf16),
                pltpu.VMEM((window, tile), f32),
            ],
        ),
        compiler_params=pltpu.CompilerParams(vmem_limit_bytes=48 << 20),
        cost_estimate=CHEAP,
        name="self_forward",
    )(lows, queries, key_values, halo_key_values, query_tags, key_tags)


def self_backward(
    queries, key_values, halo_key_values, attended, grad_attended, lse, query_tags, key_tags, lows
):
    tokens, width = queries.shape
    halo = halo_key_values.shape[0]
    tile = min(TILE, tokens)
    blocks = tokens // tile
    window = halo + tokens
    heads = width // HD
    groups = lane_groups(width)

    def kernel(
        low_ref,
        q_ref,
        kv_ref,
        halo_ref,
        o_ref,
        do_ref,
        lse_ref,
        qt_ref,
        kt_ref,
        dq_ref,
        dkv_ref,
        dhalo_ref,
        kv_all,
        k_t,
        bias,
        total,
    ):
        index = pl.program_id(0)

        @pl.when(index == 0)
        def _():
            kv_all[pl.ds(0, halo), :] = halo_ref[...]
            kv_all[pl.ds(halo, tokens), :] = kv_ref[...]
            k_t[:, pl.ds(0, halo)] = halo_ref[:, :width].T
            k_t[:, pl.ds(halo, tokens)] = kv_ref[:, :width].T
            total[...] = jnp.zeros_like(total)

        low = low_ref[index]
        last = halo // tile + index
        key_bias(bias, kt_ref, qt_ref[0:1, :], tile, low, halo, index)
        held = []
        for start, size, members in groups:
            q = (q_ref[:, start : start + size].astype(f32) * scale).astype(bf16)
            g = do_ref[:, start : start + size]
            product = (g.astype(f32) * o_ref[:, start : start + size].astype(f32)).T
            q_parts = [only_head(q, h, size) for h in members]
            g_parts = [only_head(g, h, size) for h in members]
            q_rows, g_rows = jnp.concatenate(q_parts, axis=0), jnp.concatenate(g_parts, axis=0)
            centres = [
                jnp.sum(product[h * HD : (h + 1) * HD, :], axis=0, keepdims=True) for h in members
            ]
            held.append((q_parts, g_parts, q_rows, g_rows, centres))

        def step(back, carry):
            t = last - back
            place = pl.multiple_of(t * tile, tile)
            added = bias[pl.ds(place, tile), :]
            new = []
            for (start, size, members), own in zip(groups, held):
                q_parts, g_parts, q_rows, g_rows, centres = own
                keys = kv_all[pl.ds(place, tile), start : start + size]
                values = kv_all[pl.ds(place, tile), width + start : width + start + size]
                all_weights, all_scores = [], []
                for h in members:
                    head = start // HD + h
                    lse = lse_ref[head : head + 1, :]
                    weights = jnp.exp(against(keys, q_parts[h]) + added - lse)
                    grads = weights * (against(values, g_parts[h]) - centres[h])
                    grads = grads.astype(bf16)
                    keys_t = k_t[head * HD : (head + 1) * HD, pl.ds(place, tile)]
                    new.append(carry[head] + matmul(keys_t, grads))
                    all_weights.append(weights.astype(bf16))
                    all_scores.append(grads)
                total[pl.ds(place, tile), start : start + size] += matmul(
                    jnp.concatenate(all_scores, axis=1), q_rows
                )
                total[pl.ds(place, tile), width + start : width + start + size] += matmul(
                    jnp.concatenate(all_weights, axis=1), g_rows
                )
            return tuple(new)

        empty = tuple(jnp.zeros((HD, tile), f32) for head in range(heads))
        done = lax.fori_loop(0, last + 1 - low, step, empty)
        dq_ref[...] = (jnp.concatenate(done, axis=0).T * scale).astype(bf16)

        @pl.when(index == blocks - 1)
        def _():
            dhalo_ref[...] = total[pl.ds(0, halo), :].astype(bf16)
            dkv_ref[...] = total[pl.ds(halo, tokens), :]

    return pl.pallas_call(
        kernel,
        out_shape=[
            jax.ShapeDtypeStruct((tokens, width), bf16),
            jax.ShapeDtypeStruct((tokens, 2 * width), f32),
            jax.ShapeDtypeStruct((halo, 2 * width), bf16),
        ],
        grid_spec=pltpu.PrefetchScalarGridSpec(
            num_scalar_prefetch=1,
            grid=(blocks,),
            in_specs=[
                pl.BlockSpec((tile, width), lambda i, low: (i, 0)),
                pl.BlockSpec((tokens, 2 * width), lambda i, low: (0, 0)),
                pl.BlockSpec((halo, 2 * width), lambda i, low: (0, 0)),
                pl.BlockSpec((tile, width), lambda i, low: (i, 0)),
                pl.BlockSpec((tile, width), lambda i, low: (i, 0)),
                pl.BlockSpec((8, tile), lambda i, low: (0, i)),
                pl.BlockSpec((8, tile), lambda i, low: (0, i)),
                pl.BlockSpec((window, LANES), lambda i, low: (0, 0)),
            ],
            out_specs=[
                pl.BlockSpec((tile, width), lambda i, low: (i, 0)),
                pl.BlockSpec((tokens, 2 * width), lambda i, low: (0, 0)),
                pl.BlockSpec((halo, 2 * width), lambda i, low: (0, 0)),
            ],
            scratch_shapes=[
                pltpu.VMEM((window, 2 * width), bf16),
                pltpu.VMEM((width, window), bf16),
                pltpu.VMEM((window, tile), f32),
                pltpu.VMEM((window, 2 * width), f32),
            ],
        ),
        compiler_params=pltpu.CompilerParams(vmem_limit_bytes=56 << 20),
        cost_estimate=CHEAP,
        name="self_backward",
    )(
        lows,
        queries,
        key_values,
        halo_key_values,
        attended,
        grad_attended,
        lse,
        query_tags,
        key_tags,
    )


def cross_weights(keys, part, mine):
    scores = against(keys, part)
    raised = jnp.exp(scores - jnp.max(scores, axis=0, keepdims=True))
    return jnp.where(mine, raised / jnp.sum(raised, axis=0, keepdims=True), 0.0)


def cross_forward(queries, keys, values, clips, ends, text):
    rows, width = queries.shape

    def kernel(ends_ref, q_ref, k_ref, v_ref, clip_ref, o_ref, total):
        total[...] = jnp.zeros_like(total)
        clip_row = clip_ref[0:1, :]

        def step(clip, carry):
            place = pl.multiple_of(clip * text, text)
            mine = clip_row == clip
            for start, size, members in lane_groups(width):
                q = (q_ref[:, start : start + size].astype(f32) * scale).astype(bf16)
                k = k_ref[pl.ds(place, text), start : start + size]
                v_t = v_ref[pl.ds(place, text), start : start + size].T
                for h in members:
                    weights = cross_weights(k, only_head(q, h, size), mine).astype(bf16)
                    spot = slice(start + h * HD, start + (h + 1) * HD)
                    total[spot, :] += matmul(v_t[h * HD : (h + 1) * HD, :], weights)
            return carry

        lax.fori_loop(ends_ref[0], ends_ref[1] + 1, step, 0)
        o_ref[...] = total[...].T.astype(bf16)

    return pl.pallas_call(
        kernel,
        out_shape=jax.ShapeDtypeStruct((rows, width), bf16),
        grid_spec=pltpu.PrefetchScalarGridSpec(
            num_scalar_prefetch=1,
            grid=(1,),
            in_specs=[
                pl.BlockSpec((rows, width), lambda i, e: (0, 0)),
                pl.BlockSpec(keys.shape, lambda i, e: (0, 0)),
                pl.BlockSpec(values.shape, lambda i, e: (0, 0)),
                pl.BlockSpec((8, rows), lambda i, e: (0, 0)),
            ],
            out_specs=pl.BlockSpec((rows, width), lambda i, e: (0, 0)),
            scratch_shapes=[pltpu.VMEM((width, rows), f32)],
        ),
        compiler_params=pltpu.CompilerParams(vmem_limit_bytes=48 << 20),
        cost_estimate=CHEAP,
        name="cross_forward",
    )(ends, queries, keys, values, clips)


def cross_backward(queries, keys, values, grad_attended, clips, ends, text):
    rows, width = queries.shape

    def kernel(ends_ref, q_ref, k_ref, v_ref, do_ref, clip_ref, dq_ref, dk_ref, dv_ref, total):
        total[...] = jnp.zeros_like(total)
        dk_ref[...] = jnp.zeros_like(dk_ref)
        dv_ref[...] = jnp.zeros_like(dv_ref)
        clip_row = clip_ref[0:1, :]

        def step(clip, carry):
            place = pl.multiple_of(clip * text, text)
            mine = clip_row == clip
            for start, size, members in lane_groups(width):
                q = (q_ref[:, start : start + size].astype(f32) * scale).astype(bf16)
                g = do_ref[:, start : start + size]
                k = k_ref[pl.ds(place, text), start : start + size]
                v = v_ref[pl.ds(place, text), start : start + size]
                k_t = k.T
                dk = jnp.zeros((text, size), f32)
                dv = jnp.zeros((text, size), f32)
                for h in members:
                    part, grad = only_head(q, h, size), only_head(g, h, size)
                    weights = cross_weights(k, part, mine)
                    back = against(v, grad)
                    centre = jnp.sum(weights * back, axis=0, keepdims=True)
                    grads = (weights * (back - centre)).astype(bf16)
                    spot = slice(start + h * HD, start + (h + 1) * HD)
                    total[spot, :] += matmul(k_t[h * HD : (h + 1) * HD, :], grads)
                    dk = dk + matmul(grads, part)
                    dv = dv + matmul(weights.astype(bf16), grad)
                dk_ref[pl.ds(place, text), start : start + size] = dk.astype(bf16)
                dv_ref[pl.ds(place, text), start : start + size] = dv.astype(bf16)
            return carry

        lax.fori_loop(ends_ref[0], ends_ref[1] + 1, step, 0)
        dq_ref[...] = (total[...].T * scale).astype(bf16)

    return pl.pallas_call(
        kernel,
        out_shape=[
            jax.ShapeDtypeStruct((rows, width), bf16),
            jax.ShapeDtypeStruct(keys.shape, bf16),
            jax.ShapeDtypeStruct(keys.shape, bf16),
        ],
        grid_spec=pltpu.PrefetchScalarGridSpec(
            num_scalar_prefetch=1,
            grid=(1,),
            in_specs=[
                pl.BlockSpec((rows, width), lambda i, e: (0, 0)),
                pl.BlockSpec(keys.shape, lambda i, e: (0, 0)),
                pl.BlockSpec(values.shape, lambda i, e: (0, 0)),
                pl.BlockSpec((rows, width), lambda i, e: (0, 0)),
                pl.BlockSpec((8, rows), lambda i, e: (0, 0)),
            ],
            out_specs=[
                pl.BlockSpec((rows, width), lambda i, e: (0, 0)),
                pl.BlockSpec(keys.shape, lambda i, e: (0, 0)),
                pl.BlockSpec(values.shape, lambda i, e: (0, 0)),
            ],
            scratch_shapes=[pltpu.VMEM((width, rows), f32)],
        ),
        compiler_params=pltpu.CompilerParams(vmem_limit_bytes=48 << 20),
        cost_estimate=CHEAP,
        name="cross_backward",
    )(ends, queries, keys, values, grad_attended, clips)


def after(x, *others):
    return lax.optimization_barrier((x,) + others)[0]


def row_gather(*parts):
    return lax.all_gather(jnp.concatenate(parts, axis=1), "row", axis=0, tiled=True)


def row_scatter(*parts):
    joined = jnp.concatenate([part.astype(bf16) for part in parts], axis=1)
    return lax.psum_scatter(joined, "row", scatter_dimension=0, tiled=True)


def on_device(
    frames,
    text_states,
    clip_ids,
    valid_mask,
    teacher_states,
    self_norm_gain,
    self_norm_bias,
    cross_norm_gain,
    cross_norm_bias,
    final_norm_gain,
    final_norm_bias,
    self_query,
    self_key,
    self_value,
    self_output,
    cross_query,
    cross_key,
    cross_value,
    cross_output,
    expand_weight,
    reduce_weight,
):
    rows, cols = lax.axis_size("row"), lax.axis_size("col")
    row, col = lax.axis_index("row"), lax.axis_index("col")
    tokens, (own, features) = clip_ids.shape[0], frames.shape
    width = self_query.shape[1]
    seg_count, text_rows = text_states.shape[:2]
    text = text_rows * rows
    hidden = expand_weight.shape[1]
    tile = min(TILE, tokens)
    halo = -(-(CLIP - 1) // tile) * tile
    half = rows // 2
    chip, parity = row // 2, row % 2
    aligned = width % LANES == 0

    packed = (clip_ids * 2 + valid_mask).reshape(8, tokens // 8)
    text_local = text_states.reshape(seg_count * text_rows, -1)
    first = exchange(
        "gather_tags", 1, RowGatherSmall(packed, rows), *([ColWide(text_local, n=cols)] if aligned else [])
    )
    packed_all = first[0][0].reshape(rows * tokens)
    valid_sum = jnp.sum(packed_all % 2).astype(f32)
    padded = jnp.concatenate([jnp.full((halo,), -2, jnp.int32), packed_all])
    window = lax.dynamic_slice_in_dim(padded, row * tokens, halo + tokens)
    window_clips, window_valid = window // 2, window % 2
    key_tags = jnp.where(window_valid == 1, window_clips + 1, 0)
    key_tags = jnp.broadcast_to(key_tags[:, None], (halo + tokens, LANES))
    query_tags = jnp.broadcast_to(clip_ids[None, :] + 1, (8, tokens))
    first_clips = clip_ids[::tile]
    lows = jnp.sum((window_clips[None, :] < first_clips[:, None]).astype(jnp.int32), axis=1) // tile

    own_clips = lax.dynamic_slice_in_dim(clip_ids, col * own, own)
    own_valid = lax.dynamic_slice_in_dim(valid_mask, col * own, own).astype(f32)
    clip_rows = jnp.broadcast_to(own_clips[None, :], (8, own))
    ends = jnp.stack([own_clips[0], own_clips[-1]])

    weights_one = row_gather(self_query, self_key, self_value, self_output.T)
    normed_one, unit_one, inverse_one = normalize(frames, self_norm_gain, self_norm_bias)
    (wide_one,), (expand_full,) = exchange(
        "gather_one", 2, LineGather(normed_one, cols), RowGather(expand_weight, n=rows)
    )
    expand_full = expand_full.reshape(features, hidden)
    wide_one = wide_one.reshape(tokens, features)
    weights_text = row_gather(after(cross_key, packed_all), cross_value)
    if aligned:
        text_full = first[1][0]
    else:
        text_full = lax.all_gather(text_local, "col", axis=1, tiled=True)
    ckey_full, cvalue_full = weights_text[:, :width], weights_text[:, width:]
    query_full, kv_full = weights_one[:, :width], weights_one[:, width : 3 * width]
    output_full = weights_one[:, 3 * width :]

    key_values = matmul(wide_one, kv_full).astype(bf16)
    queries = matmul(wide_one, query_full).astype(bf16)
    cross_local = (cross_query, cross_output.T)
    (halo_kv,), *cross_wide = exchange(
        "gather_halo",
        3,
        HaloGather(key_values, halo, rows),
        *([ColWide(*cross_local, n=cols)] if aligned else []),
    )
    text_full = after(text_full, halo_kv)
    text_kv = jnp.stack([matmul(text_full, ckey_full), matmul(text_full, cvalue_full)]).astype(bf16)
    text_all = lax.all_gather(text_kv, ("row", "col"), axis=0)
    attended_one, lse = self_forward(
        after(queries, text_kv), key_values, halo_kv, query_tags, key_tags, lows
    )
    if aligned:
        cross_wide = cross_wide[0]
    else:
        cross_wide = [lax.all_gather(x, "col", axis=1, tiled=True) for x in cross_local]
    partial_one = against(attended_one, output_full).astype(bf16)
    (branch_one,), cross_full = exchange(
        "scatter_one",
        4,
        LineScatter(partial_one, cols),
        RowGather(*cross_wide, n=rows),
    )
    cquery_full, coutput_full = (x.reshape(features, features) for x in cross_full)
    after_self = (frames.astype(f32) + branch_one).astype(bf16)

    text_all = text_all.reshape(rows, cols, 2, seg_count, text_rows, width)
    text_all = text_all.transpose(2, 3, 0, 4, 1, 5).reshape(2, seg_count * text, features)
    normed_two, unit_two, inverse_two = normalize(after_self, cross_norm_gain, cross_norm_bias)
    cross_queries = matmul(normed_two, cquery_full).astype(bf16)
    attended_two = cross_forward(cross_queries, text_all[0], text_all[1], clip_rows, ends, text)
    after_cross = (after_self.astype(f32) + against(attended_two, coutput_full)).astype(bf16)

    normed_three, unit_three, inverse_three = normalize(
        after_cross, final_norm_gain, final_norm_bias
    )
    (wide_three,), (reduce_full,) = exchange(
        "gather_three", 5, LineGather(normed_three, cols), RowGather(reduce_weight.T, n=rows)
    )
    reduce_full = reduce_full.reshape(features, hidden)
    wide_three = wide_three.reshape(tokens, features)
    expanded = matmul(wide_three, expand_full)
    activated = jax.nn.gelu(expanded, approximate=False).astype(bf16)
    partial_three = against(activated, reduce_full).astype(bf16)
    ((branch_three,),) = exchange("scatter_three", 6, LineScatter(partial_three, cols))
    layer_out = (after_cross.astype(f32) + branch_three).astype(bf16)
    error = layer_out.astype(f32) - teacher_states.astype(f32)
    squared = jnp.sum(error * error * own_valid[:, None])
    grad_out = error * own_valid[:, None] * (tokens * rows / valid_sum)

    ((grad_wide,),) = exchange("gather_grad", 7, LineGather(grad_out.astype(bf16), cols))
    grad_wide = grad_wide.reshape(tokens, features)
    grad_activated = matmul(grad_wide, reduce_full)
    unused, gelu_back = jax.vjp(partial(jax.nn.gelu, approximate=False), expanded)
    grad_expanded = gelu_back(grad_activated)[0].astype(bf16)
    grad_reduce = transposed(grad_wide, activated).astype(bf16)
    grad_expand = transposed(wide_three, grad_expanded).astype(bf16)
    by_row = (half, 2, features // rows)
    feed = [x.reshape(by_row + (hidden,)) for x in (grad_expand, grad_reduce)]
    back_three = against(grad_expanded, expand_full).astype(bf16)
    (back_three,), swapped = exchange(
        "scatter_grad_three", 8, LineScatter(back_three, cols), SiblingSwap(*feed)
    )
    feed = [own_half(x, y, parity) for x, y in zip(feed, swapped)]
    inner_three, gain_three, shift_three = normalize_back(
        back_three, unit_three, inverse_three, final_norm_gain
    )
    grad_after_cross = grad_out + inner_three

    grad_two = grad_after_cross.astype(bf16)
    grad_attended_two = matmul(grad_two, coutput_full).astype(bf16)
    grad_cqueries, grad_tkeys, grad_tvalues = cross_backward(
        cross_queries, text_all[0], text_all[1], grad_attended_two, clip_rows, ends, text
    )
    inner_two, gain_two, shift_two = normalize_back(
        against(grad_cqueries, cquery_full), unit_two, inverse_two, cross_norm_gain
    )
    grad_after_self = grad_after_cross + inner_two
    grad_cquery = transposed(normed_two, grad_cqueries).astype(bf16)
    grad_coutput = transposed(grad_two, attended_two).astype(bf16)
    partial_text = jnp.stack([grad_tkeys, grad_tvalues])
    partial_text = partial_text.reshape(2, seg_count, rows, text_rows, cols, width)
    partial_text = partial_text.transpose(2, 4, 0, 1, 3, 5).reshape(
        rows * cols, 2 * seg_count * text_rows, width
    )
    mine_text = lax.psum_scatter(partial_text, ("row", "col"), scatter_dimension=0, tiled=False)

    grad_one = grad_after_self.astype(bf16)
    cross = [x.reshape(by_row + (features,)) for x in (grad_cquery, grad_coutput)]
    (grad_wide_one,), received, swapped = exchange(
        "gather_grad_one", 9, LineGather(grad_one, cols), ChipExchange(*feed), SiblingSwap(*cross)
    )
    grad_wide_one = grad_wide_one.reshape(tokens, features)
    feed = [
        total_of(lax.dynamic_index_in_dim(x, chip, 0, keepdims=False), y, chip)
        for x, y in zip(feed, received)
    ]
    cross = [own_half(x, y, parity) for x, y in zip(cross, swapped)]
    grad_attended_one = matmul(grad_wide_one, output_full).astype(bf16)
    grad_queries, grad_kv_own, grad_kv_halo = self_backward(
        queries,
        key_values,
        halo_kv,
        attended_one,
        grad_attended_one,
        lse,
        query_tags,
        key_tags,
        lows,
    )
    mine_text = after(mine_text, grad_queries).reshape(2, seg_count * text_rows, width)
    grad_text_weights = [transposed(text_full, mine_text[i]).astype(bf16) for i in range(2)]
    grad_output = transposed(grad_wide_one, attended_one).astype(bf16)
    summed_output = row_scatter(after(grad_output, mine_text))
    summed_text = row_scatter(grad_text_weights[0], grad_text_weights[1])
    text_partial = against(mine_text[0], ckey_full) + against(mine_text[1], cvalue_full)
    text_partial = text_partial.astype(bf16)

    (returned,) = exchange(
        "return_halo", 10, HaloReturn(after(grad_kv_halo, text_partial), tokens, rows)
    )
    for i, piece in enumerate(returned):
        piece = jnp.where(row + i + 1 < rows, piece.astype(f32), 0.0)
        grad_kv_own = grad_kv_own + jnp.pad(piece, ((tokens - piece.shape[0], 0), (0, 0)))
    grad_kv = grad_kv_own.astype(bf16)
    grad_qkv = jnp.concatenate([grad_queries, grad_kv], axis=1)
    grad_normed_one = against(grad_qkv, weights_one[:, : 3 * width]).astype(bf16)
    (back_one,), received, *text_parts = exchange(
        "scatter_grad_one",
        11,
        LineScatter(grad_normed_one, cols),
        ChipExchange(*cross),
        *([ColExchange(text_partial, n=cols)] if aligned else []),
    )
    if aligned:
        grad_text = total_of(
            lax.dynamic_slice_in_dim(text_partial, col * width, width, 1), text_parts[0][0], col
        )
    else:
        grad_text = lax.psum_scatter(text_partial, "col", scatter_dimension=1, tiled=True)
    grad_text = grad_text.astype(f32).reshape(seg_count, text_rows, width)
    cross = [
        total_of(lax.dynamic_index_in_dim(x, chip, 0, keepdims=False), y, chip).astype(bf16)
        for x, y in zip(cross, received)
    ]
    inner_one, gain_one, shift_one = normalize_back(
        back_one, unit_one, inverse_one, self_norm_gain
    )
    grad_input = grad_after_self + inner_one
    summed_one = row_scatter(transposed(wide_one, grad_qkv))

    small = jnp.stack(
        [
            gain_one,
            shift_one,
            gain_two,
            shift_two,
            gain_three,
            shift_three,
            jnp.full((features,), squared),
            jnp.zeros((features,), f32),
        ]
    )
    (small,), *received = exchange(
        "sum_small",
        12,
        AllSum(after(small, summed_text, summed_output), rows, cols),
        *([ColExchange(*cross, n=cols, known=True)] if aligned else []),
    )
    if aligned:
        cross = [
            total_of(lax.dynamic_slice_in_dim(x, col * width, width, 1), y, col)
            for x, y in zip(cross, received[0])
        ]
    else:
        cross = [lax.psum_scatter(x, "col", scatter_dimension=1, tiled=True) for x in cross]
    loss = small[6, 0] / (valid_sum * features)

    summed_one = summed_one.astype(f32)
    summed_text = summed_text.astype(f32)
    return (
        layer_out,
        loss,
        grad_input,
        grad_text,
        small[0],
        small[1],
        small[2],
        small[3],
        small[4],
        small[5],
        summed_one[:, :width],
        summed_one[:, width : 2 * width],
        summed_one[:, 2 * width : 3 * width],
        summed_output.astype(f32).T,
        cross[0].astype(f32),
        summed_text[:, :width],
        summed_text[:, width:],
        cross[1].astype(f32).T,
        feed[0],
        feed[1].T,
    )


def solution(mesh):
    return jax.shard_map(
        on_device,
        mesh=mesh,
        in_specs=(
            P(("row", "col"), None),
            P(None, "row", "col"),
            P("row"),
            P("row"),
            P(("row", "col"), None),
            P(),
            P(),
            P(),
            P(),
            P(),
            P(),
            P("row", "col"),
            P("row", "col"),
            P("row", "col"),
            P("col", "row"),
            P("row", "col"),
            P("row", "col"),
            P("row", "col"),
            P("col", "row"),
            P("row", "col"),
            P("col", "row"),
        ),
        out_specs=(
            P(("row", "col"), None),
            P(),
            P(("row", "col"), None),
            P(None, "row", "col"),
            P(),
            P(),
            P(),
            P(),
            P(),
            P(),
            P("row", "col"),
            P("row", "col"),
            P("row", "col"),
            P("col", "row"),
            P("row", "col"),
            P("row", "col"),
            P("row", "col"),
            P("col", "row"),
            P("row", "col"),
            P("col", "row"),
        ),
        check_vma=False,
    )
```

profile of v0, /device:TPU:0, one launch (start us, length us, event | category | flops | bytes accessed | tf_op | source)
XLA Modules:
  0.0 954.4 jit_solution(17347140324382233220)
XLA Ops:
  11.0 11.3 %gather_tags.1 = (s32[8,8,128]{2,1,0:T(8,128)S(1)}, bf16[64,1536]{1,0:T(8,128)(2,1)S(1)}) custom-call(s32[8,128]{1,0:T(8,128)S(1)} %get-tuple-element.226.refs_0_, bf16[64,384]{1,0:T(8,128)(2,1)S(1)} %bitcast.125), custom_call_target="tpu_custom_call" | custom-call | flops 1048576 | bytes 1048576 | tf_op jit(solution)/shard_map/gather_tags/pallas_call | solution.py:751
  25.1 58.4 %gather_one.1 = (bf16[4,256,1536]{2,1,0:T(8,128)(2,1)S(1)}, bf16[8,192,1536]{2,1,0:T(8,128)(2,1)}) custom-call(bf16[256,1536]{1,0:T(8,128)(2,1)S(1)} %fusion.40.refs_0_, bf16[192,1536]{1,0:T(8,128)(2,1)S(1)} %copy-done.15), custom_call_target="tpu_custom_call" | custom-call | flops 1048576 | bytes 1048576 | tf_op jit(solution)/shard_map/gather_one/pallas_call | solution.py:751
  85.2 5.3 fusion.28.refs_0_.kv_ref
  90.5 24.4 %gather_halo.1 = (bf16[1536,768]{1,0:T(8,128)(2,1)S(1)}, bf16[192,1536]{1,0:T(8,128)(2,1)S(1)}, bf16[192,1536]{1,0:T(8,128)(2,1)S(1)}) custom-call(bf16[1024,768]{1,0:T(8,128)(2,1)S(1)} %fusion.28.refs_0_.kv_ref, bf16[192,384]{1,0:T(8,128)(2,1)S(1)} %copy-done.18, bf16[192,384]{1,0:T(8,128)(2,1)S(1)} %bitcast.123), custom_call_target="tpu_custom_call" | custom-call | flops 1048576 | bytes 1048576 | tf_op jit(solution)/shard_map/gather_halo/pallas_call | solution.py:751
  126.1 4.0 convolution_convert_fusion.15.q_ref
  130.6 24.7 %self_forward.1 = (bf16[1024,384]{1,0:T(8,128)(2,1)S(1)}, f32[8,1024]{1,0:T(8,128)S(1)}) custom-call(s32[4]{0:T(128)S(1)} %and_select_fusion.low_ref, bf16[1024,384]{1,0:T(8,128)(2,1)S(1)} %convolution_convert_fusion.15.q_ref, bf16[1024,768]{1,0:T(8,128)(2,1)S(1)} %fusion.28.refs_0_.kv_ref, bf16[1536,768]{1,0:T(8,128)(2,1)} %copy-done.4, ...), custom_call_target="tpu_custom_call" | custom-call | flops 1048576 | bytes 1048576 | tf_op jit(solution)/shard_map/self_forward/pallas_call | solution.py:871
  159.3 94.2 %scatter_one.1 = (f32[256,1536]{1,0:T(8,128)S(1)}, bf16[8,192,1536]{2,1,0:T(8,128)(2,1)}, bf16[8,192,1536]{2,1,0:T(8,128)(2,1)}) custom-call(bf16[4,256,1536]{2,1,0:T(8,128)(2,1)S(1)} %bitcast.117, bf16[192,1536]{1,0:T(8,128)(2,1)S(1)} %get-tuple-element.66.refs_1_, bf16[192,1536]{1,0:T(8,128)(2,1)S(1)} %get-tuple-element.67.refs_2_), custom_call_target="tpu_custom_call" | custom-call | flops 1048576 | bytes 1048576 | tf_op jit(solution)/shard_map/scatter_one/pallas_call | solution.py:751
  260.9 6.1 cross_forward.1
  272.0 76.0 %gather_three.1 = (bf16[4,256,1536]{2,1,0:T(8,128)(2,1)S(1)}, bf16[8,192,1536]{2,1,0:T(8,128)(2,1)}) custom-call(bf16[256,1536]{1,0:T(8,128)(2,1)S(1)} %add_convert_fusion.3.refs_0_, bf16[192,1536]{1,0:T(8,128)(2,1)S(1)} %bitcast.122), custom_call_target="tpu_custom_call" | custom-call | flops 1048576 | bytes 1048576 | tf_op jit(solution)/shard_map/gather_three/pallas_call | solution.py:751
  348.0 22.7 %multiply_convert_fusion = (bf16[1024,1536]{1,0:T(8,128)(2,1)S(1)}, f32[1024,1536]{1,0:T(8,128)}, f32[1024,1536]{1,0:T(8,128)}) fusion(bf16[1024,1536]{1,0:T(8,128)(2,1)S(1)} %bitcast.129, bf16[1536,1536]{1,0:T(8,128)(2,1)} %bitcast.157), kind=kOutput, calls=%fused_computation.8 | convolution fusion | flops 4934074368 | bytes 23592960 | tf_op jit(solution)/shard_map/dot_general | solution.py:27
  370.6 5.3 convolution_convert_fusion.6
  375.9 55.5 %scatter_three.1 = f32[256,1536]{1,0:T(8,128)S(1)} custom-call(bf16[4,256,1536]{2,1,0:T(8,128)(2,1)S(1)} %bitcast.116), custom_call_target="tpu_custom_call" | custom-call | flops 1048576 | bytes 1048576 | tf_op jit(solution)/shard_map/scatter_three/pallas_call | solution.py:751
  433.0 52.4 %gather_grad.1 = bf16[4,256,1536]{2,1,0:T(8,128)(2,1)S(1)} custom-call(bf16[256,1536]{1,0:T(8,128)(2,1)S(1)} %fusion.48.refs_0_), custom_call_target="tpu_custom_call" | custom-call | flops 1048576 | bytes 1048576 | tf_op jit(solution)/shard_map/gather_grad/pallas_call | solution.py:751
  485.4 10.8 %add_convert_fusion = bf16[1024,1536]{1,0:T(8,128)(2,1)S(1)} fusion(f32[1024,1536]{1,0:T(8,128)} %get-tuple-element.213, f32[1024,1536]{1,0:T(8,128)} %get-tuple-element.231, bf16[1024,1536]{1,0:T(8,128)(2,1)S(1)} %bitcast.118, bf16[1536,1536]{1,0:T(8,128)(2,1)} %bitcast.161), kind=kOutput, calls=%fused_computation.7 | convolution fusion | flops 4853858304 | bytes 23592960 | tf_op jit(solution)/shard_map/dot_general | solution.py:27
  496.3 8.9 convolution_convert_fusion.5
  505.1 7.0 convolution_convert_fusion.2
  512.1 6.8 convolution_convert_fusion.1
  519.0 58.9 %scatter_grad_three.1 = (f32[256,1536]{1,0:T(8,128)S(1)}, bf16[4,192,1536]{2,1,0:T(8,128)(2,1)S(1)}, bf16[4,192,1536]{2,1,0:T(8,128)(2,1)}) custom-call(bf16[4,256,1536]{2,1,0:T(8,128)(2,1)} %bitcast.146, bf16[4,2,192,1536]{3,2,1,0:T(8,128)(2,1)} %bitcast.137, bf16[4,2,192,1536]{3,2,1,0:T(8,128)(2,1)} %bitcast.141), custom_call_target="tpu_custom_call" | custom-call | flops 1048576 | bytes 1048576 | tf_op jit(solution)/shard_map/scatter_grad_three/pallas_call | solution.py:751
  579.5 4.3 convolution_convert_fusion.12.do_ref
  583.8 8.7 cross_backward.1
  596.2 4.0 fusion.37
  614.6 68.2 %gather_grad_one.1 = (bf16[4,256,1536]{2,1,0:T(8,128)(2,1)}, bf16[4,192,1536]{2,1,0:T(8,128)(2,1)S(1)}, bf16[4,192,1536]{2,1,0:T(8,128)(2,1)S(1)}, bf16[4,192,1536]{2,1,0:T(8,128)(2,1)}, bf16[4,192,1536]{2,1,0:T(8,128)(2,1)}) custom-call(bf16[256,1536]{1,0:T(8,128)(2,1)S(1)} %get-tuple-element.210.refs_0_, bf16[4,192,1536]{2,1,0:T(8,128)(2,1)} %get-tuple-element.234.refs_1_, ...), custom_call_target="tpu_custom_call" | custom-call | flops 1048576 | bytes 1048576 | tf_op jit(solution)/shard_map/gather_grad_one/pallas_call | solution.py:751
  685.6 4.7 convolution_convert_fusion.11
  690.6 5.1 convolution_convert_fusion.14.do_ref
  695.7 30.2 %self_backward.1 = (bf16[1024,384]{1,0:T(8,128)(2,1)}, f32[1024,768]{1,0:T(8,128)}, bf16[1536,768]{1,0:T(8,128)(2,1)}) custom-call(s32[4]{0:T(128)} %copy-done.22, bf16[1024,384]{1,0:T(8,128)(2,1)} %copy-done.5, bf16[1024,768]{1,0:T(8,128)(2,1)} %copy-done.2, bf16[1536,768]{1,0:T(8,128)(2,1)} %copy-done.4, bf16[1024,384]{1,0:T(8,128)(2,1)} %copy-done.12, ...), custom_call_target="tpu_custom_call" | custom-call | flops 1048576 | bytes 1048576 | tf_op jit(solution)/shard_map/self_backward/pallas_call | solution.py:995
  740.5 22.0 %reduce-scatter.9.cloned.1.call-done = bf16[192,384]{1,0:T(8,128)(2,1)} async-done(((bf16[1536,384]{1,0:T(8,128)(2,1)}), bf16[192,384]{1,0:T(8,128)(2,1)}) %reduce-scatter.9.cloned.1.call-update) | async-done | bytes 147472 | tf_op jit(solution)/shard_map/reduce_scatter | solution.py:1170
  767.7 43.8 %return_halo.1 = (bf16[1024,768]{1,0:T(8,128)(2,1)S(1)}, bf16[512,768]{1,0:T(8,128)(2,1)S(1)}) custom-call(bf16[1536,768]{1,0:T(8,128)(2,1)S(1)} %copy-done.6), custom_call_target="tpu_custom_call" | custom-call | flops 1048576 | bytes 1048576 | tf_op jit(solution)/shard_map/return_halo/pallas_call | solution.py:751
  812.9 5.8 convolution_convert_fusion.8
  818.7 59.3 %scatter_grad_one.1 = (f32[256,1536]{1,0:T(8,128)S(1)}, bf16[4,192,1536]{2,1,0:T(8,128)(2,1)S(1)}, bf16[4,192,1536]{2,1,0:T(8,128)(2,1)}, bf16[4,64,384]{2,1,0:T(8,128)(2,1)S(1)}) custom-call(bf16[4,256,1536]{2,1,0:T(8,128)(2,1)} %bitcast.147, bf16[4,192,1536]{2,1,0:T(8,128)(2,1)} %fusion.7.refs_1_, bf16[4,192,1536]{2,1,0:T(8,128)(2,1)} %fusion.6.refs_2_, ...), custom_call_target="tpu_custom_call" | custom-call | flops 1048576 | bytes 1048576 | tf_op jit(solution)/shard_map/scatter_grad_one/pallas_call | solution.py:751
  880.6 5.8 convolution_convert_fusion
  887.9 5.7 select_reduce_fusion
  903.8 32.1 %sum_small.1 = (f32[8,1536]{1,0:T(8,128)S(1)}, bf16[4,192,384]{2,1,0:T(8,128)(2,1)S(1)}, bf16[4,192,384]{2,1,0:T(8,128)(2,1)S(1)}) custom-call(f32[8,1536]{1,0:T(8,128)S(1)} %stack.55.refs_0_, bf16[192,1536]{1,0:T(8,128)(2,1)S(1)} %fusion.52.refs_1_, bf16[192,1536]{1,0:T(8,128)(2,1)S(1)} %fusion.51.refs_2_), custom_call_target="tpu_custom_call" | custom-call | flops 1048576 | bytes 1048576 | tf_op jit(solution)/shard_map/sum_small/pallas_call | solution.py:751
  (240 shorter events, 104.3 us)
Async XLA Ops:
  7.2 16.9 %copy-start.25 = (bf16[256,1536]{1,0:T(8,128)(2,1)S(1)}, bf16[256,1536]{1,0:T(8,128)(2,1)}, u32[]{:S(2)}) copy-start(bf16[256,1536]{1,0:T(8,128)(2,1)} %param.21) | copy-start | bytes 2359300
  7.2 17.5 %copy-start.48 = (f32[1536]{0:T(1024)S(1)}, f32[1536]{0:T(1024)}, u32[]{:S(2)}) copy-start(f32[1536]{0:T(1024)} %param.27) | copy-start | bytes 18436
  7.2 17.5 %copy-start.42 = (f32[1536]{0:T(1024)S(1)}, f32[1536]{0:T(1024)}, u32[]{:S(2)}) copy-start(f32[1536]{0:T(1024)} %param.26) | copy-start | bytes 18436
  7.2 77.9 %all-gather.4.cloned.1.call-start = ((), (), s32[]{:S(2)}) async-start(), calls=%async_computation.4 | async-start | bytes 5308416 | tf_op jit(solution)/shard_map/all_gather | solution.py:1165
  9.3 107.0 %all-gather.6.cloned.1.call-start = ((), (), s32[]{:S(2)}) async-start(), calls=%async_computation.5 | async-start | bytes 2654208 | tf_op jit(solution)/shard_map/all_gather | solution.py:1165
  22.3 95.6 %copy-start.13 = (bf16[64,1536]{1,0:T(8,128)(2,1)}, bf16[64,1536]{1,0:T(8,128)(2,1)S(1)}, u32[]{:S(2)}) copy-start(bf16[64,1536]{1,0:T(8,128)(2,1)S(1)} %get-tuple-element.71) | copy-start | bytes 589828
  24.1 234.0 %all-gather.8.cloned.1.call-start = ((), (), s32[]{:S(2)}) async-start(), calls=%async_computation.6 | async-start | bytes 3244032 | tf_op jit(solution)/shard_map/all_gather | solution.py:1257
  24.3 60.8 %copy-start.44 = (f32[256]{0:T(256)}, f32[256]{0:T(256)S(1)}, u32[]{:S(2)}) copy-start(f32[256]{0:T(256)S(1)} %broadcast_multiply_fusion.8) | copy-start | bytes 3076
  24.7 60.4 %copy-start.46 = (f32[256]{0:T(256)}, f32[256]{0:T(256)S(1)}, u32[]{:S(2)}) copy-start(f32[256]{0:T(256)S(1)} %add_rsqrt_fusion.2) | copy-start | bytes 3076
  90.4 40.1 %copy-start.2 = (bf16[1024,768]{1,0:T(8,128)(2,1)}, bf16[1024,768]{1,0:T(8,128)(2,1)S(1)}, u32[]{:S(2)}) copy-start(bf16[1024,768]{1,0:T(8,128)(2,1)S(1)} %fusion.28.refs_0_.kv_ref) | copy-start | bytes 4718596
  120.2 609.5 %reduce-scatter.7.cloned.1.call-start = ((), (), s32[]{:S(2)}) async-start(), calls=%async_computation.7 | async-start | bytes 3244032 | tf_op jit(solution)/shard_map/reduce_scatter | solution.py:1334
  130.1 25.1 %copy-start.5 = (bf16[1024,384]{1,0:T(8,128)(2,1)}, bf16[1024,384]{1,0:T(8,128)(2,1)S(1)}, u32[]{:S(2)}) copy-start(bf16[1024,384]{1,0:T(8,128)(2,1)S(1)} %convolution_convert_fusion.15.q_ref) | copy-start | bytes 2359300
  130.2 25.1 %copy-start.17 = (s32[8,1024]{1,0:T(8,128)}, s32[8,1024]{1,0:T(8,128)S(1)}, u32[]{:S(2)}) copy-start(s32[8,1024]{1,0:T(8,128)S(1)} %broadcast_in_dim.106.qt_ref) | copy-start | bytes 98308
  130.6 24.7 %copy-start.3 = (s32[2560,128]{1,0:T(8,128)}, s32[2560,128]{1,0:T(8,128)S(1)}, u32[]{:S(2)}) copy-start(s32[2560,128]{1,0:T(8,128)S(1)} %broadcast_in_dim.107.kt_ref) | copy-start | bytes 3932164
  155.9 529.7 %copy-start.12 = (bf16[1024,384]{1,0:T(8,128)(2,1)}, bf16[1024,384]{1,0:T(8,128)(2,1)S(1)}, u32[]{:S(2)}) copy-start(bf16[1024,384]{1,0:T(8,128)(2,1)S(1)} %get-tuple-element.65.o_ref) | copy-start | bytes 2359300
  159.3 94.3 %copy-start.26 = (bf16[256,1536]{1,0:T(8,128)(2,1)S(1)}, bf16[256,1536]{1,0:T(8,128)(2,1)}, u32[]{:S(2)}) copy-start(bf16[256,1536]{1,0:T(8,128)(2,1)} %param.21) | copy-start | bytes 2359300
  347.9 22.7 %copy-start.51 = (bf16[8,192,1536]{2,1,0:T(8,128)(2,1)S(1)}, bf16[8,192,1536]{2,1,0:T(8,128)(2,1)}, u32[]{:S(2)}) copy-start(bf16[8,192,1536]{2,1,0:T(8,128)(2,1)} %get-tuple-element.76) | copy-start | bytes 14155780
  375.9 55.5 %copy-start.31 = (bf16[256,1536]{1,0:T(8,128)(2,1)S(1)}, bf16[256,1536]{1,0:T(8,128)(2,1)}, u32[]{:S(2)}) copy-start(bf16[256,1536]{1,0:T(8,128)(2,1)} %param.25) | copy-start | bytes 2359300
  432.7 145.9 %copy-start.32 = (bf16[256,1536]{1,0:T(8,128)(2,1)}, bf16[256,1536]{1,0:T(8,128)(2,1)S(1)}, u32[]{:S(2)}) copy-start(bf16[256,1536]{1,0:T(8,128)(2,1)S(1)} %get-tuple-element.209) | copy-start | bytes 2359300
  595.1 167.3 %reduce-scatter.9.cloned.1.call-start = ((), (), s32[]{:S(2)}) async-start(), calls=%async_computation.8 | async-start | bytes 1327104 | tf_op jit(solution)/shard_map/reduce_scatter | solution.py:1170
  690.4 212.3 %reduce-scatter.13.cloned.1.call-start = ((), (), s32[]{:S(2)}) async-start(), calls=%async_computation.10 | async-start | bytes 2654208
  695.7 30.2 %copy-start.38 = (bf16[4,192,1536]{2,1,0:T(8,128)(2,1)S(1)}, bf16[4,192,1536]{2,1,0:T(8,128)(2,1)}, u32[]{:S(2)}) copy-start(bf16[4,192,1536]{2,1,0:T(8,128)(2,1)} %get-tuple-element.92) | copy-start | bytes 7077892
  734.9 209.3 %reduce-scatter.11.cloned.1.call-start = ((), (), s32[]{:S(2)}) async-start(), calls=%async_computation.9 | async-start | bytes 3981312 | tf_op jit(solution)/shard_map/reduce_scatter | solution.py:1170
  736.7 27.5 %copy-start.40 = (bf16[1,128,384]{2,1,0:T(8,128)(2,1)S(1)}, bf16[1,128,384]{2,1,0:T(8,128)(2,1)}, u32[]{:S(2)}) copy-start(bf16[1,128,384]{2,1,0:T(8,128)(2,1)} %reduce-scatter.7.cloned.1.call-done) | copy-start | bytes 294916
  740.4 27.2 %copy-start.6 = (bf16[1536,768]{1,0:T(8,128)(2,1)S(1)}, bf16[1536,768]{1,0:T(8,128)(2,1)}, u32[]{:S(2)}) copy-start(bf16[1536,768]{1,0:T(8,128)(2,1)} %get-tuple-element.89.refs_0_) | copy-start | bytes 7077892
  767.6 43.9 %copy-start.36 = (f32[1024,768]{1,0:T(8,128)S(1)}, f32[1024,768]{1,0:T(8,128)}, u32[]{:S(2)}) copy-start(f32[1024,768]{1,0:T(8,128)} %get-tuple-element.84) | copy-start | bytes 9437188
  767.6 44.4 %slice-start.4 = ((s8[4718592]{0:T(1024)(128)(4,1)}), s8[4194304]{0:T(1024)(128)(4,1)S(1)}, s32[]{:S(2)}) async-start(s8[4718592]{0:T(1024)(128)(4,1)} %bitcast.153), calls=%async_computation.15 | async-start | bytes 8388608
  818.6 60.8 %copy-start.27 = (bf16[256,1536]{1,0:T(8,128)(2,1)S(1)}, bf16[256,1536]{1,0:T(8,128)(2,1)}, u32[]{:S(2)}) copy-start(bf16[256,1536]{1,0:T(8,128)(2,1)} %param.21) | copy-start | bytes 2359300
  818.6 60.8 %copy-start.43 = (f32[1536]{0:T(1024)S(1)}, f32[1536]{0:T(1024)}, u32[]{:S(2)}) copy-start(f32[1536]{0:T(1024)} %param.26) | copy-start | bytes 18436
  818.6 60.8 %copy-start.45 = (f32[256]{0:T(256)S(1)}, f32[256]{0:T(256)}, u32[]{:S(2)}) copy-start(f32[256]{0:T(256)} %copy-done.44) | copy-start | bytes 3076
  818.6 60.8 %copy-start.47 = (f32[256]{0:T(256)S(1)}, f32[256]{0:T(256)}, u32[]{:S(2)}) copy-start(f32[256]{0:T(256)} %copy-done.46) | copy-start | bytes 3076
  818.7 61.6 %copy-start.24 = (bf16[4,256,1536]{2,1,0:T(8,128)(2,1)S(1)}, bf16[4,256,1536]{2,1,0:T(8,128)(2,1)}, u32[]{:S(2)}) copy-start(bf16[4,256,1536]{2,1,0:T(8,128)(2,1)} %copy-done.23) | copy-start | bytes 9437188
  (38 other events, 152.8 us)
Sparse Core Ops, SparseCore 0:
  10.5 59.2 all-gather.3
  72.3 35.1 all-gather.5
  120.3 76.3 all-gather.7
  595.2 127.6 reduce-scatter.6
  726.6 35.7 reduce-scatter.8
  766.0 48.6 reduce-scatter.12
  886.5 48.2 reduce-scatter.10
where the time goes:
time: 966 us; the launch traced here: 954 us
  Pallas kernels  704 us (73%)
  matrix products  128 us (13%)
  other arithmetic  47.2 us (5%)
  local copies, waits for them, and re-layouts  33.8 us (3%)
  waiting for transfers between devices  22.1 us (2%)
  between operations  18 us (2%)
    pallas_call x12, Pallas kernels, exchange(): pl.pallas_call(kernel, out_shape=[out for job in jobs for out in job.outs...  634 us
    dot_general x9, matrix products, matmul(): return jnp.dot(left, right, preferred_element_type=f32)  59.1 us
    dot_general x8, matrix products, against(): lax.dot_general(left, right, (((1,), (1,)), ((), ())), preferred_element_...  34.7 us
    dot_general x8, matrix products, transposed(): lax.dot_general(left, right, (((0,), (0,)), ((), ())), preferred_element_...  34.6 us
    pallas_call x1, Pallas kernels, self_backward(): pl.pallas_call(kernel, out_shape=[jax.ShapeDtypeStruct((tokens, width), b...  30.2 us
    pallas_call x1, Pallas kernels, self_forward(): pl.pallas_call(kernel, out_shape=[jax.ShapeDtypeStruct((tokens, width), b...  24.7 us
    reduce_scatter x2, waiting for transfers between devices, row_scatter(): return lax.psum_scatter(joined, 'row', scatter_dimension=0, tiled=True)  22 us
    unnamed x130, local copies, waits for them, and re-layouts  21.4 us
  transfers between devices with their start and end apart: 7, of which 1 were waited for; matrix products, arithmetic and copies ran while one was open for 11% of the time, Pallas kernels for 47%

commit v1 on v0

--- a/solution.py
+++ b/solution.py
@@ -1,5 +1,3 @@
-from functools import partial
-
 import jax
 import jax.numpy as jnp
 from jax import lax
@@ -117,9 +115,8 @@
 
         return right, left
 
-    def begin(self, refs):
-        x, out, held, load = refs[:4]
-        me, n = place()[1], self.n
+    def launch(self, refs):
+        x, me, n = refs[0], place()[1], self.n
         right, left = self.copies(refs)
 
         @pl.when(me < n - 1)
@@ -130,39 +127,45 @@
         def _():
             left(x, me, 0).start()
 
+    def begin(self, refs):
+        x, out, held, load = refs[:4]
+        me = place()[1]
+        self.launch(refs)
         own = pltpu.make_async_copy(x, held, load.at[0])
         own.start()
         own.wait()
         pltpu.make_async_copy(held, out.at[me], load.at[0]).start()
 
-    def run(self, refs):
+    def pass_on(self, refs, step):
         x, out = refs[:2]
         me, n = place()[1], self.n
         right, left = self.copies(refs)
-        for step in range(n - 1):
-            before, later = me - 1 - step, me + 1 + step
-
-            @pl.when(before >= 0)
-            def _():
-                right(x, me, step).wait_recv()
-
-            @pl.when((before >= 0) & (me < n - 1))
-            def _():
-                owner = jnp.maximum(before, 0)
-                right(out.at[owner], owner, step + 1).start()
-
-            @pl.when(later < n)
-            def _():
-                left(x, me, step).wait_recv()
-
-            @pl.when((later < n) & (me > 0))
-            def _():
-                owner = jnp.minimum(later, n - 1)
-                left(out.at[owner], owner, step + 1).start()
-
-    def end(self, refs):
-        x, out, held, load = refs[:4]
-        me, n = place()[1], self.n
+        before, later = me - 1 - step, me + 1 + step
+
+        @pl.when(before >= 0)
+        def _():
+            right(x, me, step).wait_recv()
+
+        @pl.when((before >= 0) & (me < n - 1))
+        def _():
+            owner = jnp.maximum(before, 0)
+            right(out.at[owner], owner, step + 1).start()
+
+        @pl.when(later < n)
+        def _():
+            left(x, me, step).wait_recv()
+
+        @pl.when((later < n) & (me > 0))
+        def _():
+            owner = jnp.minimum(later, n - 1)
+            left(out.at[owner], owner, step + 1).start()
+
+    def run(self, refs):
+        for step in range(self.n - 1):
+            self.pass_on(refs, step)
+
+    def sent(self, refs):
+        x, me, n = refs[0], place()[1], self.n
         right, left = self.copies(refs)
         for step in range(n):
 
@@ -174,7 +177,10 @@
             def _():
                 left(x, me, step).wait_send()
 
-        pltpu.make_async_copy(held, out.at[me], load.at[0]).wait()
+    def end(self, refs):
+        x, out, held, load = refs[:4]
+        self.sent(refs)
+        pltpu.make_async_copy(held, out.at[place()[1]], load.at[0]).wait()
 
 
 class LineScatter:
@@ -1157,6 +1163,359 @@
     )(ends, queries, keys, values, grad_attended, clips)
 
 
+def greet_col(barrier, n):
+    row, col = place()
+    for i in range(1, n):
+        greet(barrier, row, lax.rem(col + i, n))
+    return n - 1
+
+
+def hand_over(part, got, sends, recvs, to):
+    row, me = place()
+    return push(part.at[to], got.at[me], sends.at[to], recvs.at[me], row, to)
+
+
+def add_terms(out, part, got, sends, recvs, n):
+    me = place()[1]
+    for other in range(n):
+
+        @pl.when(me != other)
+        def _():
+            row = place()[0]
+            push(
+                part.at[other], got.at[other], sends.at[other], recvs.at[other], row, other
+            ).wait_recv()
+            out[...] += got[other].astype(f32)
+
+    for other in range(n):
+
+        @pl.when(me != other)
+        def _():
+            hand_over(part, got, sends, recvs, other).wait_send()
+
+
+def both_sides(step, n, work):
+    me = place()[1]
+    before, later = me - 1 - step, me + 1 + step
+
+    @pl.when(before >= 0)
+    def _():
+        work(jnp.maximum(before, 0))
+
+    @pl.when(later < n)
+    def _():
+        work(jnp.minimum(later, n - 1))
+
+
+def chunk_of(size):
+    return TILE if size % TILE == 0 else LANES
+
+
+def feed_forward(x, expand, reduce_block, n, rows, collective_id):
+    own, features = x.shape
+    hidden = expand.shape[1]
+    block = features // rows
+    line, gather = LineGather(x, n), RowGather(reduce_block, n=rows)
+    wide_shape, hidden_shape = (n, own, features), (n, own, hidden)
+    turn = min(1, n - 2)
+    step_h, step_f = chunk_of(hidden), chunk_of(features)
+
+    def kernel(
+        x_ref,
+        expand_ref,
+        block_ref,
+        out,
+        wide_out,
+        act_out,
+        slope_out,
+        reduce_out,
+        wide,
+        act,
+        slope,
+        expand_v,
+        reduce_v,
+        part,
+        got,
+        loads,
+        stores,
+        sends,
+        recvs,
+        line_a,
+        line_b,
+        line_c,
+        line_d,
+        *gather_refs,
+    ):
+        row, me = place()
+        line_refs = [x_ref, wide, None, None, line_a, line_b, line_c, line_d]
+        gather_refs = [block_ref, reduce_out, *gather_refs]
+        barrier = pltpu.get_barrier_semaphore()
+        pl.semaphore_wait(barrier, greet_col(barrier, n) + gather.greet(barrier))
+        line.launch(line_refs)
+        own_load = pltpu.make_async_copy(x_ref, wide.at[me], loads.at[0])
+        expand_load = pltpu.make_async_copy(expand_ref, expand_v, loads.at[1])
+        own_load.start()
+        expand_load.start()
+        gather.begin(gather_refs)
+        own_load.wait()
+        expand_load.wait()
+
+        def first(b):
+            @pl.loop(0, hidden // step_h)
+            def _(i):
+                spot = pl.ds(pl.multiple_of(i * step_h, step_h), step_h)
+                value = matmul(wide[b], expand_v[:, spot])
+                upper = 0.5 * (1.0 + lax.erf(value * (0.5**0.5)))
+                bell = jnp.exp(-0.5 * value * value) * (0.5 / jnp.pi) ** 0.5
+                act[b, :, spot] = (value * upper).astype(bf16)
+                slope[b, :, spot] = (upper + value * bell).astype(bf16)
+
+        def second(b, mine=False):
+            @pl.loop(0, features // step_f)
+            def _(i):
+                spot = pl.ds(pl.multiple_of(i * step_f, step_f), step_f)
+                value = against(act[b], reduce_v[spot, :])
+                if mine:
+                    out[:, spot] = value
+                else:
+                    part[b, :, spot] = value.astype(bf16)
+
+            if not mine:
+                hand_over(part, got, sends, recvs, b).start()
+
+        first(me)
+        for step in range(n - 1):
+            line.pass_on(line_refs, step)
+            both_sides(step, n, first)
+            if step == turn:
+                gather.end(gather_refs)
+                weights = [
+                    pltpu.make_async_copy(
+                        reduce_out.at[r], reduce_v.at[pl.ds(r * block, block)], loads.at[2 + r]
+                    )
+                    for r in range(rows)
+                ]
+                for copy in weights:
+                    copy.start()
+                for copy in weights:
+                    copy.wait()
+                for earlier in range(step, -1, -1):
+                    both_sides(earlier, n, second)
+            elif step > turn:
+                both_sides(step, n, second)
+        kept = [(wide, wide_out), (act, act_out), (slope, slope_out)]
+        kept = [pltpu.make_async_copy(a, b, stores.at[i]) for i, (a, b) in enumerate(kept)]
+        for copy in kept:
+            copy.start()
+        second(me, mine=True)
+        add_terms(out, part, got, sends, recvs, n)
+        line.sent(line_refs)
+        for copy in kept:
+            copy.wait()
+
+    return pl.pallas_call(
+        kernel,
+        out_shape=[
+            jax.ShapeDtypeStruct((own, features), f32),
+            jax.ShapeDtypeStruct(wide_shape, bf16),
+            jax.ShapeDtypeStruct(hidden_shape, bf16),
+            jax.ShapeDtypeStruct(hidden_shape, bf16),
+            jax.ShapeDtypeStruct((rows, block, hidden), bf16),
+        ],
+        in_specs=[ANY] * 3,
+        out_specs=[VMEM] + [ANY] * 4,
+        scratch_shapes=[
+            pltpu.VMEM(wide_shape, bf16),
+            pltpu.VMEM(hidden_shape, bf16),
+            pltpu.VMEM(hidden_shape, bf16),
+            pltpu.VMEM((features, hidden), bf16),
+            pltpu.VMEM((features, hidden), bf16),
+            pltpu.VMEM(wide_shape, bf16),
+            pltpu.VMEM(wide_shape, bf16),
+            dma(2 + rows),
+            dma(3),
+            dma(n),
+            dma(n),
+        ]
+        + [dma(n)] * 4
+        + gather.scratch,
+        compiler_params=pltpu.CompilerParams(
+            collective_id=collective_id, has_side_effects=True, vmem_limit_bytes=56 << 20
+        ),
+        cost_estimate=CHEAP,
+        name="feed_forward",
+    )(x, expand, reduce_block)
+
+
+def feed_forward_back(grad, expand, reduce, act, slope, wide, n, rows, collective_id):
+    own, features = grad.shape
+    hidden = expand.shape[1]
+    half, block = rows // 2, features // rows
+    line = LineGather(grad, n)
+    wide_shape, hidden_shape = (n, own, features), (n, own, hidden)
+    step_h, step_f = chunk_of(hidden), chunk_of(features)
+
+    def kernel(
+        g_ref,
+        expand_ref,
+        reduce_ref,
+        act_ref,
+        slope_ref,
+        wide_ref,
+        out,
+        mine_e,
+        mine_r,
+        swap_e,
+        swap_r,
+        g_wide,
+        expand_v,
+        reduce_v,
+        act_v,
+        slope_v,
+        wide_v,
+        part,
+        got,
+        sum_e,
+        sum_r,
+        loads,
+        stores,
+        sends,
+        recvs,
+        swap_send,
+        swap_recv,
+        line_a,
+        line_b,
+        line_c,
+        line_d,
+    ):
+        row, me = place()
+        line_refs = [g_ref, g_wide, None, None, line_a, line_b, line_c, line_d]
+        barrier = pltpu.get_barrier_semaphore()
+        other = 1 - lax.rem(row, 2)
+        sibling = row + 2 * other - 1
+        count = greet_col(barrier, n)
+        place_of = place()[1]
+        greet(barrier, sibling, place_of)
+        pl.semaphore_wait(barrier, count + 1)
+        line.launch(line_refs)
+        pairs = [
+            (g_ref, g_wide.at[me]),
+            (reduce_ref, reduce_v),
+            (slope_ref, slope_v),
+            (expand_ref, expand_v),
+            (act_ref, act_v),
+            (wide_ref, wide_v),
+        ]
+        copies = [pltpu.make_async_copy(a, b, loads.at[i]) for i, (a, b) in enumerate(pairs)]
+        for copy in copies:
+            copy.start()
+        for copy in copies:
+            copy.wait()
+
+        def work(b, mine=False):
+            @pl.loop(0, hidden // step_h)
+            def _(i):
+                spot = pl.ds(pl.multiple_of(i * step_h, step_h), step_h)
+                value = matmul(g_wide[b], reduce_v[:, spot])
+                slope_v[b, :, spot] = (value * slope_v[b, :, spot].astype(f32)).astype(bf16)
+
+            @pl.loop(0, features // step_f)
+            def _(i):
+                spot = pl.ds(pl.multiple_of(i * step_f, step_f), step_f)
+                value = against(slope_v[b], expand_v[spot, :])
+                if mine:
+                    out[:, spot] = value
+                else:
+                    part[b, :, spot] = value.astype(bf16)
+
+            if not mine:
+                hand_over(part, got, sends, recvs, b).start()
+
+        work(me, mine=True)
+        for step in range(n - 1):
+            line.pass_on(line_refs, step)
+            both_sides(step, n, work)
+
+        def weight_sums(left, right, total):
+            @pl.loop(0, features // step_f)
+            def _(i):
+                spot = pl.ds(pl.multiple_of(i * step_f, step_f), step_f)
+                rows_of = left[:, :, spot].reshape(n * own, step_f)
+                for start in range(0, hidden, 2 * step_h):
+                    size = min(2 * step_h, hidden - start)
+                    columns = right[:, :, start : start + size].reshape(n * own, size)
+                    total[spot, start : start + size] = transposed(rows_of, columns).astype(bf16)
+
+        def swaps(total, swap, first):
+            return [
+                push(
+                    total.at[pl.ds((2 * j + other) * block, block)],
+                    swap.at[j],
+                    swap_send.at[first + j],
+                    swap_recv.at[first + j],
+                    sibling,
+                    place_of,
+                )
+                for j in range(half)
+            ]
+
+        def keeps(total, mine, first):
+            return [
+                pltpu.make_async_copy(
+                    total.at[pl.ds((2 * j + 1 - other) * block, block)],
+                    mine.at[j],
+                    stores.at[first + j],
+                )
+                for j in range(half)
+            ]
+
+        weight_sums(g_wide, act_v, sum_r)
+        late = swaps(sum_r, swap_r, 0) + keeps(sum_r, mine_r, 0)
+        for copy in late:
+            copy.start()
+        weight_sums(wide_v, slope_v, sum_e)
+        more = swaps(sum_e, swap_e, half) + keeps(sum_e, mine_e, half)
+        for copy in more:
+            copy.start()
+        add_terms(out, part, got, sends, recvs, n)
+        line.sent(line_refs)
+        for copy in late + more:
+            copy.wait()
+
+    half_shape = (half, block, hidden)
+    return pl.pallas_call(
+        kernel,
+        out_shape=[jax.ShapeDtypeStruct((own, features), f32)]
+        + [jax.ShapeDtypeStruct(half_shape, bf16)] * 4,
+        in_specs=[ANY] * 6,
+        out_specs=[VMEM] + [ANY] * 4,
+        scratch_shapes=[
+            pltpu.VMEM(wide_shape, bf16),
+            pltpu.VMEM((features, hidden), bf16),
+            pltpu.VMEM((features, hidden), bf16),
+            pltpu.VMEM(hidden_shape, bf16),
+            pltpu.VMEM(hidden_shape, bf16),
+            pltpu.VMEM(wide_shape, bf16),
+            pltpu.VMEM(wide_shape, bf16),
+            pltpu.VMEM(wide_shape, bf16),
+            pltpu.VMEM((features, hidden), bf16),
+            pltpu.VMEM((features, hidden), bf16),
+            dma(6),
+            dma(2 * half),
+            dma(n),
+            dma(n),
+            dma(2 * half),
+            dma(2 * half),
+        ]
+        + [dma(n)] * 4,
+        compiler_params=pltpu.CompilerParams(
+            collective_id=collective_id, has_side_effects=True, vmem_limit_bytes=58 << 20
+        ),
+        cost_estimate=CHEAP,
+        name="feed_forward_back",
+    )(grad, expand, reduce, act, slope, wide)
+
+
 def after(x, *others):
     return lax.optimization_barrier((x,) + others)[0]
 
@@ -1207,11 +1566,30 @@
     aligned = width % LANES == 0
 
     packed = (clip_ids * 2 + valid_mask).reshape(8, tokens // 8)
+    weights_one = row_gather(
+        self_query, self_key, self_value, self_output.T, cross_key, cross_value
+    )
+    normed_one, unit_one, inverse_one = normalize(frames, self_norm_gain, self_norm_bias)
     text_local = text_states.reshape(seg_count * text_rows, -1)
-    first = exchange(
-        "gather_tags", 1, RowGatherSmall(packed, rows), *([ColWide(text_local, n=cols)] if aligned else [])
-    )
-    packed_all = first[0][0].reshape(rows * tokens)
+    (wide_one,), (expand_full,), (packed_all,), *text_full = exchange(
+        "gather_one",
+        2,
+        LineGather(normed_one, cols),
+        RowGather(expand_weight, n=rows),
+        RowGatherSmall(packed, rows),
+        *([ColWide(text_local, n=cols)] if aligned else []),
+    )
+    wide_one = wide_one.reshape(tokens, features)
+    expand_full = expand_full.reshape(features, hidden)
+    packed_all = packed_all.reshape(rows * tokens)
+    if aligned:
+        text_full = text_full[0][0]
+    else:
+        text_full = lax.all_gather(text_local, "col", axis=1, tiled=True)
+    query_full, kv_full = weights_one[:, :width], weights_one[:, width : 3 * width]
+    output_full, text_weights = weights_one[:, 3 * width : 4 * width], weights_one[:, 4 * width :]
+    ckey_full, cvalue_full = text_weights[:, :width], text_weights[:, width:]
+
     valid_sum = jnp.sum(packed_all % 2).astype(f32)
     padded = jnp.concatenate([jnp.full((halo,), -2, jnp.int32), packed_all])
     window = lax.dynamic_slice_in_dim(padded, row * tokens, halo + tokens)
@@ -1227,23 +1605,9 @@
     clip_rows = jnp.broadcast_to(own_clips[None, :], (8, own))
     ends = jnp.stack([own_clips[0], own_clips[-1]])
 
-    weights_one = row_gather(self_query, self_key, self_value, self_output.T)
-    normed_one, unit_one, inverse_one = normalize(frames, self_norm_gain, self_norm_bias)
-    (wide_one,), (expand_full,) = exchange(
-        "gather_one", 2, LineGather(normed_one, cols), RowGather(expand_weight, n=rows)
-    )
-    expand_full = expand_full.reshape(features, hidden)
-    wide_one = wide_one.reshape(tokens, features)
-    weights_text = row_gather(after(cross_key, packed_all), cross_value)
-    if aligned:
-        text_full = first[1][0]
-    else:
-        text_full = lax.all_gather(text_local, "col", axis=1, tiled=True)
-    ckey_full, cvalue_full = weights_text[:, :width], weights_text[:, width:]
-    query_full, kv_full = weights_one[:, :width], weights_one[:, width : 3 * width]
-    output_full = weights_one[:, 3 * width :]
-
-    key_values = matmul(wide_one, kv_full).astype(bf16)
+    text_kv = matmul(text_full, text_weights).astype(bf16)
+    text_all = lax.all_gather(text_kv, ("row", "col"), axis=0)
+    key_values = matmul(after(wide_one, text_kv), kv_full).astype(bf16)
     queries = matmul(wide_one, query_full).astype(bf16)
     cross_local = (cross_query, cross_output.T)
     (halo_kv,), *cross_wide = exchange(
@@ -1252,11 +1616,8 @@
         HaloGather(key_values, halo, rows),
         *([ColWide(*cross_local, n=cols)] if aligned else []),
     )
-    text_full = after(text_full, halo_kv)
-    text_kv = jnp.stack([matmul(text_full, ckey_full), matmul(text_full, cvalue_full)]).astype(bf16)
-    text_all = lax.all_gather(text_kv, ("row", "col"), axis=0)
     attended_one, lse = self_forward(
-        after(queries, text_kv), key_values, halo_kv, query_tags, key_tags, lows
+        queries, key_values, halo_kv, query_tags, key_tags, lows
     )
     if aligned:
         cross_wide = cross_wide[0]
@@ -1272,8 +1633,8 @@
     cquery_full, coutput_full = (x.reshape(features, features) for x in cross_full)
     after_self = (frames.astype(f32) + branch_one).astype(bf16)
 
-    text_all = text_all.reshape(rows, cols, 2, seg_count, text_rows, width)
-    text_all = text_all.transpose(2, 3, 0, 4, 1, 5).reshape(2, seg_count * text, features)
+    text_all = text_all.reshape(rows, cols, seg_count, text_rows, 2, width)
+    text_all = text_all.transpose(4, 2, 0, 3, 1, 5).reshape(2, seg_count * text, features)
     normed_two, unit_two, inverse_two = normalize(after_self, cross_norm_gain, cross_norm_bias)
     cross_queries = matmul(normed_two, cquery_full).astype(bf16)
     attended_two = cross_forward(cross_queries, text_all[0], text_all[1], clip_rows, ends, text)
@@ -1282,34 +1643,31 @@
     normed_three, unit_three, inverse_three = normalize(
         after_cross, final_norm_gain, final_norm_bias
     )
-    (wide_three,), (reduce_full,) = exchange(
-        "gather_three", 5, LineGather(normed_three, cols), RowGather(reduce_weight.T, n=rows)
+    branch_three, wide_three, activated, slope, reduce_full = feed_forward(
+        normed_three, expand_full, reduce_weight.T, cols, rows, 5
     )
     reduce_full = reduce_full.reshape(features, hidden)
-    wide_three = wide_three.reshape(tokens, features)
-    expanded = matmul(wide_three, expand_full)
-    activated = jax.nn.gelu(expanded, approximate=False).astype(bf16)
-    partial_three = against(activated, reduce_full).astype(bf16)
-    ((branch_three,),) = exchange("scatter_three", 6, LineScatter(partial_three, cols))
     layer_out = (after_cross.astype(f32) + branch_three).astype(bf16)
     error = layer_out.astype(f32) - teacher_states.astype(f32)
     squared = jnp.sum(error * error * own_valid[:, None])
     grad_out = error * own_valid[:, None] * (tokens * rows / valid_sum)
 
-    ((grad_wide,),) = exchange("gather_grad", 7, LineGather(grad_out.astype(bf16), cols))
-    grad_wide = grad_wide.reshape(tokens, features)
-    grad_activated = matmul(grad_wide, reduce_full)
-    unused, gelu_back = jax.vjp(partial(jax.nn.gelu, approximate=False), expanded)
-    grad_expanded = gelu_back(grad_activated)[0].astype(bf16)
-    grad_reduce = transposed(grad_wide, activated).astype(bf16)
-    grad_expand = transposed(wide_three, grad_expanded).astype(bf16)
+    back_three, *feed = feed_forward_back(
+        grad_out.astype(bf16),
+        expand_full,
+        reduce_full,
+        activated,
+        slope,
+        wide_three,
+        cols,
+        rows,
+        7,
+    )
     by_row = (half, 2, features // rows)
-    feed = [x.reshape(by_row + (hidden,)) for x in (grad_expand, grad_reduce)]
-    back_three = against(grad_expanded, expand_full).astype(bf16)
-    (back_three,), swapped = exchange(
-        "scatter_grad_three", 8, LineScatter(back_three, cols), SiblingSwap(*feed)
-    )
-    feed = [own_half(x, y, parity) for x, y in zip(feed, swapped)]
+    feed = [
+        (mine.astype(f32) + swapped.astype(f32)).astype(bf16)
+        for mine, swapped in zip(feed[:2], feed[2:])
+    ]
     inner_three, gain_three, shift_three = normalize_back(
         back_three, unit_three, inverse_three, final_norm_gain
     )
@@ -1358,15 +1716,18 @@
     )
     mine_text = after(mine_text, grad_queries).reshape(2, seg_count * text_rows, width)
     grad_text_weights = [transposed(text_full, mine_text[i]).astype(bf16) for i in range(2)]
-    grad_output = transposed(grad_wide_one, attended_one).astype(bf16)
-    summed_output = row_scatter(after(grad_output, mine_text))
+    grad_output = transposed(grad_wide_one, attended_one).astype(bf16).reshape(by_row + (width,))
     summed_text = row_scatter(grad_text_weights[0], grad_text_weights[1])
     text_partial = against(mine_text[0], ckey_full) + against(mine_text[1], cvalue_full)
     text_partial = text_partial.astype(bf16)
 
-    (returned,) = exchange(
-        "return_halo", 10, HaloReturn(after(grad_kv_halo, text_partial), tokens, rows)
-    )
+    returned, (swapped,) = exchange(
+        "return_halo",
+        10,
+        HaloReturn(after(grad_kv_halo, text_partial), tokens, rows),
+        SiblingSwap(grad_output),
+    )
+    cross.append(own_half(grad_output, swapped, parity))
     for i, piece in enumerate(returned):
         piece = jnp.where(row + i + 1 < rows, piece.astype(f32), 0.0)
         grad_kv_own = grad_kv_own + jnp.pad(piece, ((tokens - piece.shape[0], 0), (0, 0)))
@@ -1388,9 +1749,11 @@
         grad_text = lax.psum_scatter(text_partial, "col", scatter_dimension=1, tiled=True)
     grad_text = grad_text.astype(f32).reshape(seg_count, text_rows, width)
     cross = [
-        total_of(lax.dynamic_index_in_dim(x, chip, 0, keepdims=False), y, chip).astype(bf16)
+        total_of(lax.dynamic_index_in_dim(x, chip, 0, keepdims=False), y, chip)
         for x, y in zip(cross, received)
     ]
+    summed_output = cross.pop()
+    cross = [x.astype(bf16) for x in cross]
     inner_one, gain_one, shift_one = normalize_back(
         back_one, unit_one, inverse_one, self_norm_gain
     )
@@ -1412,7 +1775,7 @@
     (small,), *received = exchange(
         "sum_small",
         12,
-        AllSum(after(small, summed_text, summed_output), rows, cols),
+        AllSum(after(small, summed_text), rows, cols),
         *([ColExchange(*cross, n=cols, known=True)] if aligned else []),
     )
     if aligned:
@@ -1440,7 +1803,7 @@
         summed_one[:, :width],
         summed_one[:, width : 2 * width],
         summed_one[:, 2 * width : 3 * width],
-        summed_output.astype(f32).T,
+        summed_output.T,
         cross[0].astype(f32),
         summed_text[:, :width],
         summed_text[:, width:],

time: 966 us -> 906 us (0.938)
  matrix products: 128 us -> 64.5 us
  Pallas kernels: 704 us -> 736 us
  waiting for transfers between devices: 22.1 us -> 0.11 us
    pallas_call x0 -> x2, Pallas kernels: none -> 257 us  [the longest x1 141 us: feed_forward_back(): pl.pallas_call(kernel, out_shape=[jax.ShapeDtypeStruct((own, features), f...]
    pallas_call x12 -> x7, Pallas kernels: 634 us -> 416 us  [exchange(): pl.pallas_call(kernel, out_shape=[out for job in jobs for out in job.outs...]
    dot_general x9 -> x6, matrix products: 59.1 us -> 25.9 us  [matmul(): return jnp.dot(left, right, preferred_element_type=f32)]
    reduce_scatter x2 -> x1, waiting for transfers between devices: 22 us -> 0.01 us  [row_scatter(): return lax.psum_scatter(joined, 'row', scatter_dimension=0, tiled=True)]
    dot_general x8 -> x6, matrix products: 34.7 us -> 18.9 us  [against(): lax.dot_general(left, right, (((1,), (1,)), ((), ())), preferred_element_...]
    dot_general x8 -> x6, matrix products: 34.6 us -> 19.8 us  [transposed(): lax.dot_general(left, right, (((0,), (0,)), ((), ())), preferred_element_...]
    unnamed x130 -> x127, local copies, waits for them, and re-layouts: 21.4 us -> 23.2 us
  transfers between devices with their start and end apart: 7 -> 5, of which waited for: 1 -> 0; matrix products, arithmetic and copies ran while one was open for 11% -> 10% of each run, Pallas kernels for 47% -> 51%
where the time goes in v1:
time: 906 us; the launch traced here: 901 us
  Pallas kernels  736 us (81%)
  matrix products  64.5 us (7%)
  other arithmetic  48.7 us (5%)
  local copies, waits for them, and re-layouts  34.2 us (4%)
  between operations  17.8 us (2%)
    pallas_call x7, Pallas kernels, exchange(): pl.pallas_call(kernel, out_shape=[out for job in jobs for out in job.outs...  416 us
    pallas_call x1, Pallas kernels, feed_forward_back(): pl.pallas_call(kernel, out_shape=[jax.ShapeDtypeStruct((own, features), f...  141 us
    pallas_call x1, Pallas kernels, feed_forward(): pl.pallas_call(kernel, out_shape=[jax.ShapeDtypeStruct((own, features), f...  116 us
    pallas_call x1, Pallas kernels, self_backward(): pl.pallas_call(kernel, out_shape=[jax.ShapeDtypeStruct((tokens, width), b...  26.2 us
    dot_general x6, matrix products, matmul(): return jnp.dot(left, right, preferred_element_type=f32)  25.9 us
    unnamed x127, local copies, waits for them, and re-layouts  23.2 us
    pallas_call x1, Pallas kernels, self_forward(): pl.pallas_call(kernel, out_shape=[jax.ShapeDtypeStruct((tokens, width), b...  20.6 us
    dot_general x6, matrix products, transposed(): lax.dot_general(left, right, (((0,), (0,)), ((), ())), preferred_element_...  19.8 us
  transfers between devices with their start and end apart: 5, of which 0 were waited for; matrix products, arithmetic and copies ran while one was open for 10% of the time, Pallas kernels for 51%

profile of v1, /device:TPU:0, one launch (start us, length us, event | category | flops | bytes accessed | tf_op | source)
XLA Modules:
  0.0 901.1 jit_solution(11268374628021822177)
XLA Ops:
  14.2 67.8 %gather_one.1 = (bf16[4,256,1536]{2,1,0:T(8,128)(2,1)S(1)}, bf16[8,192,1536]{2,1,0:T(8,128)(2,1)}, s32[8,8,128]{2,1,0:T(8,128)S(1)}, bf16[64,1536]{1,0:T(8,128)(2,1)S(1)}) custom-call(bf16[256,1536]{1,0:T(8,128)(2,1)S(1)} %fusion.34.refs_0_, bf16[192,1536]{1,0:T(8,128)(2,1)S(1)} %copy-done.11, s32[8,128]{1,0:T(8,128)S(1)} %get-tuple-element.236.refs_2_, ...), custom_call_target="tpu_custom_call" | custom-call | flops 1048576 | bytes 1048576 | tf_op jit(solution)/shard_map/gather_one/pallas_call | solution.py:757
  83.5 3.0 fusion.51
  91.1 4.3 fusion.22.refs_0_.kv_ref
  95.4 25.1 %gather_halo.1 = (bf16[1536,768]{1,0:T(8,128)(2,1)S(1)}, bf16[192,1536]{1,0:T(8,128)(2,1)S(1)}, bf16[192,1536]{1,0:T(8,128)(2,1)S(1)}) custom-call(bf16[1024,768]{1,0:T(8,128)(2,1)S(1)} %fusion.22.refs_0_.kv_ref, bf16[192,384]{1,0:T(8,128)(2,1)S(1)} %copy-done.13, bf16[192,384]{1,0:T(8,128)(2,1)S(1)} %bitcast.98), custom_call_target="tpu_custom_call" | custom-call | flops 1048576 | bytes 1048576 | tf_op jit(solution)/shard_map/gather_halo/pallas_call | solution.py:757
  120.5 3.9 convolution_convert_fusion.11.q_ref
  124.9 20.6 %self_forward.1 = (bf16[1024,384]{1,0:T(8,128)(2,1)S(1)}, f32[8,1024]{1,0:T(8,128)S(1)}) custom-call(s32[4]{0:T(128)S(1)} %and_select_fusion.low_ref, bf16[1024,384]{1,0:T(8,128)(2,1)S(1)} %convolution_convert_fusion.11.q_ref, bf16[1024,768]{1,0:T(8,128)(2,1)S(1)} %fusion.22.refs_0_.kv_ref, bf16[1536,768]{1,0:T(8,128)(2,1)} %copy-done.4, ...), custom_call_target="tpu_custom_call" | custom-call | flops 1048576 | bytes 1048576 | tf_op jit(solution)/shard_map/self_forward/pallas_call | solution.py:877
  145.5 3.4 convolution_convert_fusion.3
  148.9 95.9 %scatter_one.1 = (f32[256,1536]{1,0:T(8,128)S(1)}, bf16[8,192,1536]{2,1,0:T(8,128)(2,1)}, bf16[8,192,1536]{2,1,0:T(8,128)(2,1)}) custom-call(bf16[4,256,1536]{2,1,0:T(8,128)(2,1)S(1)} %bitcast.93, bf16[192,1536]{1,0:T(8,128)(2,1)S(1)} %get-tuple-element.74.refs_1_, bf16[192,1536]{1,0:T(8,128)(2,1)S(1)} %get-tuple-element.75.refs_2_), custom_call_target="tpu_custom_call" | custom-call | flops 1048576 | bytes 1048576 | tf_op jit(solution)/shard_map/scatter_one/pallas_call | solution.py:757
  245.6 3.8 convolution_convert_fusion.9.q_ref
  252.6 6.1 cross_forward.1
  262.2 116.2 %feed_forward.1 = (f32[256,1536]{1,0:T(8,128)}, bf16[4,256,1536]{2,1,0:T(8,128)(2,1)}, bf16[4,256,1536]{2,1,0:T(8,128)(2,1)}, bf16[4,256,1536]{2,1,0:T(8,128)(2,1)}, bf16[8,192,1536]{2,1,0:T(8,128)(2,1)}) custom-call(bf16[256,1536]{1,0:T(8,128)(2,1)} %add_convert_fusion.4.x_ref, bf16[1536,1536]{1,0:T(8,128)(2,1)} %bitcast.106, bf16[192,1536]{1,0:T(8,128)(2,1)} %bitcast.115), custom_call_target="tpu_custom_call" | custom-call | flops 1048576 | bytes 1048576 | tf_op jit(solution)/shard_map/feed_forward/pallas_call | solution.py:1316
  378.4 2.7 multiply_reduce_fusion
  382.3 140.9 %feed_forward_back.1 = (f32[256,1536]{1,0:T(8,128)}, bf16[4,192,1536]{2,1,0:T(8,128)(2,1)}, bf16[4,192,1536]{2,1,0:T(8,128)(2,1)}, bf16[4,192,1536]{2,1,0:T(8,128)(2,1)}, bf16[4,192,1536]{2,1,0:T(8,128)(2,1)}) custom-call(bf16[256,1536]{1,0:T(8,128)(2,1)} %fusion.42.g_ref, bf16[1536,1536]{1,0:T(8,128)(2,1)} %bitcast.107, bf16[1536,1536]{1,0:T(8,128)(2,1)} %bitcast.112, ...), custom_call_target="tpu_custom_call" | custom-call | flops 1048576 | bytes 1048576 | tf_op jit(solution)/shard_map/feed_forward_back/pallas_call | solution.py:1486
  526.2 4.3 convolution_convert_fusion.8.do_ref
  530.6 9.2 %cross_backward.1 = (bf16[256,1536]{1,0:T(8,128)(2,1)S(1)}, bf16[512,1536]{1,0:T(8,128)(2,1)S(1)}, bf16[512,1536]{1,0:T(8,128)(2,1)S(1)}) custom-call(s32[2]{0:T(128)S(1)} %copy-done.18, bf16[256,1536]{1,0:T(8,128)(2,1)S(1)} %convolution_convert_fusion.9.q_ref, bf16[512,1536]{1,0:T(8,128)(2,1)} %bitcast.92, bf16[512,1536]{1,0:T(8,128)(2,1)} %bitcast.90, ...), custom_call_target="tpu_custom_call" | custom-call | flops 1048576 | bytes 1048576 | tf_op jit(solution)/shard_map/cross_backward/pallas_call | solution.py:1136
  539.8 3.8 convolution_convert_fusion.2
  543.6 2.8 fusion.31
  550.4 3.8 convolution_convert_fusion.1
  557.3 3.7 add_convert_fusion
  561.0 70.7 %gather_grad_one.1 = (bf16[4,256,1536]{2,1,0:T(8,128)(2,1)}, bf16[4,192,1536]{2,1,0:T(8,128)(2,1)S(1)}, bf16[4,192,1536]{2,1,0:T(8,128)(2,1)S(1)}, bf16[4,192,1536]{2,1,0:T(8,128)(2,1)}, bf16[4,192,1536]{2,1,0:T(8,128)(2,1)}) custom-call(bf16[256,1536]{1,0:T(8,128)(2,1)S(1)} %get-tuple-element.222.refs_0_, bf16[4,192,1536]{2,1,0:T(8,128)(2,1)} %get-tuple-element.243.refs_1_, ...), custom_call_target="tpu_custom_call" | custom-call | flops 1048576 | bytes 1048576 | tf_op jit(solution)/shard_map/gather_grad_one/pallas_call | solution.py:757
  631.7 6.6 convolution_convert_fusion.10.do_ref
  638.3 26.2 %self_backward.1 = (bf16[1024,384]{1,0:T(8,128)(2,1)}, f32[1024,768]{1,0:T(8,128)}, bf16[1536,768]{1,0:T(8,128)(2,1)}) custom-call(s32[4]{0:T(128)} %copy-done.17, bf16[1024,384]{1,0:T(8,128)(2,1)} %copy-done.5, bf16[1024,768]{1,0:T(8,128)(2,1)} %copy-done.2, bf16[1536,768]{1,0:T(8,128)(2,1)} %copy-done.4, bf16[1024,384]{1,0:T(8,128)(2,1)} %copy-done.9, ...), custom_call_target="tpu_custom_call" | custom-call | flops 1048576 | bytes 1048576 | tf_op jit(solution)/shard_map/self_backward/pallas_call | solution.py:1001
  664.5 3.9 convolution_convert_fusion.7
  668.4 3.9 fusion.refs_2_
  672.3 3.8 fusion.1.refs_1_
  680.2 4.3 copy.72
  688.9 70.4 %return_halo.1 = (bf16[1024,768]{1,0:T(8,128)(2,1)S(1)}, bf16[512,768]{1,0:T(8,128)(2,1)S(1)}, bf16[4,192,384]{2,1,0:T(8,128)(2,1)S(1)}) custom-call(bf16[1536,768]{1,0:T(8,128)(2,1)} %get-tuple-element.99.refs_0_, bf16[4,2,192,384]{3,2,1,0:T(8,128)(2,1)S(1)} %bitcast.94), custom_call_target="tpu_custom_call" | custom-call | flops 1048576 | bytes 1048576 | tf_op jit(solution)/shard_map/return_halo/pallas_call | solution.py:757
  762.4 7.7 convolution_convert_fusion.4
  770.0 54.5 %scatter_grad_one.1 = (f32[256,1536]{1,0:T(8,128)S(1)}, bf16[4,192,1536]{2,1,0:T(8,128)(2,1)S(1)}, bf16[4,192,1536]{2,1,0:T(8,128)(2,1)}, bf16[4,192,384]{2,1,0:T(8,128)(2,1)S(1)}, bf16[4,64,384]{2,1,0:T(8,128)(2,1)S(1)}) custom-call(bf16[4,256,1536]{2,1,0:T(8,128)(2,1)} %bitcast.114, bf16[4,192,1536]{2,1,0:T(8,128)(2,1)} %fusion.1.refs_1_, ...), custom_call_target="tpu_custom_call" | custom-call | flops 1048576 | bytes 1048576 | tf_op jit(solution)/shard_map/scatter_grad_one/pallas_call | solution.py:757
  827.4 5.7 convolution_convert_fusion
  835.4 6.1 select_reduce_fusion
  851.7 32.2 %sum_small.1 = (f32[8,1536]{1,0:T(8,128)S(1)}, bf16[4,192,384]{2,1,0:T(8,128)(2,1)S(1)}, bf16[4,192,384]{2,1,0:T(8,128)(2,1)S(1)}) custom-call(f32[8,1536]{1,0:T(8,128)S(1)} %stack.43.refs_0_, bf16[192,1536]{1,0:T(8,128)(2,1)S(1)} %fusion.49.refs_1_, bf16[192,1536]{1,0:T(8,128)(2,1)S(1)} %fusion.48.refs_2_), custom_call_target="tpu_custom_call" | custom-call | flops 1048576 | bytes 1048576 | tf_op jit(solution)/shard_map/sum_small/pallas_call | solution.py:757
  (220 shorter events, 66.4 us)
Async XLA Ops:
  7.2 4.9 copy-start.45
  7.2 5.9 copy-start.22
  7.2 76.3 %all-gather.4.cloned.1.call-start = ((), (), s32[]{:S(2)}) async-start(), calls=%async_computation.3 | async-start | bytes 7962624 | tf_op jit(solution)/shard_map/all_gather | solution.py:1524
  13.1 236.3 %all-gather.6.cloned.1.call-start = ((), (), s32[]{:S(2)}) async-start(), calls=%async_computation.6 | async-start | bytes 3244032 | tf_op jit(solution)/shard_map/all_gather | solution.py:1609
  83.5 7.5 copy-start.20
  86.6 589.5 %reduce-scatter.6.cloned.1.call-start = ((), (), s32[]{:S(2)}) async-start(), calls=%async_computation.4 | async-start | bytes 3244032 | tf_op jit(solution)/shard_map/reduce_scatter | solution.py:1692
  91.0 33.8 %copy-start.17 = (s32[4]{0:T(128)}, s32[4]{0:T(128)S(1)}, u32[]{:S(2)}) copy-start(s32[4]{0:T(128)S(1)} %and_select_fusion.low_ref) | copy-start | bytes 52
  91.0 4.3 copy-start.13
  91.1 4.3 copy-start.14
  95.4 29.5 %copy-start.2 = (bf16[1024,768]{1,0:T(8,128)(2,1)}, bf16[1024,768]{1,0:T(8,128)(2,1)S(1)}, u32[]{:S(2)}) copy-start(bf16[1024,768]{1,0:T(8,128)(2,1)S(1)} %fusion.22.refs_0_.kv_ref) | copy-start | bytes 4718596
  120.5 3.9 copy-start.4
  124.4 21.0 %copy-start.5 = (bf16[1024,384]{1,0:T(8,128)(2,1)}, bf16[1024,384]{1,0:T(8,128)(2,1)S(1)}, u32[]{:S(2)}) copy-start(bf16[1024,384]{1,0:T(8,128)(2,1)S(1)} %convolution_convert_fusion.11.q_ref) | copy-start | bytes 2359300
  124.8 20.6 %copy-start.3 = (s32[2560,128]{1,0:T(8,128)}, s32[2560,128]{1,0:T(8,128)S(1)}, u32[]{:S(2)}) copy-start(s32[2560,128]{1,0:T(8,128)S(1)} %broadcast_in_dim.113.kt_ref) | copy-start | bytes 3932164
  124.9 20.6 %copy-start.12 = (s32[8,1024]{1,0:T(8,128)}, s32[8,1024]{1,0:T(8,128)S(1)}, u32[]{:S(2)}) copy-start(s32[8,1024]{1,0:T(8,128)S(1)} %broadcast_in_dim.112.qt_ref) | copy-start | bytes 98308
  148.9 95.9 %copy-start.23 = (bf16[256,1536]{1,0:T(8,128)(2,1)S(1)}, bf16[256,1536]{1,0:T(8,128)(2,1)}, u32[]{:S(2)}) copy-start(bf16[256,1536]{1,0:T(8,128)(2,1)} %param.21) | copy-start | bytes 2359300
  245.1 13.6 %copy-start.29 = (bf16[256,1536]{1,0:T(8,128)(2,1)}, bf16[256,1536]{1,0:T(8,128)(2,1)S(1)}, u32[]{:S(2)}) copy-start(bf16[256,1536]{1,0:T(8,128)(2,1)S(1)} %get-tuple-element.225) | copy-start | bytes 2359300
  249.4 9.3 %slice-start.2 = ((s8[4718592]{0:T(1024)(128)(4,1)}), s8[4194304]{0:T(1024)(128)(4,1)S(1)}, s32[]{:S(2)}) async-start(s8[4718592]{0:T(1024)(128)(4,1)} %bitcast.125), calls=%async_computation.10 | async-start | bytes 8388608
  252.0 6.8 slice-start.3
  252.3 6.4 copy-start
  252.3 6.4 copy-start.1
  262.2 116.2 %copy-start.27 = (bf16[256,1536]{1,0:T(8,128)(2,1)S(1)}, bf16[256,1536]{1,0:T(8,128)(2,1)}, u32[]{:S(2)}) copy-start(bf16[256,1536]{1,0:T(8,128)(2,1)} %param.25) | copy-start | bytes 2359300
  381.1 144.3 %copy-start.28 = (bf16[256,1536]{1,0:T(8,128)(2,1)}, bf16[256,1536]{1,0:T(8,128)(2,1)S(1)}, u32[]{:S(2)}) copy-start(bf16[256,1536]{1,0:T(8,128)(2,1)S(1)} %get-tuple-element.221) | copy-start | bytes 2359300
  526.2 4.3 copy-start.25
  530.5 9.2 %copy-start.30 = (bf16[256,1536]{1,0:T(8,128)(2,1)S(1)}, bf16[256,1536]{1,0:T(8,128)(2,1)}, u32[]{:S(2)}) copy-start(bf16[256,1536]{1,0:T(8,128)(2,1)} %copy-done.29) | copy-start | bytes 2359300
  530.6 13.0 %slice-start = ((s8[4718592]{0:T(1024)(128)(4,1)}), s8[4194304]{0:T(1024)(128)(4,1)S(1)}, s32[]{:S(2)}) async-start(s8[4718592]{0:T(1024)(128)(4,1)} %bitcast.121), calls=%async_computation.8 | async-start | bytes 8388608
  549.0 301.5 %reduce-scatter.10.cloned.1.call-start = ((), (), s32[]{:S(2)}) async-start(), calls=%async_computation.7 | async-start | bytes 2654208
  550.4 5.6 copy-start.37
  550.4 5.6 copy-start.38
  631.7 6.6 copy-start.6
  631.7 6.6 copy-start.7
  638.3 26.2 %copy-start.10 = (bf16[1024,384]{1,0:T(8,128)(2,1)S(1)}, bf16[1024,384]{1,0:T(8,128)(2,1)}, u32[]{:S(2)}) copy-start(bf16[1024,384]{1,0:T(8,128)(2,1)} %copy-done.9) | copy-start | bytes 2359300
  684.6 206.5 %reduce-scatter.8.cloned.1.call-start = ((), (), s32[]{:S(2)}) async-start(), calls=%async_computation.5 | async-start | bytes 3981312 | tf_op jit(solution)/shard_map/reduce_scatter | solution.py:1529
  (32 other events, 68.1 us)
Sparse Core Ops, SparseCore 0:
  13.2 69.0 all-gather.3
  86.7 73.2 all-gather.5
  549.1 113.4 reduce-scatter.5
  684.7 72.5 reduce-scatter.9
  833.2 48.4 reduce-scatter.7

commit v2 on v1

--- a/solution.py
+++ b/solution.py
@@ -328,62 +328,6 @@
                 self.copy(refs, i).wait_recv()
 
             @pl.when(row + i + 1 < self.n)
-            def _():
-                self.copy(refs, i).wait_send()
-
-
-class HaloReturn:
-    def __init__(self, x, tokens, n):
-        halo, width = x.shape
-        self.n, self.halo = n, halo
-        self.parts = reach_parts(tokens, halo)
-        self.ins, self.in_specs = [x], [ANY]
-        self.outs = [shape_of(x, (part, width)) for part in self.parts]
-        self.out_specs = [ANY] * len(self.parts)
-        self.scratch = [dma(len(self.parts))] * 2
-
-    def greet(self, barrier):
-        (row, col), n = place(), self.n
-        for i in range(len(self.parts)):
-
-            @pl.when(row + i + 1 < n)
-            def _():
-                greet(barrier, lax.rem(row + i + 1, n), col)
-
-        return jnp.minimum(row, len(self.parts))
-
-    def copy(self, refs, i):
-        x, outs, (send, recv) = refs[0], refs[1:-2], refs[-2:]
-        (row, col), part = place(), self.parts[i]
-        return push(
-            x.at[pl.ds(self.halo - sum(self.parts[: i + 1]), part)],
-            outs[i],
-            send.at[i],
-            recv.at[i],
-            lax.rem(row + self.n - i - 1, self.n),
-            col,
-        )
-
-    def begin(self, refs):
-        row = place()[0]
-        for i in range(len(self.parts)):
-
-            @pl.when(row >= i + 1)
-            def _():
-                self.copy(refs, i).start()
-
-    def run(self, refs):
-        pass
-
-    def end(self, refs):
-        row = place()[0]
-        for i in range(len(self.parts)):
-
-            @pl.when(row + i + 1 < self.n)
-            def _():
-                self.copy(refs, i).wait_recv()
-
-            @pl.when(row >= i + 1)
             def _():
                 self.copy(refs, i).wait_send()
 
@@ -915,6 +859,7 @@
     blocks = tokens // tile
     window = halo + tokens
     heads = width // HD
+    parts = reach_parts(tokens, halo)
     groups = lane_groups(width)
 
     def kernel(
@@ -929,12 +874,9 @@
         kt_ref,
         dq_ref,
         dkv_ref,
-        dhalo_ref,
-        kv_all,
-        k_t,
-        bias,
-        total,
+        *others,
     ):
+        halo_refs, (kv_all, k_t, bias, total) = others[: len(parts)], others[len(parts) :]
         index = pl.program_id(0)
 
         @pl.when(index == 0)
@@ -995,7 +937,9 @@
 
         @pl.when(index == blocks - 1)
         def _():
-            dhalo_ref[...] = total[pl.ds(0, halo), :].astype(bf16)
+            for i, part in enumerate(parts):
+                start = halo - sum(parts[: i + 1])
+                halo_refs[i][...] = total[pl.ds(start, part), :].astype(bf16)
             dkv_ref[...] = total[pl.ds(halo, tokens), :]
 
     return pl.pallas_call(
@@ -1003,8 +947,8 @@
         out_shape=[
             jax.ShapeDtypeStruct((tokens, width), bf16),
             jax.ShapeDtypeStruct((tokens, 2 * width), f32),
-            jax.ShapeDtypeStruct((halo, 2 * width), bf16),
-        ],
+        ]
+        + [jax.ShapeDtypeStruct((part, 2 * width), bf16) for part in parts],
         grid_spec=pltpu.PrefetchScalarGridSpec(
             num_scalar_prefetch=1,
             grid=(blocks,),
@@ -1021,8 +965,8 @@
             out_specs=[
                 pl.BlockSpec((tile, width), lambda i, low: (i, 0)),
                 pl.BlockSpec((tokens, 2 * width), lambda i, low: (0, 0)),
-                pl.BlockSpec((halo, 2 * width), lambda i, low: (0, 0)),
-            ],
+            ]
+            + [pl.BlockSpec((part, 2 * width), lambda i, low: (0, 0)) for part in parts],
             scratch_shapes=[
                 pltpu.VMEM((window, 2 * width), bf16),
                 pltpu.VMEM((width, window), bf16),
@@ -1170,146 +1114,216 @@
     return n - 1
 
 
-def hand_over(part, got, sends, recvs, to):
-    row, me = place()
-    return push(part.at[to], got.at[me], sends.at[to], recvs.at[me], row, to)
-
-
-def add_terms(out, part, got, sends, recvs, n):
-    me = place()[1]
-    for other in range(n):
-
-        @pl.when(me != other)
+PIECES = 2
+
+
+class Stream:
+    def __init__(self, n, own, x, wide, part, from_l, from_r, sems):
+        self.n, self.size, self.last = n, own // PIECES, (n - 1) * PIECES
+        self.x, self.wide, self.part, self.from_l, self.from_r = x, wide, part, from_l, from_r
+        self.sems = sems
+
+    def rows(self, c):
+        start = c * self.size
+        return pl.ds(start if isinstance(c, int) else pl.multiple_of(start, self.size), self.size)
+
+    def step(self, src, b, c, place_on_link, way):
+        (row, me), n = place(), self.n
+        send, recv = self.sems[2 * way], self.sems[2 * way + 1]
+        to = lax.rem(me + 1, n) if way == 0 else lax.rem(me + n - 1, n)
+        dst = self.wide.at[b, self.rows(c)]
+        return push(src, dst, send.at[place_on_link], recv.at[place_on_link], row, to)
+
+    def launch(self):
+        me, n = place()[1], self.n
+        for c in range(PIECES):
+
+            @pl.when(me < n - 1)
+            def _():
+                self.step(self.x.at[self.rows(c)], me, c, c, 0).start()
+
+            @pl.when(me > 0)
+            def _():
+                self.step(self.x.at[self.rows(c)], me, c, c, 1).start()
+
+    def take(self, a, work):
+        me, n = place()[1], self.n
+        c = a % PIECES
+        before, later = me - 1 - a // PIECES, me + 1 + a // PIECES
+        for way, there, owner, more in (
+            (0, before >= 0, jnp.maximum(before, 0), me < n - 1),
+            (1, later < n, jnp.minimum(later, n - 1), me > 0),
+        ):
+
+            @pl.when(there)
+            def _():
+                self.step(self.x.at[self.rows(c)], me, c, a, way).wait_recv()
+
+            @pl.when(there & more)
+            def _():
+                src = self.wide.at[owner, self.rows(c)]
+                self.step(src, owner, c, a + PIECES, way).start()
+
+        self.both(a, work)
+
+    def both(self, a, work):
+        me, n = place()[1], self.n
+        before, later = me - 1 - a // PIECES, me + 1 + a // PIECES
+
+        @pl.when(before >= 0)
         def _():
-            row = place()[0]
-            push(
-                part.at[other], got.at[other], sends.at[other], recvs.at[other], row, other
-            ).wait_recv()
-            out[...] += got[other].astype(f32)
-
-    for other in range(n):
-
-        @pl.when(me != other)
+            work(jnp.maximum(before, 0), a % PIECES)
+
+        @pl.when(later < n)
         def _():
-            hand_over(part, got, sends, recvs, other).wait_send()
-
-
-def both_sides(step, n, work):
-    me = place()[1]
-    before, later = me - 1 - step, me + 1 + step
-
-    @pl.when(before >= 0)
-    def _():
-        work(jnp.maximum(before, 0))
-
-    @pl.when(later < n)
-    def _():
-        work(jnp.minimum(later, n - 1))
+            work(jnp.minimum(later, n - 1), a % PIECES)
+
+    def term(self, d, c, way):
+        (row, me), n = place(), self.n
+        send, recv = self.sems[4 + 2 * way], self.sems[5 + 2 * way]
+        to = lax.rem(me + 1, n) if way == 0 else lax.rem(me + n - 1, n)
+        into = (self.from_l, self.from_r)[way].at[d, self.rows(c)]
+        spot = d * PIECES + c
+        return push(self.part.at[d, self.rows(c)], into, send.at[spot], recv.at[spot], row, to)
+
+    def give(self, slot):
+        me, n = place()[1], self.n
+        for way, q in ((0, slot - 1 - me), (1, slot - 1 - (n - 1 - me))):
+            some = jnp.maximum(q, 0)
+            c, blocks = lax.rem(some, PIECES), lax.div(some, PIECES)
+            d = 1 + blocks if way == 0 else n - 2 - blocks
+            due = (q >= 0) & ((d > me) & (d < n) if way == 0 else (d >= 0) & (d < me))
+            started = me > 0 if way == 0 else me < n - 1
+
+            @pl.when(due & started)
+            def _():
+                self.term(d, c, way).wait_recv()
+                spot = self.rows(c)
+                more = (self.from_l, self.from_r)[way][d, spot, :].astype(f32)
+                self.part[d, spot, :] = (self.part[d, spot, :].astype(f32) + more).astype(bf16)
+
+            @pl.when(due)
+            def _():
+                self.term(d, c, way).start()
+
+    def slots(self):
+        return range(1, self.last + self.n - 1)
+
+    def finish(self, out):
+        me, n = place()[1], self.n
+        for way, comes in ((0, me > 0), (1, me < n - 1)):
+
+            @pl.when(comes)
+            def _():
+                for c in range(PIECES):
+                    self.term(me, c, way).wait_recv()
+                out[...] += (self.from_l, self.from_r)[way][me].astype(f32)
+
+        for c in range(PIECES):
+            for d in range(n):
+
+                @pl.when(me < d)
+                def _():
+                    self.term(d, c, 0).wait_send()
+
+                @pl.when(me > d)
+                def _():
+                    self.term(d, c, 1).wait_send()
+
+        for a in range(n * PIECES):
+
+            @pl.when((me < n - 1) & (a < (me + 1) * PIECES))
+            def _():
+                self.step(self.x.at[self.rows(0)], me, 0, a, 0).wait_send()
+
+            @pl.when((me > 0) & (a < (n - me) * PIECES))
+            def _():
+                self.step(self.x.at[self.rows(0)], me, 0, a, 1).wait_send()
 
 
 def chunk_of(size):
-    return TILE if size % TILE == 0 else LANES
-
-
-def feed_forward(x, expand, reduce_block, n, rows, collective_id):
+    return next(c for c in (512, 256, 128) if size % c == 0)
+
+
+def feed_forward(x, expand, reduce, n, collective_id):
     own, features = x.shape
     hidden = expand.shape[1]
-    block = features // rows
-    line, gather = LineGather(x, n), RowGather(reduce_block, n=rows)
     wide_shape, hidden_shape = (n, own, features), (n, own, hidden)
-    turn = min(1, n - 2)
     step_h, step_f = chunk_of(hidden), chunk_of(features)
 
     def kernel(
         x_ref,
         expand_ref,
-        block_ref,
+        reduce_ref,
         out,
         wide_out,
         act_out,
         slope_out,
-        reduce_out,
         wide,
         act,
         slope,
         expand_v,
         reduce_v,
         part,
-        got,
+        from_l,
+        from_r,
         loads,
         stores,
-        sends,
-        recvs,
-        line_a,
-        line_b,
-        line_c,
-        line_d,
-        *gather_refs,
+        *sems,
     ):
-        row, me = place()
-        line_refs = [x_ref, wide, None, None, line_a, line_b, line_c, line_d]
-        gather_refs = [block_ref, reduce_out, *gather_refs]
+        me = place()[1]
+        stream = Stream(n, own, x_ref, wide, part, from_l, from_r, sems)
         barrier = pltpu.get_barrier_semaphore()
-        pl.semaphore_wait(barrier, greet_col(barrier, n) + gather.greet(barrier))
-        line.launch(line_refs)
-        own_load = pltpu.make_async_copy(x_ref, wide.at[me], loads.at[0])
-        expand_load = pltpu.make_async_copy(expand_ref, expand_v, loads.at[1])
-        own_load.start()
-        expand_load.start()
-        gather.begin(gather_refs)
-        own_load.wait()
-        expand_load.wait()
-
-        def first(b):
+        pl.semaphore_wait(barrier, greet_col(barrier, n))
+        stream.launch()
+        pairs = [(x_ref, wide.at[me]), (expand_ref, expand_v), (reduce_ref, reduce_v)]
+        copies = [pltpu.make_async_copy(a, b, loads.at[i]) for i, (a, b) in enumerate(pairs)]
+        for copy in copies:
+            copy.start()
+        for copy in copies:
+            copy.wait()
+
+        def first(b, c):
+            at = stream.rows(c)
+
             @pl.loop(0, hidden // step_h)
             def _(i):
                 spot = pl.ds(pl.multiple_of(i * step_h, step_h), step_h)
-                value = matmul(wide[b], expand_v[:, spot])
+                value = matmul(wide[b, at, :], expand_v[:, spot])
                 upper = 0.5 * (1.0 + lax.erf(value * (0.5**0.5)))
                 bell = jnp.exp(-0.5 * value * value) * (0.5 / jnp.pi) ** 0.5
-                act[b, :, spot] = (value * upper).astype(bf16)
-                slope[b, :, spot] = (upper + value * bell).astype(bf16)
-
-        def second(b, mine=False):
+                act[b, at, spot] = (value * upper).astype(bf16)
+                slope[b, at, spot] = (upper + value * bell).astype(bf16)
+
+        def second(b, c, mine=False):
+            at = stream.rows(c)
+
             @pl.loop(0, features // step_f)
             def _(i):
                 spot = pl.ds(pl.multiple_of(i * step_f, step_f), step_f)
-                value = against(act[b], reduce_v[spot, :])
+                value = against(act[b, at, :], reduce_v[spot, :])
                 if mine:
-                    out[:, spot] = value
+                    out[at, spot] = value
                 else:
-                    part[b, :, spot] = value.astype(bf16)
-
-            if not mine:
-                hand_over(part, got, sends, recvs, b).start()
-
-        first(me)
-        for step in range(n - 1):
-            line.pass_on(line_refs, step)
-            both_sides(step, n, first)
-            if step == turn:
-                gather.end(gather_refs)
-                weights = [
-                    pltpu.make_async_copy(
-                        reduce_out.at[r], reduce_v.at[pl.ds(r * block, block)], loads.at[2 + r]
-                    )
-                    for r in range(rows)
-                ]
-                for copy in weights:
-                    copy.start()
-                for copy in weights:
-                    copy.wait()
-                for earlier in range(step, -1, -1):
-                    both_sides(earlier, n, second)
-            elif step > turn:
-                both_sides(step, n, second)
+                    part[b, at, spot] = value.astype(bf16)
+
+        def work(b, c):
+            first(b, c)
+            second(b, c)
+
+        for c in range(PIECES):
+            first(me, c)
+        for slot in stream.slots():
+            if slot <= stream.last:
+                stream.take(slot - 1, work)
+            stream.give(slot)
         kept = [(wide, wide_out), (act, act_out), (slope, slope_out)]
         kept = [pltpu.make_async_copy(a, b, stores.at[i]) for i, (a, b) in enumerate(kept)]
         for copy in kept:
             copy.start()
-        second(me, mine=True)
-        add_terms(out, part, got, sends, recvs, n)
-        line.sent(line_refs)
+        for c in range(PIECES):
+            second(me, c, mine=True)
+        stream.finish(out)
         for copy in kept:
             copy.wait()
 
@@ -1320,10 +1334,9 @@
             jax.ShapeDtypeStruct(wide_shape, bf16),
             jax.ShapeDtypeStruct(hidden_shape, bf16),
             jax.ShapeDtypeStruct(hidden_shape, bf16),
-            jax.ShapeDtypeStruct((rows, block, hidden), bf16),
         ],
         in_specs=[ANY] * 3,
-        out_specs=[VMEM] + [ANY] * 4,
+        out_specs=[VMEM] + [ANY] * 3,
         scratch_shapes=[
             pltpu.VMEM(wide_shape, bf16),
             pltpu.VMEM(hidden_shape, bf16),
@@ -1332,26 +1345,23 @@
             pltpu.VMEM((features, hidden), bf16),
             pltpu.VMEM(wide_shape, bf16),
             pltpu.VMEM(wide_shape, bf16),
-            dma(2 + rows),
+            pltpu.VMEM(wide_shape, bf16),
             dma(3),
-            dma(n),
-            dma(n),
+            dma(3),
         ]
-        + [dma(n)] * 4
-        + gather.scratch,
+        + [dma(n * PIECES)] * 8,
         compiler_params=pltpu.CompilerParams(
             collective_id=collective_id, has_side_effects=True, vmem_limit_bytes=56 << 20
         ),
         cost_estimate=CHEAP,
         name="feed_forward",
-    )(x, expand, reduce_block)
+    )(x, expand, reduce)
 
 
 def feed_forward_back(grad, expand, reduce, act, slope, wide, n, rows, collective_id):
     own, features = grad.shape
     hidden = expand.shape[1]
-    half, block = rows // 2, features // rows
-    line = LineGather(grad, n)
+    half, block, step_w = rows // 2, features // rows, TILE
     wide_shape, hidden_shape = (n, own, features), (n, own, hidden)
     step_h, step_f = chunk_of(hidden), chunk_of(features)
 
@@ -1374,22 +1384,18 @@
         slope_v,
         wide_v,
         part,
-        got,
+        from_l,
+        from_r,
         sum_e,
         sum_r,
         loads,
         stores,
-        sends,
-        recvs,
         swap_send,
         swap_recv,
-        line_a,
-        line_b,
-        line_c,
-        line_d,
+        *sems,
     ):
         row, me = place()
-        line_refs = [g_ref, g_wide, None, None, line_a, line_b, line_c, line_d]
+        stream = Stream(n, own, g_ref, g_wide, part, from_l, from_r, sems)
         barrier = pltpu.get_barrier_semaphore()
         other = 1 - lax.rem(row, 2)
         sibling = row + 2 * other - 1
@@ -1397,7 +1403,7 @@
         place_of = place()[1]
         greet(barrier, sibling, place_of)
         pl.semaphore_wait(barrier, count + 1)
-        line.launch(line_refs)
+        stream.launch()
         pairs = [
             (g_ref, g_wide.at[me]),
             (reduce_ref, reduce_v),
@@ -1412,39 +1418,39 @@
         for copy in copies:
             copy.wait()
 
-        def work(b, mine=False):
+        def work(b, c, mine=False):
+            at = stream.rows(c)
+
             @pl.loop(0, hidden // step_h)
             def _(i):
                 spot = pl.ds(pl.multiple_of(i * step_h, step_h), step_h)
-                value = matmul(g_wide[b], reduce_v[:, spot])
-                slope_v[b, :, spot] = (value * slope_v[b, :, spot].astype(f32)).astype(bf16)
+                value = matmul(g_wide[b, at, :], reduce_v[:, spot])
+                slope_v[b, at, spot] = (value * slope_v[b, at, spot].astype(f32)).astype(bf16)
 
             @pl.loop(0, features // step_f)
             def _(i):
                 spot = pl.ds(pl.multiple_of(i * step_f, step_f), step_f)
-                value = against(slope_v[b], expand_v[spot, :])
+                value = against(slope_v[b, at, :], expand_v[spot, :])
                 if mine:
-                    out[:, spot] = value
+                    out[at, spot] = value
                 else:
-                    part[b, :, spot] = value.astype(bf16)
-
-            if not mine:
-                hand_over(part, got, sends, recvs, b).start()
-
-        work(me, mine=True)
-        for step in range(n - 1):
-            line.pass_on(line_refs, step)
-            both_sides(step, n, work)
+                    part[b, at, spot] = value.astype(bf16)
+
+        for c in range(PIECES):
+            work(me, c, mine=True)
+        for slot in stream.slots():
+            if slot <= stream.last:
+                stream.take(slot - 1, work)
+            stream.give(slot)
 
         def weight_sums(left, right, total):
-            @pl.loop(0, features // step_f)
+            @pl.loop(0, features // step_w)
             def _(i):
-                spot = pl.ds(pl.multiple_of(i * step_f, step_f), step_f)
-                rows_of = left[:, :, spot].reshape(n * own, step_f)
-                for start in range(0, hidden, 2 * step_h):
-                    size = min(2 * step_h, hidden - start)
-                    columns = right[:, :, start : start + size].reshape(n * own, size)
-                    total[spot, start : start + size] = transposed(rows_of, columns).astype(bf16)
+                spot = pl.ds(pl.multiple_of(i * step_w, step_w), step_w)
+                rows_of = left[:, :, spot].reshape(n * own, step_w)
+                for start in range(0, hidden, step_h):
+                    columns = right[:, :, start : start + step_h].reshape(n * own, step_h)
+                    total[spot, start : start + step_h] = transposed(rows_of, columns).astype(bf16)
 
         def swaps(total, swap, first):
             return [
@@ -1477,8 +1483,7 @@
         more = swaps(sum_e, swap_e, half) + keeps(sum_e, mine_e, half)
         for copy in more:
             copy.start()
-        add_terms(out, part, got, sends, recvs, n)
-        line.sent(line_refs)
+        stream.finish(out)
         for copy in late + more:
             copy.wait()
 
@@ -1498,16 +1503,15 @@
             pltpu.VMEM(wide_shape, bf16),
             pltpu.VMEM(wide_shape, bf16),
             pltpu.VMEM(wide_shape, bf16),
+            pltpu.VMEM(wide_shape, bf16),
             pltpu.VMEM((features, hidden), bf16),
             pltpu.VMEM((features, hidden), bf16),
             dma(6),
             dma(2 * half),
-            dma(n),
-            dma(n),
             dma(2 * half),
             dma(2 * half),
         ]
-        + [dma(n)] * 4,
+        + [dma(n * PIECES)] * 8,
         compiler_params=pltpu.CompilerParams(
             collective_id=collective_id, has_side_effects=True, vmem_limit_bytes=58 << 20
         ),
@@ -1607,6 +1611,7 @@
 
     text_kv = matmul(text_full, text_weights).astype(bf16)
     text_all = lax.all_gather(text_kv, ("row", "col"), axis=0)
+    reduce_full = row_gather(after(reduce_weight, text_kv).T)
     key_values = matmul(after(wide_one, text_kv), kv_full).astype(bf16)
     queries = matmul(wide_one, query_full).astype(bf16)
     cross_local = (cross_query, cross_output.T)
@@ -1643,10 +1648,9 @@
     normed_three, unit_three, inverse_three = normalize(
         after_cross, final_norm_gain, final_norm_bias
     )
-    branch_three, wide_three, activated, slope, reduce_full = feed_forward(
-        normed_three, expand_full, reduce_weight.T, cols, rows, 5
-    )
-    reduce_full = reduce_full.reshape(features, hidden)
+    branch_three, wide_three, activated, slope = feed_forward(
+        normed_three, expand_full, reduce_full, cols, 5
+    )
     layer_out = (after_cross.astype(f32) + branch_three).astype(bf16)
     error = layer_out.astype(f32) - teacher_states.astype(f32)
     squared = jnp.sum(error * error * own_valid[:, None])
@@ -1703,7 +1707,7 @@
     ]
     cross = [own_half(x, y, parity) for x, y in zip(cross, swapped)]
     grad_attended_one = matmul(grad_wide_one, output_full).astype(bf16)
-    grad_queries, grad_kv_own, grad_kv_halo = self_backward(
+    grad_queries, grad_kv_own, *grad_kv_halo = self_backward(
         queries,
         key_values,
         halo_kv,
@@ -1717,28 +1721,29 @@
     mine_text = after(mine_text, grad_queries).reshape(2, seg_count * text_rows, width)
     grad_text_weights = [transposed(text_full, mine_text[i]).astype(bf16) for i in range(2)]
     grad_output = transposed(grad_wide_one, attended_one).astype(bf16).reshape(by_row + (width,))
-    summed_text = row_scatter(grad_text_weights[0], grad_text_weights[1])
     text_partial = against(mine_text[0], ckey_full) + against(mine_text[1], cvalue_full)
     text_partial = text_partial.astype(bf16)
 
-    returned, (swapped,) = exchange(
-        "return_halo",
-        10,
-        HaloReturn(after(grad_kv_halo, text_partial), tokens, rows),
-        SiblingSwap(grad_output),
-    )
-    cross.append(own_half(grad_output, swapped, parity))
-    for i, piece in enumerate(returned):
-        piece = jnp.where(row + i + 1 < rows, piece.astype(f32), 0.0)
+    returned = [
+        lax.ppermute(x, "row", [(r, r - i - 1) for r in range(i + 1, rows)])
+        for i, x in enumerate(grad_kv_halo)
+    ]
+    returned, text_partial, grad_text_weights, grad_output, cross, feed = lax.optimization_barrier(
+        (returned, text_partial, grad_text_weights, grad_output, cross, feed)
+    )
+    summed_text = row_scatter(grad_text_weights[0], grad_text_weights[1])
+    for piece in returned:
+        piece = piece.astype(f32)
         grad_kv_own = grad_kv_own + jnp.pad(piece, ((tokens - piece.shape[0], 0), (0, 0)))
     grad_kv = grad_kv_own.astype(bf16)
     grad_qkv = jnp.concatenate([grad_queries, grad_kv], axis=1)
     grad_normed_one = against(grad_qkv, weights_one[:, : 3 * width]).astype(bf16)
-    (back_one,), received, *text_parts = exchange(
+    (back_one,), received, (swapped,), *text_parts = exchange(
         "scatter_grad_one",
         11,
         LineScatter(grad_normed_one, cols),
         ChipExchange(*cross),
+        SiblingSwap(grad_output),
         *([ColExchange(text_partial, n=cols)] if aligned else []),
     )
     if aligned:
@@ -1749,11 +1754,10 @@
         grad_text = lax.psum_scatter(text_partial, "col", scatter_dimension=1, tiled=True)
     grad_text = grad_text.astype(f32).reshape(seg_count, text_rows, width)
     cross = [
-        total_of(lax.dynamic_index_in_dim(x, chip, 0, keepdims=False), y, chip)
+        total_of(lax.dynamic_index_in_dim(x, chip, 0, keepdims=False), y, chip).astype(bf16)
         for x, y in zip(cross, received)
     ]
-    summed_output = cross.pop()
-    cross = [x.astype(bf16) for x in cross]
+    grad_output = own_half(grad_output, swapped, parity)
     inner_one, gain_one, shift_one = normalize_back(
         back_one, unit_one, inverse_one, self_norm_gain
     )
@@ -1772,11 +1776,15 @@
             jnp.zeros((features,), f32),
         ]
     )
-    (small,), *received = exchange(
+    (small,), (output_parts,), *received = exchange(
         "sum_small",
         12,
         AllSum(after(small, summed_text), rows, cols),
+        ChipExchange(grad_output, known=True),
         *([ColExchange(*cross, n=cols, known=True)] if aligned else []),
+    )
+    summed_output = total_of(
+        lax.dynamic_index_in_dim(grad_output, chip, 0, keepdims=False), output_parts, chip
     )
     if aligned:
         cross = [

time: 906 us -> 832 us (0.918)
  Pallas kernels: 736 us -> 631 us
  waiting for transfers between devices: 0.11 us -> 43 us
    pallas_call x1, Pallas kernels: 141 us -> 90.2 us  [feed_forward_back(): pl.pallas_call(kernel, out_shape=[jax.ShapeDtypeStruct((own, features), f...]
    ppermute x0 -> x2, waiting for transfers between devices: none -> 42.2 us  [on_device(): lax.ppermute(x, 'row', [(r, r - i - 1) for r in range(i + 1, rows)])]
    pallas_call x7 -> x6, Pallas kernels: 416 us -> 381 us  [exchange(): pl.pallas_call(kernel, out_shape=[out for job in jobs for out in job.outs...]
    pallas_call x1, Pallas kernels: 116 us -> 97.9 us  [feed_forward(): pl.pallas_call(kernel, out_shape=[jax.ShapeDtypeStruct((own, features), f...]
    unnamed x127 -> x139, local copies, waits for them, and re-layouts: 23.2 us -> 13.8 us
  transfers between devices with their start and end apart: 5 -> 8, of which waited for: 0 -> 1; matrix products, arithmetic and copies ran while one was open for 10% -> 12% of each run, Pallas kernels for 51% -> 52%
where the time goes in v2:
time: 832 us; the launch traced here: 833 us
  Pallas kernels  631 us (76%)
  matrix products  61.1 us (7%)
  other arithmetic  51.8 us (6%)
  waiting for transfers between devices  43 us (5%)
  local copies, waits for them, and re-layouts  25.6 us (3%)
  between operations  18.1 us (2%)
    pallas_call x6, Pallas kernels, exchange(): pl.pallas_call(kernel, out_shape=[out for job in jobs for out in job.outs...  381 us
    pallas_call x1, Pallas kernels, feed_forward(): pl.pallas_call(kernel, out_shape=[jax.ShapeDtypeStruct((own, features), f...  97.9 us
    pallas_call x1, Pallas kernels, feed_forward_back(): pl.pallas_call(kernel, out_shape=[jax.ShapeDtypeStruct((own, features), f...  90.2 us
    ppermute x2, waiting for transfers between devices, on_device(): lax.ppermute(x, 'row', [(r, r - i - 1) for r in range(i + 1, rows)])  42.2 us
    pallas_call x1, Pallas kernels, self_backward(): pl.pallas_call(kernel, out_shape=[jax.ShapeDtypeStruct((tokens, width), b...  26.3 us
    dot_general x6, matrix products, matmul(): return jnp.dot(left, right, preferred_element_type=f32)  22.1 us
    pallas_call x1, Pallas kernels, self_forward(): pl.pallas_call(kernel, out_shape=[jax.ShapeDtypeStruct((tokens, width), b...  20.5 us
    dot_general x6, matrix products, transposed(): lax.dot_general(left, right, (((0,), (0,)), ((), ())), preferred_element_...  19.5 us
  transfers between devices with their start and end apart: 8, of which 1 were waited for; matrix products, arithmetic and copies ran while one was open for 12% of the time, Pallas kernels for 52%

profile of v2, /device:TPU:0, one launch (start us, length us, event | category | flops | bytes accessed | tf_op | source)
XLA Modules:
  0.0 833.1 jit_solution(13786385962528848414)
XLA Ops:
  14.2 67.8 %gather_one.1 = (bf16[4,256,1536]{2,1,0:T(8,128)(2,1)S(1)}, bf16[8,192,1536]{2,1,0:T(8,128)(2,1)}, s32[8,8,128]{2,1,0:T(8,128)S(1)}, bf16[64,1536]{1,0:T(8,128)(2,1)S(1)}) custom-call(bf16[256,1536]{1,0:T(8,128)(2,1)S(1)} %fusion.34.refs_0_, bf16[192,1536]{1,0:T(8,128)(2,1)S(1)} %copy-done.13, s32[8,128]{1,0:T(8,128)S(1)} %get-tuple-element.172.refs_2_, ...), custom_call_target="tpu_custom_call" | custom-call | flops 1048576 | bytes 1048576 | tf_op jit(solution)/shard_map/gather_one/pallas_call | solution.py:701
  83.6 3.0 fusion.50
  91.3 4.3 fusion.22.refs_0_.kv_ref
  95.6 25.0 %gather_halo.1 = (bf16[1536,768]{1,0:T(8,128)(2,1)S(1)}, bf16[192,1536]{1,0:T(8,128)(2,1)S(1)}, bf16[192,1536]{1,0:T(8,128)(2,1)S(1)}) custom-call(bf16[1024,768]{1,0:T(8,128)(2,1)S(1)} %fusion.22.refs_0_.kv_ref, bf16[192,384]{1,0:T(8,128)(2,1)S(1)} %copy-done.18, bf16[192,384]{1,0:T(8,128)(2,1)S(1)} %bitcast.93), custom_call_target="tpu_custom_call" | custom-call | flops 1048576 | bytes 1048576 | tf_op jit(solution)/shard_map/gather_halo/pallas_call | solution.py:701
  120.7 3.9 convolution_convert_fusion.11.q_ref
  125.1 20.5 %self_forward.1 = (bf16[1024,384]{1,0:T(8,128)(2,1)S(1)}, f32[8,1024]{1,0:T(8,128)S(1)}) custom-call(s32[4]{0:T(128)S(1)} %and_select_fusion.low_ref, bf16[1024,384]{1,0:T(8,128)(2,1)S(1)} %convolution_convert_fusion.11.q_ref, bf16[1024,768]{1,0:T(8,128)(2,1)S(1)} %fusion.22.refs_0_.kv_ref, bf16[1536,768]{1,0:T(8,128)(2,1)} %copy-done.4, ...), custom_call_target="tpu_custom_call" | custom-call | flops 1048576 | bytes 1048576 | tf_op jit(solution)/shard_map/self_forward/pallas_call | solution.py:821
  145.7 3.4 convolution_convert_fusion.3
  149.1 105.2 %scatter_one.1 = (f32[256,1536]{1,0:T(8,128)S(1)}, bf16[8,192,1536]{2,1,0:T(8,128)(2,1)}, bf16[8,192,1536]{2,1,0:T(8,128)(2,1)}) custom-call(bf16[4,256,1536]{2,1,0:T(8,128)(2,1)S(1)} %bitcast.88, bf16[192,1536]{1,0:T(8,128)(2,1)S(1)} %get-tuple-element.82.refs_1_, bf16[192,1536]{1,0:T(8,128)(2,1)S(1)} %get-tuple-element.83.refs_2_), custom_call_target="tpu_custom_call" | custom-call | flops 1048576 | bytes 1048576 | tf_op jit(solution)/shard_map/scatter_one/pallas_call | solution.py:701
  255.1 4.7 convolution_convert_fusion.9.q_ref
  259.8 2.5 copy.63
  263.4 6.1 cross_forward.1
  273.0 97.9 %feed_forward.1 = (f32[256,1536]{1,0:T(8,128)}, bf16[4,256,1536]{2,1,0:T(8,128)(2,1)}, bf16[4,256,1536]{2,1,0:T(8,128)(2,1)}, bf16[4,256,1536]{2,1,0:T(8,128)(2,1)}) custom-call(bf16[256,1536]{1,0:T(8,128)(2,1)} %add_convert_fusion.4.x_ref, bf16[1536,1536]{1,0:T(8,128)(2,1)} %bitcast.103, bf16[1536,1536]{1,0:T(8,128)(2,1)} %all-gather.7.cloned.1.call-done.reduce_ref), custom_call_target="tpu_custom_call" | custom-call | flops 1048576 | bytes 1048576 | tf_op jit(solution)/shard_map/feed_forward/pallas_call | solution.py:1330
  371.0 2.7 multiply_reduce_fusion
  374.9 90.2 %feed_forward_back.1 = (f32[256,1536]{1,0:T(8,128)}, bf16[4,192,1536]{2,1,0:T(8,128)(2,1)}, bf16[4,192,1536]{2,1,0:T(8,128)(2,1)}, bf16[4,192,1536]{2,1,0:T(8,128)(2,1)}, bf16[4,192,1536]{2,1,0:T(8,128)(2,1)}) custom-call(bf16[256,1536]{1,0:T(8,128)(2,1)} %fusion.42.g_ref, bf16[1536,1536]{1,0:T(8,128)(2,1)} %bitcast.104, ...), custom_call_target="tpu_custom_call" | custom-call | flops 1048576 | bytes 1048576 | tf_op jit(solution)/shard_map/feed_forward_back/pallas_call | solution.py:1491
  468.5 3.6 convolution_convert_fusion.1
  473.5 8.9 %cross_backward.1 = (bf16[256,1536]{1,0:T(8,128)(2,1)S(1)}, bf16[512,1536]{1,0:T(8,128)(2,1)S(1)}, bf16[512,1536]{1,0:T(8,128)(2,1)S(1)}) custom-call(s32[2]{0:T(128)S(1)} %pad_add_fusion.ends_ref, bf16[256,1536]{1,0:T(8,128)(2,1)S(1)} %copy-done.7, bf16[512,1536]{1,0:T(8,128)(2,1)} %bitcast.87, bf16[512,1536]{1,0:T(8,128)(2,1)} %bitcast.85, ...), custom_call_target="tpu_custom_call" | custom-call | flops 1048576 | bytes 1048576 | tf_op jit(solution)/shard_map/cross_backward/pallas_call | solution.py:1080
  482.5 3.7 convolution_convert_fusion.2
  486.2 2.8 fusion.31
  489.3 2.3 copy.57
  491.7 7.4 add_convert_fusion
  501.0 75.3 %gather_grad_one.1 = (bf16[4,256,1536]{2,1,0:T(8,128)(2,1)}, bf16[4,192,1536]{2,1,0:T(8,128)(2,1)S(1)}, bf16[4,192,1536]{2,1,0:T(8,128)(2,1)S(1)}, bf16[4,192,1536]{2,1,0:T(8,128)(2,1)}, bf16[4,192,1536]{2,1,0:T(8,128)(2,1)}) custom-call(bf16[256,1536]{1,0:T(8,128)(2,1)S(1)} %get-tuple-element.158.refs_0_, bf16[4,192,1536]{2,1,0:T(8,128)(2,1)} %get-tuple-element.179.refs_1_, ...), custom_call_target="tpu_custom_call" | custom-call | flops 1048576 | bytes 1048576 | tf_op jit(solution)/shard_map/gather_grad_one/pallas_call | solution.py:701
  576.4 4.9 convolution_convert_fusion.10.do_ref
  581.2 26.3 %self_backward.1 = (bf16[1024,384]{1,0:T(8,128)(2,1)}, f32[1024,768]{1,0:T(8,128)}, bf16[1024,768]{1,0:T(8,128)(2,1)}, bf16[512,768]{1,0:T(8,128)(2,1)}) custom-call(s32[4]{0:T(128)} %copy-done.22, bf16[1024,384]{1,0:T(8,128)(2,1)} %copy-done.5, bf16[1024,768]{1,0:T(8,128)(2,1)} %copy-done.2, bf16[1536,768]{1,0:T(8,128)(2,1)} %copy-done.4, ...), custom_call_target="tpu_custom_call" | custom-call | flops 1048576 | bytes 1048576 | tf_op jit(solution)/shard_map/self_backward/pallas_call | solution.py:945
  610.1 3.7 convolution_convert_fusion.7
  614.9 2.8 convert_add_fusion.6
  630.9 42.2 %collective-permute-done.1 = bf16[512,768]{1,0:T(8,128)(2,1)S(1)} collective-permute-done((bf16[512,768]{1,0:T(8,128)(2,1)}, bf16[512,768]{1,0:T(8,128)(2,1)S(1)}, u32[]{:S(2)}, u32[]{:S(2)}) %collective-permute-start.1) | collective-permute-done | bytes 786464 | tf_op jit(solution)/shard_map/ppermute | solution.py:1728
  675.2 3.1 add_convert_fusion.2
  678.9 5.8 convolution_convert_fusion
  684.7 8.3 convolution_convert_fusion.4
  693.0 73.7 %scatter_grad_one.1 = (f32[256,1536]{1,0:T(8,128)S(1)}, bf16[4,192,1536]{2,1,0:T(8,128)(2,1)S(1)}, bf16[4,192,1536]{2,1,0:T(8,128)(2,1)}, bf16[4,192,384]{2,1,0:T(8,128)(2,1)S(1)}, bf16[4,64,384]{2,1,0:T(8,128)(2,1)S(1)}) custom-call(bf16[4,256,1536]{2,1,0:T(8,128)(2,1)} %bitcast.112, bf16[4,192,1536]{2,1,0:T(8,128)(2,1)} %fusion.1.refs_1_, ...), custom_call_target="tpu_custom_call" | custom-call | flops 1048576 | bytes 1048576 | tf_op jit(solution)/shard_map/scatter_grad_one/pallas_call | solution.py:701
  773.1 3.9 select_reduce_fusion
  781.8 33.6 %sum_small.1 = (f32[8,1536]{1,0:T(8,128)S(1)}, bf16[4,192,384]{2,1,0:T(8,128)(2,1)S(1)}, bf16[4,192,384]{2,1,0:T(8,128)(2,1)S(1)}, bf16[4,192,384]{2,1,0:T(8,128)(2,1)S(1)}) custom-call(f32[8,1536]{1,0:T(8,128)S(1)} %copy-done.17, bf16[4,192,384]{2,1,0:T(8,128)(2,1)S(1)} %fusion.49.refs_1_, bf16[192,1536]{1,0:T(8,128)(2,1)S(1)} %fusion.48.refs_2_, ...), custom_call_target="tpu_custom_call" | custom-call | flops 1048576 | bytes 1048576 | tf_op jit(solution)/shard_map/sum_small/pallas_call | solution.py:701
  (241 shorter events, 65.4 us)
Async XLA Ops:
  7.2 5.9 copy-start.26
  7.2 76.3 %all-gather.5.cloned.1.call-start = ((), (), s32[]{:S(2)}) async-start(), calls=%async_computation.3 | async-start | bytes 7962624 | tf_op jit(solution)/shard_map/all_gather | solution.py:1528
  13.1 246.7 %all-gather.9.cloned.1.call-start = ((), (), s32[]{:S(2)}) async-start(), calls=%async_computation.8 | async-start | bytes 3244032 | tf_op jit(solution)/shard_map/all_gather | solution.py:1613
  83.6 7.7 copy-start.24
  86.6 186.4 %all-gather.7.cloned.1.call-start = ((), (), s32[]{:S(2)}) async-start(), calls=%async_computation.4 | async-start | bytes 5308416 | tf_op jit(solution)/shard_map/all_gather | solution.py:1528
  87.3 537.4 %reduce-scatter.4.cloned.1.call-start = ((), (), s32[]{:S(2)}) async-start(), calls=%async_computation.5 | async-start | bytes 3244032 | tf_op jit(solution)/shard_map/reduce_scatter | solution.py:1696
  88.9 525.0 %copy-start.51 = (pred[4]{0:T(512)(128)(4,1)}, pred[4]{0:T(512)(128)(4,1)S(1)}, u32[]{:S(2)}) copy-start(pred[4]{0:T(512)(128)(4,1)S(1)} %iota_compare_fusion.1) | copy-start | bytes 16
  91.3 33.8 %copy-start.22 = (s32[4]{0:T(128)}, s32[4]{0:T(128)S(1)}, u32[]{:S(2)}) copy-start(s32[4]{0:T(128)S(1)} %and_select_fusion.low_ref) | copy-start | bytes 52
  95.6 29.4 %copy-start.2 = (bf16[1024,768]{1,0:T(8,128)(2,1)}, bf16[1024,768]{1,0:T(8,128)(2,1)S(1)}, u32[]{:S(2)}) copy-start(bf16[1024,768]{1,0:T(8,128)(2,1)S(1)} %fusion.22.refs_0_.kv_ref) | copy-start | bytes 4718596
  124.6 21.0 %copy-start.5 = (bf16[1024,384]{1,0:T(8,128)(2,1)}, bf16[1024,384]{1,0:T(8,128)(2,1)S(1)}, u32[]{:S(2)}) copy-start(bf16[1024,384]{1,0:T(8,128)(2,1)S(1)} %convolution_convert_fusion.11.q_ref) | copy-start | bytes 2359300
  125.0 20.6 %copy-start.3 = (s32[2560,128]{1,0:T(8,128)}, s32[2560,128]{1,0:T(8,128)S(1)}, u32[]{:S(2)}) copy-start(s32[2560,128]{1,0:T(8,128)S(1)} %broadcast_in_dim.105.kt_ref) | copy-start | bytes 3932164
  125.1 20.6 %copy-start.16 = (s32[8,1024]{1,0:T(8,128)}, s32[8,1024]{1,0:T(8,128)S(1)}, u32[]{:S(2)}) copy-start(s32[8,1024]{1,0:T(8,128)S(1)} %broadcast_in_dim.104.qt_ref) | copy-start | bytes 98308
  149.1 105.2 %copy-start.27 = (bf16[256,1536]{1,0:T(8,128)(2,1)S(1)}, bf16[256,1536]{1,0:T(8,128)(2,1)}, u32[]{:S(2)}) copy-start(bf16[256,1536]{1,0:T(8,128)(2,1)} %param.21) | copy-start | bytes 2359300
  254.7 14.9 %copy-start.32 = (bf16[256,1536]{1,0:T(8,128)(2,1)}, bf16[256,1536]{1,0:T(8,128)(2,1)S(1)}, u32[]{:S(2)}) copy-start(bf16[256,1536]{1,0:T(8,128)(2,1)S(1)} %get-tuple-element.161) | copy-start | bytes 2359300
  259.8 9.8 %slice-start.6 = ((s8[4718592]{0:T(1024)(128)(4,1)}), s8[4194304]{0:T(1024)(128)(4,1)S(1)}, s32[]{:S(2)}) async-start(s8[4718592]{0:T(1024)(128)(4,1)} %bitcast.123), calls=%async_computation.15 | async-start | bytes 8388608
  262.3 7.3 slice-start.7
  262.7 6.8 copy-start
  262.8 6.8 copy-start.1
  273.0 98.0 %copy-start.30 = (bf16[256,1536]{1,0:T(8,128)(2,1)S(1)}, bf16[256,1536]{1,0:T(8,128)(2,1)}, u32[]{:S(2)}) copy-start(bf16[256,1536]{1,0:T(8,128)(2,1)} %param.25) | copy-start | bytes 2359300
  373.7 93.6 %copy-start.31 = (bf16[256,1536]{1,0:T(8,128)(2,1)}, bf16[256,1536]{1,0:T(8,128)(2,1)S(1)}, u32[]{:S(2)}) copy-start(bf16[256,1536]{1,0:T(8,128)(2,1)S(1)} %get-tuple-element.157) | copy-start | bytes 2359300
  473.5 9.0 %copy-start.33 = (bf16[256,1536]{1,0:T(8,128)(2,1)S(1)}, bf16[256,1536]{1,0:T(8,128)(2,1)}, u32[]{:S(2)}) copy-start(bf16[256,1536]{1,0:T(8,128)(2,1)} %copy-done.32) | copy-start | bytes 2359300
  473.5 12.7 %slice-start.4 = ((s8[4718592]{0:T(1024)(128)(4,1)}), s8[524288]{0:T(1024)(128)(4,1)S(1)}, s32[]{:S(2)}) async-start(s8[4718592]{0:T(1024)(128)(4,1)} %bitcast.120), calls=%async_computation.13 | async-start | bytes 1048576
  491.7 290.2 %reduce-scatter.6.cloned.1.call-start = ((), (), s32[]{:S(2)}) async-start(), calls=%async_computation.6 | async-start | bytes 2654208 | tf_op jit(solution)/shard_map/reduce_scatter | solution.py:1533
  491.7 7.4 copy-start.38
  581.2 28.9 %copy-start.12 = (bf16[1024,384]{1,0:T(8,128)(2,1)S(1)}, bf16[1024,384]{1,0:T(8,128)(2,1)}, u32[]{:S(2)}) copy-start(bf16[1024,384]{1,0:T(8,128)(2,1)} %copy-done.11) | copy-start | bytes 2359300
  607.5 65.6 %collective-permute-start = (bf16[1024,768]{1,0:T(8,128)(2,1)}, bf16[1024,768]{1,0:T(8,128)(2,1)}, u32[]{:S(2)}, u32[]{:S(2)}) collective-permute-start(bf16[1024,768]{1,0:T(8,128)(2,1)} %get-tuple-element.103), channel_id=1, source_target_pairs={{4,0},{8,4},{12,8},{16,12},{20,16},{24,20},{28,24},{5,1},{9,5},{13... | collective-permute-start | bytes 4718600 | tf_op jit(solution)/shard_map/ppermute | solution.py:1728
  608.8 64.3 %collective-permute-start.1 = (bf16[512,768]{1,0:T(8,128)(2,1)}, bf16[512,768]{1,0:T(8,128)(2,1)S(1)}, u32[]{:S(2)}, u32[]{:S(2)}) collective-permute-start(bf16[512,768]{1,0:T(8,128)(2,1)} %get-tuple-element.104), channel_id=1, source_target_pairs={{8,0},{12,4},{16,8},{20,12},{24,16},{28,20},{9,1},{13,5},{17,9},{2... | collective-permute-start | bytes 2359304 | tf_op jit(solution)/shard_map/ppermute | solution.py:1728
  674.8 148.1 %reduce-scatter.8.cloned.1.call-start = ((), (), s32[]{:S(2)}) async-start(), calls=%async_computation.7 | async-start | bytes 3981312 | tf_op jit(solution)/shard_map/reduce_scatter | solution.py:1533
  675.1 96.0 %copy-start.53 = (pred[4]{0:T(512)(128)(4,1)}, pred[4]{0:T(512)(128)(4,1)S(1)}, u32[]{:S(2)}) copy-start(pred[4]{0:T(512)(128)(4,1)S(1)} %iota_compare_fusion) | copy-start | bytes 16
  693.0 76.0 %copy-start.28 = (bf16[256,1536]{1,0:T(8,128)(2,1)S(1)}, bf16[256,1536]{1,0:T(8,128)(2,1)}, u32[]{:S(2)}) copy-start(bf16[256,1536]{1,0:T(8,128)(2,1)} %param.21) | copy-start | bytes 2359300
  781.8 36.3 %copy-start.52 = (pred[4]{0:T(512)(128)(4,1)S(1)}, pred[4]{0:T(512)(128)(4,1)}, u32[]{:S(2)}) copy-start(pred[4]{0:T(512)(128)(4,1)} %copy-done.51) | copy-start | bytes 16
  781.8 36.5 %copy-start.54 = (pred[4]{0:T(512)(128)(4,1)S(1)}, pred[4]{0:T(512)(128)(4,1)}, u32[]{:S(2)}) copy-start(pred[4]{0:T(512)(128)(4,1)} %copy-done.53) | copy-start | bytes 16
  (43 other events, 110.4 us)
Sparse Core Ops, SparseCore 0:
  13.2 69.0 all-gather.4
  86.7 70.5 all-gather.8
  159.2 64.5 all-gather.6
  491.8 127.1 reduce-scatter.3
  674.9 82.9 reduce-scatter.5
  761.6 57.6 reduce-scatter.7

commit v3 on v2

--- a/solution.py
+++ b/solution.py
@@ -9,6 +9,7 @@
 CLIP = 1500
 LANES = 128
 TILE = 256
+KEY_TILE = 512
 MESH = pl.DeviceIdType.MESH
 
 eps_norm = 1e-05
@@ -284,35 +285,56 @@
         self.parts = reach_parts(tokens, halo)
         self.ins, self.in_specs = [x], [ANY]
         self.outs, self.out_specs = [shape_of(x, (halo, width))], [ANY]
-        self.scratch = [dma(len(self.parts))] * 2
+        self.scratch = [dma(len(self.parts) + 1), dma(len(self.parts))]
+
+    def direct(self, target, i):
+        here = (target > i) & (target < self.n)
+        return here & (lax.rem(target, 2) == 0) if i == 1 else here
 
     def greet(self, barrier):
-        (row, col), n = place(), self.n
+        (row, col), n, count = place(), self.n, 0
         for i in range(len(self.parts)):
 
-            @pl.when(row >= i + 1)
+            @pl.when(self.direct(row, i))
             def _():
                 greet(barrier, lax.rem(row + n - i - 1, n), col)
 
-        return jnp.minimum(n - 1 - row, len(self.parts))
+            count = count + jnp.where(self.direct(row + i + 1, i), 1, 0)
+        return count
+
+    def spot(self, i):
+        return pl.ds(self.halo - sum(self.parts[: i + 1]), self.parts[i])
 
     def copy(self, refs, i):
         x, out, send, recv = refs
         (row, col), part = place(), self.parts[i]
         return push(
             x.at[pl.ds(self.tokens - part, part)],
-            out.at[pl.ds(self.halo - sum(self.parts[: i + 1]), part)],
+            out.at[self.spot(i)],
             send.at[i],
             recv.at[i],
             lax.rem(row + i + 1, self.n),
             col,
         )
 
+    def relay(self, refs):
+        out, send, recv = refs[1:]
+        row, col = place()
+        part = self.parts[1]
+        return push(
+            out.at[pl.ds(self.halo - part, part)],
+            out.at[self.spot(1)],
+            send.at[len(self.parts)],
+            recv.at[1],
+            lax.rem(row + 1, self.n),
+            col,
+        )
+
     def begin(self, refs):
         row = place()[0]
         for i in range(len(self.parts)):
 
-            @pl.when(row + i + 1 < self.n)
+            @pl.when(self.direct(row + i + 1, i))
             def _():
                 self.copy(refs, i).start()
 
@@ -320,16 +342,29 @@
         pass
 
     def end(self, refs):
-        row = place()[0]
+        row, n = place()[0], self.n
         for i in range(len(self.parts)):
 
             @pl.when(row >= i + 1)
             def _():
                 self.copy(refs, i).wait_recv()
 
-            @pl.when(row + i + 1 < self.n)
+            @pl.when(self.direct(row + i + 1, i))
             def _():
                 self.copy(refs, i).wait_send()
+
+            if i == 0 and len(self.parts) > 1:
+                relays = (row >= 2) & (lax.rem(row, 2) == 0)
+
+                @pl.when(relays)
+                def _():
+                    self.relay(refs).start()
+
+        if len(self.parts) > 1:
+
+            @pl.when(relays)
+            def _():
+                self.relay(refs).wait_send()
 
 
 class AllSum:
@@ -742,7 +777,7 @@
     return jnp.where((lane >= head * HD) & (lane < (head + 1) * HD), values, jnp.zeros_like(values))
 
 
-def key_bias(bias_ref, key_tags_ref, query_tags, tile, low, halo, index):
+def key_bias(bias_ref, key_tags_ref, query_tags, tile, low, last, halo, index):
     shape = (tile, query_tags.shape[1])
 
     def fill(t, carry):
@@ -754,13 +789,13 @@
         bias_ref[pl.ds(place, tile), :] = jnp.where(allowed, 0.0, masked_score)
         return carry
 
-    lax.fori_loop(low, halo // tile + index + 1, fill, 0)
+    lax.fori_loop(low, last + 1, fill, 0)
 
 
 def self_forward(queries, key_values, halo_key_values, query_tags, key_tags, lows):
     tokens, width = queries.shape
     halo = halo_key_values.shape[0]
-    tile = min(TILE, tokens)
+    tile, key_tile = min(TILE, tokens), min(KEY_TILE, tokens)
     blocks = tokens // tile
     window = halo + tokens
     heads = width // HD
@@ -777,8 +812,8 @@
             v_t[:, pl.ds(halo, tokens)] = kv_ref[:, width:].T
 
         low = low_ref[index]
-        last = halo // tile + index
-        key_bias(bias, kt_ref, qt_ref[0:1, :], tile, low, halo, index)
+        last = (halo + (index + 1) * tile - 1) // key_tile
+        key_bias(bias, kt_ref, qt_ref[0:1, :], key_tile, low, last, halo, index)
         parts = []
         for start, size, members in groups:
             q = (q_ref[:, start : start + size].astype(f32) * scale).astype(bf16)
@@ -786,11 +821,11 @@
 
         def step(back, carry):
             t = last - back
-            place = pl.multiple_of(t * tile, tile)
-            added = bias[pl.ds(place, tile), :]
+            place = pl.multiple_of(t * key_tile, key_tile)
+            added = bias[pl.ds(place, key_tile), :]
             new = []
             for start, size, members in groups:
-                keys = kv_all[pl.ds(place, tile), start : start + size]
+                keys = kv_all[pl.ds(place, key_tile), start : start + size]
                 for h in members:
                     head = start // HD + h
                     peak, total, mixed = carry[head]
@@ -799,7 +834,7 @@
                     weights = jnp.exp(scores - top)
                     fade = jnp.exp(peak - top)
                     total = total * fade + jnp.sum(weights, axis=0, keepdims=True)
-                    values_t = v_t[head * HD : (head + 1) * HD, pl.ds(place, tile)]
+                    values_t = v_t[head * HD : (head + 1) * HD, pl.ds(place, key_tile)]
                     mixed = mixed * fade + matmul(values_t, weights.astype(bf16))
                     new.append((top, total, mixed))
             return tuple(new)
@@ -855,7 +890,7 @@
 ):
     tokens, width = queries.shape
     halo = halo_key_values.shape[0]
-    tile = min(TILE, tokens)
+    tile, key_tile = min(TILE, tokens), min(KEY_TILE, tokens)
     blocks = tokens // tile
     window = halo + tokens
     heads = width // HD
@@ -888,8 +923,8 @@
             total[...] = jnp.zeros_like(total)
 
         low = low_ref[index]
-        last = halo // tile + index
-        key_bias(bias, kt_ref, qt_ref[0:1, :], tile, low, halo, index)
+        last = (halo + (index + 1) * tile - 1) // key_tile
+        key_bias(bias, kt_ref, qt_ref[0:1, :], key_tile, low, last, halo, index)
         held = []
         for start, size, members in groups:
             q = (q_ref[:, start : start + size].astype(f32) * scale).astype(bf16)
@@ -905,13 +940,13 @@
 
         def step(back, carry):
             t = last - back
-            place = pl.multiple_of(t * tile, tile)
-            added = bias[pl.ds(place, tile), :]
+            place = pl.multiple_of(t * key_tile, key_tile)
+            added = bias[pl.ds(place, key_tile), :]
             new = []
             for (start, size, members), own in zip(groups, held):
                 q_parts, g_parts, q_rows, g_rows, centres = own
-                keys = kv_all[pl.ds(place, tile), start : start + size]
-                values = kv_all[pl.ds(place, tile), width + start : width + start + size]
+                keys = kv_all[pl.ds(place, key_tile), start : start + size]
+                values = kv_all[pl.ds(place, key_tile), width + start : width + start + size]
                 all_weights, all_scores = [], []
                 for h in members:
                     head = start // HD + h
@@ -919,14 +954,14 @@
                     weights = jnp.exp(against(keys, q_parts[h]) + added - lse)
                     grads = weights * (against(values, g_parts[h]) - centres[h])
                     grads = grads.astype(bf16)
-                    keys_t = k_t[head * HD : (head + 1) * HD, pl.ds(place, tile)]
+                    keys_t = k_t[head * HD : (head + 1) * HD, pl.ds(place, key_tile)]
                     new.append(carry[head] + matmul(keys_t, grads))
                     all_weights.append(weights.astype(bf16))
                     all_scores.append(grads)
-                total[pl.ds(place, tile), start : start + size] += matmul(
+                total[pl.ds(place, key_tile), start : start + size] += matmul(
                     jnp.concatenate(all_scores, axis=1), q_rows
                 )
-                total[pl.ds(place, tile), width + start : width + start + size] += matmul(
+                total[pl.ds(place, key_tile), width + start : width + start + size] += matmul(
                     jnp.concatenate(all_weights, axis=1), g_rows
                 )
             return tuple(new)
@@ -1563,8 +1598,8 @@
     seg_count, text_rows = text_states.shape[:2]
     text = text_rows * rows
     hidden = expand_weight.shape[1]
-    tile = min(TILE, tokens)
-    halo = -(-(CLIP - 1) // tile) * tile
+    tile, key_tile = min(TILE, tokens), min(KEY_TILE, tokens)
+    halo = -(-(CLIP - 1) // key_tile) * key_tile
     half = rows // 2
     chip, parity = row // 2, row % 2
     aligned = width % LANES == 0
@@ -1602,17 +1637,16 @@
     key_tags = jnp.broadcast_to(key_tags[:, None], (halo + tokens, LANES))
     query_tags = jnp.broadcast_to(clip_ids[None, :] + 1, (8, tokens))
     first_clips = clip_ids[::tile]
-    lows = jnp.sum((window_clips[None, :] < first_clips[:, None]).astype(jnp.int32), axis=1) // tile
+    lows = jnp.sum((window_clips[None, :] < first_clips[:, None]).astype(jnp.int32), axis=1)
+    lows = lows // key_tile
 
     own_clips = lax.dynamic_slice_in_dim(clip_ids, col * own, own)
     own_valid = lax.dynamic_slice_in_dim(valid_mask, col * own, own).astype(f32)
     clip_rows = jnp.broadcast_to(own_clips[None, :], (8, own))
     ends = jnp.stack([own_clips[0], own_clips[-1]])
 
-    text_kv = matmul(text_full, text_weights).astype(bf16)
-    text_all = lax.all_gather(text_kv, ("row", "col"), axis=0)
-    reduce_full = row_gather(after(reduce_weight, text_kv).T)
-    key_values = matmul(after(wide_one, text_kv), kv_full).astype(bf16)
+    reduce_full = row_gather(after(reduce_weight, wide_one).T)
+    key_values = matmul(wide_one, kv_full).astype(bf16)
     queries = matmul(wide_one, query_full).astype(bf16)
     cross_local = (cross_query, cross_output.T)
     (halo_kv,), *cross_wide = exchange(
@@ -1621,8 +1655,10 @@
         HaloGather(key_values, halo, rows),
         *([ColWide(*cross_local, n=cols)] if aligned else []),
     )
+    text_kv = matmul(after(text_full, halo_kv), text_weights).astype(bf16)
+    text_all = lax.all_gather(text_kv, ("row", "col"), axis=0)
     attended_one, lse = self_forward(
-        queries, key_values, halo_kv, query_tags, key_tags, lows
+        after(queries, text_kv), key_values, halo_kv, query_tags, key_tags, lows
     )
     if aligned:
         cross_wide = cross_wide[0]

time: 832 us -> 832 us (level)
    pallas_call x1, Pallas kernels: 97.9 us -> 89.5 us  [feed_forward(): pl.pallas_call(kernel, out_shape=[jax.ShapeDtypeStruct((own, features), f...]
    unnamed x139 -> x147, local copies, waits for them, and re-layouts: 13.8 us -> 17.9 us
  transfers between devices with their start and end apart: 8 -> 8, of which waited for: 1 -> 1; matrix products, arithmetic and copies ran while one was open for 12% -> 11% of each run, Pallas kernels for 52% -> 49%
where the time goes in v3:
time: 832 us; the launch traced here: 827 us
  Pallas kernels  624 us (75%)
  matrix products  62.2 us (7%)
  other arithmetic  51.3 us (6%)
  waiting for transfers between devices  38.5 us (5%)
  local copies, waits for them, and re-layouts  29.7 us (4%)
  between operations  18 us (2%)
    pallas_call x6, Pallas kernels, exchange(): pl.pallas_call(kernel, out_shape=[out for job in jobs for out in job.outs...  373 us
    pallas_call x1, Pallas kernels, feed_forward_back(): pl.pallas_call(kernel, out_shape=[jax.ShapeDtypeStruct((own, features), f...  97.5 us
    pallas_call x1, Pallas kernels, feed_forward(): pl.pallas_call(kernel, out_shape=[jax.ShapeDtypeStruct((own, features), f...  89.5 us
    ppermute x2, waiting for transfers between devices, on_device(): lax.ppermute(x, 'row', [(r, r - i - 1) for r in range(i + 1, rows)])  37.7 us
    pallas_call x1, Pallas kernels, self_backward(): pl.pallas_call(kernel, out_shape=[jax.ShapeDtypeStruct((tokens, width), b...  27.8 us
    dot_general x6, matrix products, matmul(): return jnp.dot(left, right, preferred_element_type=f32)  23.1 us
    pallas_call x1, Pallas kernels, self_forward(): pl.pallas_call(kernel, out_shape=[jax.ShapeDtypeStruct((tokens, width), b...  21.1 us
    dot_general x6, matrix products, against(): lax.dot_general(left, right, (((1,), (1,)), ((), ())), preferred_element_...  19.7 us
  transfers between devices with their start and end apart: 8, of which 1 were waited for; matrix products, arithmetic and copies ran while one was open for 11% of the time, Pallas kernels for 49%

profile of v3, /device:TPU:0, one launch (start us, length us, event | category | flops | bytes accessed | tf_op | source)
XLA Modules:
  0.0 826.7 jit_solution(813515851126818843)
XLA Ops:
  14.2 67.8 %gather_one.1 = (bf16[4,256,1536]{2,1,0:T(8,128)(2,1)S(1)}, bf16[8,192,1536]{2,1,0:T(8,128)(2,1)}, s32[8,8,128]{2,1,0:T(8,128)S(1)}, bf16[64,1536]{1,0:T(8,128)(2,1)S(1)}) custom-call(bf16[256,1536]{1,0:T(8,128)(2,1)S(1)} %fusion.34.refs_0_, bf16[192,1536]{1,0:T(8,128)(2,1)S(1)} %copy-done.13, s32[8,128]{1,0:T(8,128)S(1)} %get-tuple-element.174.refs_2_, ...), custom_call_target="tpu_custom_call" | custom-call | flops 1048576 | bytes 1048576 | tf_op jit(solution)/shard_map/gather_one/pallas_call | solution.py:736
  83.6 5.3 fusion.22.refs_0_.kv_ref
  88.9 23.7 %gather_halo.1 = (bf16[1536,768]{1,0:T(8,128)(2,1)S(1)}, bf16[192,1536]{1,0:T(8,128)(2,1)S(1)}, bf16[192,1536]{1,0:T(8,128)(2,1)S(1)}) custom-call(bf16[1024,768]{1,0:T(8,128)(2,1)S(1)} %fusion.22.refs_0_.kv_ref, bf16[192,384]{1,0:T(8,128)(2,1)S(1)} %copy-done.18, bf16[192,384]{1,0:T(8,128)(2,1)S(1)} %bitcast.93), custom_call_target="tpu_custom_call" | custom-call | flops 1048576 | bytes 1048576 | tf_op jit(solution)/shard_map/gather_halo/pallas_call | solution.py:736
  113.9 2.8 fusion.50
  121.5 4.0 convolution_convert_fusion.11.q_ref
  125.9 21.1 %self_forward.1 = (bf16[1024,384]{1,0:T(8,128)(2,1)S(1)}, f32[8,1024]{1,0:T(8,128)S(1)}) custom-call(s32[4]{0:T(128)S(1)} %and_select_fusion.low_ref, bf16[1024,384]{1,0:T(8,128)(2,1)S(1)} %convolution_convert_fusion.11.q_ref, bf16[1024,768]{1,0:T(8,128)(2,1)S(1)} %fusion.22.refs_0_.kv_ref, bf16[1536,768]{1,0:T(8,128)(2,1)} %copy-done.4, ...), custom_call_target="tpu_custom_call" | custom-call | flops 1048576 | bytes 1048576 | tf_op jit(solution)/shard_map/self_forward/pallas_call | solution.py:856
  147.7 3.4 convolution_convert_fusion.3
  151.1 108.2 %scatter_one.1 = (f32[256,1536]{1,0:T(8,128)S(1)}, bf16[8,192,1536]{2,1,0:T(8,128)(2,1)}, bf16[8,192,1536]{2,1,0:T(8,128)(2,1)}) custom-call(bf16[4,256,1536]{2,1,0:T(8,128)(2,1)S(1)} %bitcast.88, bf16[192,1536]{1,0:T(8,128)(2,1)S(1)} %get-tuple-element.84.refs_1_, bf16[192,1536]{1,0:T(8,128)(2,1)S(1)} %get-tuple-element.85.refs_2_), custom_call_target="tpu_custom_call" | custom-call | flops 1048576 | bytes 1048576 | tf_op jit(solution)/shard_map/scatter_one/pallas_call | solution.py:736
  260.5 4.7 convolution_convert_fusion.9.q_ref
  265.2 2.5 copy.63
  268.9 6.1 cross_forward.1
  278.4 89.5 %feed_forward.1 = (f32[256,1536]{1,0:T(8,128)}, bf16[4,256,1536]{2,1,0:T(8,128)(2,1)}, bf16[4,256,1536]{2,1,0:T(8,128)(2,1)}, bf16[4,256,1536]{2,1,0:T(8,128)(2,1)}) custom-call(bf16[256,1536]{1,0:T(8,128)(2,1)} %add_convert_fusion.4.x_ref, bf16[1536,1536]{1,0:T(8,128)(2,1)} %bitcast.103, bf16[1536,1536]{1,0:T(8,128)(2,1)} %all-gather.7.cloned.1.call-done.reduce_ref), custom_call_target="tpu_custom_call" | custom-call | flops 1048576 | bytes 1048576 | tf_op jit(solution)/shard_map/feed_forward/pallas_call | solution.py:1365
  368.0 2.8 multiply_reduce_fusion
  371.9 97.5 %feed_forward_back.1 = (f32[256,1536]{1,0:T(8,128)}, bf16[4,192,1536]{2,1,0:T(8,128)(2,1)}, bf16[4,192,1536]{2,1,0:T(8,128)(2,1)}, bf16[4,192,1536]{2,1,0:T(8,128)(2,1)}, bf16[4,192,1536]{2,1,0:T(8,128)(2,1)}) custom-call(bf16[256,1536]{1,0:T(8,128)(2,1)} %fusion.42.g_ref, bf16[1536,1536]{1,0:T(8,128)(2,1)} %bitcast.104, ...), custom_call_target="tpu_custom_call" | custom-call | flops 1048576 | bytes 1048576 | tf_op jit(solution)/shard_map/feed_forward_back/pallas_call | solution.py:1526
  472.9 3.6 convolution_convert_fusion.1
  477.9 8.9 %cross_backward.1 = (bf16[256,1536]{1,0:T(8,128)(2,1)S(1)}, bf16[512,1536]{1,0:T(8,128)(2,1)S(1)}, bf16[512,1536]{1,0:T(8,128)(2,1)S(1)}) custom-call(s32[2]{0:T(128)S(1)} %pad_add_fusion.ends_ref, bf16[256,1536]{1,0:T(8,128)(2,1)S(1)} %copy-done.7, bf16[512,1536]{1,0:T(8,128)(2,1)} %bitcast.87, bf16[512,1536]{1,0:T(8,128)(2,1)} %bitcast.85, ...), custom_call_target="tpu_custom_call" | custom-call | flops 1048576 | bytes 1048576 | tf_op jit(solution)/shard_map/cross_backward/pallas_call | solution.py:1115
  486.9 3.7 convolution_convert_fusion.2
  490.6 2.7 fusion.31
  493.7 2.2 copy.57
  497.6 6.8 add_convert_fusion
  506.2 71.1 %gather_grad_one.1 = (bf16[4,256,1536]{2,1,0:T(8,128)(2,1)}, bf16[4,192,1536]{2,1,0:T(8,128)(2,1)S(1)}, bf16[4,192,1536]{2,1,0:T(8,128)(2,1)S(1)}, bf16[4,192,1536]{2,1,0:T(8,128)(2,1)}, bf16[4,192,1536]{2,1,0:T(8,128)(2,1)}) custom-call(bf16[256,1536]{1,0:T(8,128)(2,1)S(1)} %get-tuple-element.160.refs_0_, bf16[4,192,1536]{2,1,0:T(8,128)(2,1)} %get-tuple-element.181.refs_1_, ...), custom_call_target="tpu_custom_call" | custom-call | flops 1048576 | bytes 1048576 | tf_op jit(solution)/shard_map/gather_grad_one/pallas_call | solution.py:736
  577.3 4.9 convolution_convert_fusion.10.do_ref
  582.3 27.8 %self_backward.1 = (bf16[1024,384]{1,0:T(8,128)(2,1)}, f32[1024,768]{1,0:T(8,128)}, bf16[1024,768]{1,0:T(8,128)(2,1)}, bf16[512,768]{1,0:T(8,128)(2,1)}) custom-call(s32[4]{0:T(128)} %copy-done.22, bf16[1024,384]{1,0:T(8,128)(2,1)} %copy-done.5, bf16[1024,768]{1,0:T(8,128)(2,1)} %copy-done.2, bf16[1536,768]{1,0:T(8,128)(2,1)} %copy-done.4, ...), custom_call_target="tpu_custom_call" | custom-call | flops 1048576 | bytes 1048576 | tf_op jit(solution)/shard_map/self_backward/pallas_call | solution.py:980
  612.7 3.7 convolution_convert_fusion.7
  617.5 2.8 convert_add_fusion.6
  633.5 37.7 %collective-permute-done.1 = bf16[512,768]{1,0:T(8,128)(2,1)S(1)} collective-permute-done((bf16[512,768]{1,0:T(8,128)(2,1)}, bf16[512,768]{1,0:T(8,128)(2,1)S(1)}, u32[]{:S(2)}, u32[]{:S(2)}) %collective-permute-start.1) | collective-permute-done | bytes 786464 | tf_op jit(solution)/shard_map/ppermute | solution.py:1764
  673.3 3.1 add_convert_fusion.2
  677.0 5.8 convolution_convert_fusion
  682.8 8.6 %convolution_convert_fusion.4 = bf16[1024,1536]{1,0:T(8,128)(2,1)} fusion(bf16[1536,2304]{1,0:T(8,128)(2,1)} %all-gather.5.cloned.1.call-done, bf16[1024,768]{1,0:T(8,128)(2,1)S(1)} %add_convert_fusion.2, bf16[1024,384]{1,0:T(8,128)(2,1)} %get-tuple-element.103), kind=kOutput, calls=%fused_computation.14 | convolution fusion | flops 3630170112 | bytes 9043968 | tf_op jit(solution)/shard_map/dot_general | solution.py:30
  691.3 63.6 %scatter_grad_one.1 = (f32[256,1536]{1,0:T(8,128)S(1)}, bf16[4,192,1536]{2,1,0:T(8,128)(2,1)S(1)}, bf16[4,192,1536]{2,1,0:T(8,128)(2,1)}, bf16[4,192,384]{2,1,0:T(8,128)(2,1)S(1)}, bf16[4,64,384]{2,1,0:T(8,128)(2,1)S(1)}) custom-call(bf16[4,256,1536]{2,1,0:T(8,128)(2,1)} %bitcast.112, bf16[4,192,1536]{2,1,0:T(8,128)(2,1)} %fusion.1.refs_1_, ...), custom_call_target="tpu_custom_call" | custom-call | flops 1048576 | bytes 1048576 | tf_op jit(solution)/shard_map/scatter_grad_one/pallas_call | solution.py:736
  761.3 4.1 select_reduce_fusion
  770.4 38.7 %sum_small.1 = (f32[8,1536]{1,0:T(8,128)S(1)}, bf16[4,192,384]{2,1,0:T(8,128)(2,1)S(1)}, bf16[4,192,384]{2,1,0:T(8,128)(2,1)S(1)}, bf16[4,192,384]{2,1,0:T(8,128)(2,1)S(1)}) custom-call(f32[8,1536]{1,0:T(8,128)S(1)} %copy-done.17, bf16[4,192,384]{2,1,0:T(8,128)(2,1)S(1)} %fusion.49.refs_1_, bf16[192,1536]{1,0:T(8,128)(2,1)S(1)} %fusion.48.refs_2_, ...), custom_call_target="tpu_custom_call" | custom-call | flops 1048576 | bytes 1048576 | tf_op jit(solution)/shard_map/sum_small/pallas_call | solution.py:736
  (249 shorter events, 69.6 us)
Async XLA Ops:
  7.2 5.9 copy-start.25
  7.2 76.3 %all-gather.5.cloned.1.call-start = ((), (), s32[]{:S(2)}) async-start(), calls=%async_computation.3 | async-start | bytes 7962624 | tf_op jit(solution)/shard_map/all_gather | solution.py:1563
  13.1 252.1 %all-gather.9.cloned.1.call-start = ((), (), s32[]{:S(2)}) async-start(), calls=%async_computation.8 | async-start | bytes 3244032 | tf_op jit(solution)/shard_map/all_gather | solution.py:1659
  88.8 37.1 %copy-start.2 = (bf16[1024,768]{1,0:T(8,128)(2,1)}, bf16[1024,768]{1,0:T(8,128)(2,1)S(1)}, u32[]{:S(2)}) copy-start(bf16[1024,768]{1,0:T(8,128)(2,1)S(1)} %fusion.22.refs_0_.kv_ref) | copy-start | bytes 4718596
  116.8 161.7 %all-gather.7.cloned.1.call-start = ((), (), s32[]{:S(2)}) async-start(), calls=%async_computation.4 | async-start | bytes 5308416 | tf_op jit(solution)/shard_map/all_gather | solution.py:1563
  117.5 509.8 %reduce-scatter.4.cloned.1.call-start = ((), (), s32[]{:S(2)}) async-start(), calls=%async_computation.5 | async-start | bytes 3244032 | tf_op jit(solution)/shard_map/reduce_scatter | solution.py:1732
  119.1 497.3 %copy-start.55 = (pred[4]{0:T(512)(128)(4,1)}, pred[4]{0:T(512)(128)(4,1)S(1)}, u32[]{:S(2)}) copy-start(pred[4]{0:T(512)(128)(4,1)S(1)} %iota_compare_fusion.1) | copy-start | bytes 16
  125.5 21.6 %copy-start.5 = (bf16[1024,384]{1,0:T(8,128)(2,1)}, bf16[1024,384]{1,0:T(8,128)(2,1)S(1)}, u32[]{:S(2)}) copy-start(bf16[1024,384]{1,0:T(8,128)(2,1)S(1)} %convolution_convert_fusion.11.q_ref) | copy-start | bytes 2359300
  125.9 21.2 %copy-start.3 = (s32[2560,128]{1,0:T(8,128)}, s32[2560,128]{1,0:T(8,128)S(1)}, u32[]{:S(2)}) copy-start(s32[2560,128]{1,0:T(8,128)S(1)} %broadcast_in_dim.105.kt_ref) | copy-start | bytes 3932164
  125.9 21.1 %copy-start.16 = (s32[8,1024]{1,0:T(8,128)}, s32[8,1024]{1,0:T(8,128)S(1)}, u32[]{:S(2)}) copy-start(s32[8,1024]{1,0:T(8,128)S(1)} %broadcast_in_dim.104.qt_ref) | copy-start | bytes 98308
  151.1 108.2 %copy-start.26 = (bf16[256,1536]{1,0:T(8,128)(2,1)S(1)}, bf16[256,1536]{1,0:T(8,128)(2,1)}, u32[]{:S(2)}) copy-start(bf16[256,1536]{1,0:T(8,128)(2,1)} %param.21) | copy-start | bytes 2359300
  265.2 9.8 %slice-start.6 = ((s8[4718592]{0:T(1024)(128)(4,1)}), s8[4194304]{0:T(1024)(128)(4,1)S(1)}, s32[]{:S(2)}) async-start(s8[4718592]{0:T(1024)(128)(4,1)} %bitcast.123), calls=%async_computation.15 | async-start | bytes 8388608
  267.7 7.2 slice-start.7
  268.2 6.8 copy-start
  268.2 6.8 copy-start.1
  268.9 6.1 copy-start.34
  278.4 89.6 %copy-start.31 = (bf16[256,1536]{1,0:T(8,128)(2,1)S(1)}, bf16[256,1536]{1,0:T(8,128)(2,1)}, u32[]{:S(2)}) copy-start(bf16[256,1536]{1,0:T(8,128)(2,1)} %param.25) | copy-start | bytes 2359300
  370.8 100.9 %copy-start.32 = (bf16[256,1536]{1,0:T(8,128)(2,1)}, bf16[256,1536]{1,0:T(8,128)(2,1)S(1)}, u32[]{:S(2)}) copy-start(bf16[256,1536]{1,0:T(8,128)(2,1)S(1)} %get-tuple-element.159) | copy-start | bytes 2359300
  477.9 9.0 %copy-start.35 = (bf16[256,1536]{1,0:T(8,128)(2,1)S(1)}, bf16[256,1536]{1,0:T(8,128)(2,1)}, u32[]{:S(2)}) copy-start(bf16[256,1536]{1,0:T(8,128)(2,1)} %copy-done.33) | copy-start | bytes 2359300
  477.9 12.7 %slice-start.4 = ((s8[4718592]{0:T(1024)(128)(4,1)}), s8[524288]{0:T(1024)(128)(4,1)S(1)}, s32[]{:S(2)}) async-start(s8[4718592]{0:T(1024)(128)(4,1)} %bitcast.120), calls=%async_computation.13 | async-start | bytes 1048576
  495.9 274.4 %reduce-scatter.6.cloned.1.call-start = ((), (), s32[]{:S(2)}) async-start(), calls=%async_computation.6 | async-start | bytes 2654208 | tf_op jit(solution)/shard_map/reduce_scatter | solution.py:1568
  497.6 6.8 copy-start.30
  497.6 6.8 copy-start.36
  497.6 6.8 copy-start.42
  582.3 30.4 %copy-start.12 = (bf16[1024,384]{1,0:T(8,128)(2,1)S(1)}, bf16[1024,384]{1,0:T(8,128)(2,1)}, u32[]{:S(2)}) copy-start(bf16[1024,384]{1,0:T(8,128)(2,1)} %copy-done.11) | copy-start | bytes 2359300
  610.1 61.1 %collective-permute-start = (bf16[1024,768]{1,0:T(8,128)(2,1)}, bf16[1024,768]{1,0:T(8,128)(2,1)}, u32[]{:S(2)}, u32[]{:S(2)}) collective-permute-start(bf16[1024,768]{1,0:T(8,128)(2,1)} %get-tuple-element.105), channel_id=1, source_target_pairs={{4,0},{8,4},{12,8},{16,12},{20,16},{24,20},{28,24},{5,1},{9,5},{13... | collective-permute-start | bytes 4718600 | tf_op jit(solution)/shard_map/ppermute | solution.py:1764
  611.4 59.8 %collective-permute-start.1 = (bf16[512,768]{1,0:T(8,128)(2,1)}, bf16[512,768]{1,0:T(8,128)(2,1)S(1)}, u32[]{:S(2)}, u32[]{:S(2)}) collective-permute-start(bf16[512,768]{1,0:T(8,128)(2,1)} %get-tuple-element.106), channel_id=1, source_target_pairs={{8,0},{12,4},{16,8},{20,12},{24,16},{28,20},{9,1},{13,5},{17,9},{2... | collective-permute-start | bytes 2359304 | tf_op jit(solution)/shard_map/ppermute | solution.py:1764
  672.9 143.6 %reduce-scatter.8.cloned.1.call-start = ((), (), s32[]{:S(2)}) async-start(), calls=%async_computation.7 | async-start | bytes 3981312 | tf_op jit(solution)/shard_map/reduce_scatter | solution.py:1568
  673.2 86.1 %copy-start.57 = (pred[4]{0:T(512)(128)(4,1)}, pred[4]{0:T(512)(128)(4,1)S(1)}, u32[]{:S(2)}) copy-start(pred[4]{0:T(512)(128)(4,1)S(1)} %iota_compare_fusion) | copy-start | bytes 16
  691.3 65.8 %copy-start.27 = (bf16[256,1536]{1,0:T(8,128)(2,1)S(1)}, bf16[256,1536]{1,0:T(8,128)(2,1)}, u32[]{:S(2)}) copy-start(bf16[256,1536]{1,0:T(8,128)(2,1)} %param.21) | copy-start | bytes 2359300
  770.4 41.4 %copy-start.56 = (pred[4]{0:T(512)(128)(4,1)S(1)}, pred[4]{0:T(512)(128)(4,1)}, u32[]{:S(2)}) copy-start(pred[4]{0:T(512)(128)(4,1)} %copy-done.55) | copy-start | bytes 16
  770.4 41.6 %copy-start.58 = (pred[4]{0:T(512)(128)(4,1)S(1)}, pred[4]{0:T(512)(128)(4,1)}, u32[]{:S(2)}) copy-start(pred[4]{0:T(512)(128)(4,1)} %copy-done.57) | copy-start | bytes 16
  (47 other events, 118.6 us)
Sparse Core Ops, SparseCore 0:
  13.2 69.0 all-gather.4
  116.9 65.2 all-gather.8
  184.1 72.3 all-gather.6
  496.1 128.8 reduce-scatter.3
  673.0 77.9 reduce-scatter.5
  754.8 56.7 reduce-scatter.7

commit v4 on v3

--- a/solution.py
+++ b/solution.py
@@ -8,7 +8,7 @@
 HD = 64
 CLIP = 1500
 LANES = 128
-TILE = 256
+TILE = 512
 KEY_TILE = 512
 MESH = pl.DeviceIdType.MESH
 
@@ -1396,7 +1396,7 @@
 def feed_forward_back(grad, expand, reduce, act, slope, wide, n, rows, collective_id):
     own, features = grad.shape
     hidden = expand.shape[1]
-    half, block, step_w = rows // 2, features // rows, TILE
+    half, block, step_w = rows // 2, features // rows, 256
     wide_shape, hidden_shape = (n, own, features), (n, own, hidden)
     step_h, step_f = chunk_of(hidden), chunk_of(features)
 

time: 832 us -> 811 us (0.975)
  Pallas kernels: 624 us -> 600 us
    pallas_call x6, Pallas kernels: 373 us -> 360 us  [exchange(): pl.pallas_call(kernel, out_shape=[out for job in jobs for out in job.outs...]
  transfers between devices with their start and end apart: 8 -> 8, of which waited for: 1 -> 3; matrix products, arithmetic and copies ran while one was open for 11% -> 12% of each run, Pallas kernels for 49% -> 48%
where the time goes in v4:
time: 811 us; the launch traced here: 802 us
  Pallas kernels  600 us (74%)
  matrix products  62 us (8%)
  other arithmetic  51.3 us (6%)
  waiting for transfers between devices  36.3 us (4%)
  local copies, waits for them, and re-layouts  30.4 us (4%)
  between operations  18.2 us (2%)
    pallas_call x6, Pallas kernels, exchange(): pl.pallas_call(kernel, out_shape=[out for job in jobs for out in job.outs...  360 us
    pallas_call x1, Pallas kernels, feed_forward(): pl.pallas_call(kernel, out_shape=[jax.ShapeDtypeStruct((own, features), f...  94.9 us
    pallas_call x1, Pallas kernels, feed_forward_back(): pl.pallas_call(kernel, out_shape=[jax.ShapeDtypeStruct((own, features), f...  90.2 us
    ppermute x2, waiting for transfers between devices, on_device(): lax.ppermute(x, 'row', [(r, r - i - 1) for r in range(i + 1, rows)])  31.5 us
    pallas_call x1, Pallas kernels, self_backward(): pl.pallas_call(kernel, out_shape=[jax.ShapeDtypeStruct((tokens, width), b...  24.9 us
    dot_general x6, matrix products, matmul(): return jnp.dot(left, right, preferred_element_type=f32)  23.1 us
    dot_general x6, matrix products, transposed(): lax.dot_general(left, right, (((0,), (0,)), ((), ())), preferred_element_...  19.5 us
    dot_general x6, matrix products, against(): lax.dot_general(left, right, (((1,), (1,)), ((), ())), preferred_element_...  19.4 us
  transfers between devices with their start and end apart: 8, of which 3 were waited for; matrix products, arithmetic and copies ran while one was open for 12% of the time, Pallas kernels for 48%

profile of v4, /device:TPU:0, one launch (start us, length us, event | category | flops | bytes accessed | tf_op | source)
XLA Modules:
  0.0 801.7 jit_solution(18312856756769162381)
XLA Ops:
  14.2 67.8 %gather_one.1 = (bf16[4,256,1536]{2,1,0:T(8,128)(2,1)S(1)}, bf16[8,192,1536]{2,1,0:T(8,128)(2,1)}, s32[8,8,128]{2,1,0:T(8,128)S(1)}, bf16[64,1536]{1,0:T(8,128)(2,1)S(1)}) custom-call(bf16[256,1536]{1,0:T(8,128)(2,1)S(1)} %fusion.34.refs_0_, bf16[192,1536]{1,0:T(8,128)(2,1)S(1)} %copy-done.13, s32[8,128]{1,0:T(8,128)S(1)} %get-tuple-element.174.refs_2_, ...), custom_call_target="tpu_custom_call" | custom-call | flops 1048576 | bytes 1048576 | tf_op jit(solution)/shard_map/gather_one/pallas_call | solution.py:736
  83.6 5.3 fusion.22.refs_0_.kv_ref
  88.9 23.7 %gather_halo.1 = (bf16[1536,768]{1,0:T(8,128)(2,1)S(1)}, bf16[192,1536]{1,0:T(8,128)(2,1)S(1)}, bf16[192,1536]{1,0:T(8,128)(2,1)S(1)}) custom-call(bf16[1024,768]{1,0:T(8,128)(2,1)S(1)} %fusion.22.refs_0_.kv_ref, bf16[192,384]{1,0:T(8,128)(2,1)S(1)} %copy-done.18, bf16[192,384]{1,0:T(8,128)(2,1)S(1)} %bitcast.93), custom_call_target="tpu_custom_call" | custom-call | flops 1048576 | bytes 1048576 | tf_op jit(solution)/shard_map/gather_halo/pallas_call | solution.py:736
  113.9 2.8 fusion.50
  121.5 4.0 convolution_convert_fusion.11.q_ref
  125.9 15.0 %self_forward.1 = (bf16[1024,384]{1,0:T(8,128)(2,1)S(1)}, f32[8,1024]{1,0:T(8,128)S(1)}) custom-call(s32[2]{0:T(128)S(1)} %and_select_fusion.low_ref, bf16[1024,384]{1,0:T(8,128)(2,1)S(1)} %convolution_convert_fusion.11.q_ref, bf16[1024,768]{1,0:T(8,128)(2,1)S(1)} %fusion.22.refs_0_.kv_ref, bf16[1536,768]{1,0:T(8,128)(2,1)} %copy-done.4, ...), custom_call_target="tpu_custom_call" | custom-call | flops 1048576 | bytes 1048576 | tf_op jit(solution)/shard_map/self_forward/pallas_call | solution.py:856
  141.6 3.4 convolution_convert_fusion.3
  145.0 84.5 %scatter_one.1 = (f32[256,1536]{1,0:T(8,128)S(1)}, bf16[8,192,1536]{2,1,0:T(8,128)(2,1)}, bf16[8,192,1536]{2,1,0:T(8,128)(2,1)}) custom-call(bf16[4,256,1536]{2,1,0:T(8,128)(2,1)S(1)} %bitcast.88, bf16[192,1536]{1,0:T(8,128)(2,1)S(1)} %get-tuple-element.84.refs_1_, bf16[192,1536]{1,0:T(8,128)(2,1)S(1)} %get-tuple-element.85.refs_2_), custom_call_target="tpu_custom_call" | custom-call | flops 1048576 | bytes 1048576 | tf_op jit(solution)/shard_map/scatter_one/pallas_call | solution.py:736
  230.7 4.7 convolution_convert_fusion.9.q_ref
  235.4 3.2 copy.63
  239.8 6.1 cross_forward.1
  249.3 3.4 all-gather.7.cloned.1.call-done.reduce_ref
  252.7 94.9 %feed_forward.1 = (f32[256,1536]{1,0:T(8,128)}, bf16[4,256,1536]{2,1,0:T(8,128)(2,1)}, bf16[4,256,1536]{2,1,0:T(8,128)(2,1)}, bf16[4,256,1536]{2,1,0:T(8,128)(2,1)}) custom-call(bf16[256,1536]{1,0:T(8,128)(2,1)} %add_convert_fusion.4.x_ref, bf16[1536,1536]{1,0:T(8,128)(2,1)} %bitcast.103, bf16[1536,1536]{1,0:T(8,128)(2,1)} %all-gather.7.cloned.1.call-done.reduce_ref), custom_call_target="tpu_custom_call" | custom-call | flops 1048576 | bytes 1048576 | tf_op jit(solution)/shard_map/feed_forward/pallas_call | solution.py:1365
  347.6 2.8 multiply_reduce_fusion
  351.5 90.2 %feed_forward_back.1 = (f32[256,1536]{1,0:T(8,128)}, bf16[4,192,1536]{2,1,0:T(8,128)(2,1)}, bf16[4,192,1536]{2,1,0:T(8,128)(2,1)}, bf16[4,192,1536]{2,1,0:T(8,128)(2,1)}, bf16[4,192,1536]{2,1,0:T(8,128)(2,1)}) custom-call(bf16[256,1536]{1,0:T(8,128)(2,1)} %fusion.42.g_ref, bf16[1536,1536]{1,0:T(8,128)(2,1)} %bitcast.104, ...), custom_call_target="tpu_custom_call" | custom-call | flops 1048576 | bytes 1048576 | tf_op jit(solution)/shard_map/feed_forward_back/pallas_call | solution.py:1526
  445.2 3.6 convolution_convert_fusion.1
  450.2 9.1 %cross_backward.1 = (bf16[256,1536]{1,0:T(8,128)(2,1)S(1)}, bf16[512,1536]{1,0:T(8,128)(2,1)S(1)}, bf16[512,1536]{1,0:T(8,128)(2,1)S(1)}) custom-call(s32[2]{0:T(128)S(1)} %pad_add_fusion.ends_ref, bf16[256,1536]{1,0:T(8,128)(2,1)S(1)} %copy-done.7, bf16[512,1536]{1,0:T(8,128)(2,1)} %bitcast.87, bf16[512,1536]{1,0:T(8,128)(2,1)} %bitcast.85, ...), custom_call_target="tpu_custom_call" | custom-call | flops 1048576 | bytes 1048576 | tf_op jit(solution)/shard_map/cross_backward/pallas_call | solution.py:1115
  459.4 3.7 convolution_convert_fusion.2
  463.1 2.7 fusion.31
  470.1 6.8 add_convert_fusion
  478.7 75.4 %gather_grad_one.1 = (bf16[4,256,1536]{2,1,0:T(8,128)(2,1)}, bf16[4,192,1536]{2,1,0:T(8,128)(2,1)S(1)}, bf16[4,192,1536]{2,1,0:T(8,128)(2,1)S(1)}, bf16[4,192,1536]{2,1,0:T(8,128)(2,1)}, bf16[4,192,1536]{2,1,0:T(8,128)(2,1)}) custom-call(bf16[256,1536]{1,0:T(8,128)(2,1)S(1)} %get-tuple-element.160.refs_0_, bf16[4,192,1536]{2,1,0:T(8,128)(2,1)} %get-tuple-element.181.refs_1_, ...), custom_call_target="tpu_custom_call" | custom-call | flops 1048576 | bytes 1048576 | tf_op jit(solution)/shard_map/gather_grad_one/pallas_call | solution.py:736
  554.1 5.0 convolution_convert_fusion.10.do_ref
  559.1 24.9 %self_backward.1 = (bf16[1024,384]{1,0:T(8,128)(2,1)}, f32[1024,768]{1,0:T(8,128)}, bf16[1024,768]{1,0:T(8,128)(2,1)}, bf16[512,768]{1,0:T(8,128)(2,1)}) custom-call(s32[2]{0:T(128)} %copy-done.22, bf16[1024,384]{1,0:T(8,128)(2,1)} %copy-done.5, bf16[1024,768]{1,0:T(8,128)(2,1)} %copy-done.2, bf16[1536,768]{1,0:T(8,128)(2,1)} %copy-done.4, ...), custom_call_target="tpu_custom_call" | custom-call | flops 1048576 | bytes 1048576 | tf_op jit(solution)/shard_map/self_backward/pallas_call | solution.py:980
  586.8 3.7 convolution_convert_fusion.7
  591.6 2.7 convert_add_fusion.6
  608.2 31.5 %collective-permute-done.1 = bf16[512,768]{1,0:T(8,128)(2,1)S(1)} collective-permute-done((bf16[512,768]{1,0:T(8,128)(2,1)}, bf16[512,768]{1,0:T(8,128)(2,1)S(1)}, u32[]{:S(2)}, u32[]{:S(2)}) %collective-permute-start.1) | collective-permute-done | bytes 786464 | tf_op jit(solution)/shard_map/ppermute | solution.py:1764
  641.6 3.1 add_convert_fusion.2
  645.3 5.8 convolution_convert_fusion
  651.1 8.3 %convolution_convert_fusion.4 = bf16[1024,1536]{1,0:T(8,128)(2,1)} fusion(bf16[1536,2304]{1,0:T(8,128)(2,1)} %all-gather.5.cloned.1.call-done, bf16[1024,768]{1,0:T(8,128)(2,1)S(1)} %add_convert_fusion.2, bf16[1024,384]{1,0:T(8,128)(2,1)} %get-tuple-element.103), kind=kOutput, calls=%fused_computation.14 | convolution fusion | flops 3630170112 | bytes 9043968 | tf_op jit(solution)/shard_map/dot_general | solution.py:30
  659.4 76.0 %scatter_grad_one.1 = (f32[256,1536]{1,0:T(8,128)S(1)}, bf16[4,192,1536]{2,1,0:T(8,128)(2,1)S(1)}, bf16[4,192,1536]{2,1,0:T(8,128)(2,1)}, bf16[4,192,384]{2,1,0:T(8,128)(2,1)S(1)}, bf16[4,64,384]{2,1,0:T(8,128)(2,1)S(1)}) custom-call(bf16[4,256,1536]{2,1,0:T(8,128)(2,1)} %bitcast.112, bf16[4,192,1536]{2,1,0:T(8,128)(2,1)} %fusion.1.refs_1_, ...), custom_call_target="tpu_custom_call" | custom-call | flops 1048576 | bytes 1048576 | tf_op jit(solution)/shard_map/scatter_grad_one/pallas_call | solution.py:736
  741.8 4.1 select_reduce_fusion
  750.9 33.0 %sum_small.1 = (f32[8,1536]{1,0:T(8,128)S(1)}, bf16[4,192,384]{2,1,0:T(8,128)(2,1)S(1)}, bf16[4,192,384]{2,1,0:T(8,128)(2,1)S(1)}, bf16[4,192,384]{2,1,0:T(8,128)(2,1)S(1)}) custom-call(f32[8,1536]{1,0:T(8,128)S(1)} %copy-done.17, bf16[4,192,384]{2,1,0:T(8,128)(2,1)S(1)} %fusion.49.refs_1_, bf16[192,1536]{1,0:T(8,128)(2,1)S(1)} %fusion.48.refs_2_, ...), custom_call_target="tpu_custom_call" | custom-call | flops 1048576 | bytes 1048576 | tf_op jit(solution)/shard_map/sum_small/pallas_call | solution.py:736
  (249 shorter events, 72.6 us)
Async XLA Ops:
  7.2 5.9 copy-start.25
  7.2 76.3 %all-gather.5.cloned.1.call-start = ((), (), s32[]{:S(2)}) async-start(), calls=%async_computation.3 | async-start | bytes 7962624 | tf_op jit(solution)/shard_map/all_gather | solution.py:1563
  13.1 222.3 %all-gather.9.cloned.1.call-start = ((), (), s32[]{:S(2)}) async-start(), calls=%async_computation.8 | async-start | bytes 3244032 | tf_op jit(solution)/shard_map/all_gather | solution.py:1659
  88.8 37.1 %copy-start.2 = (bf16[1024,768]{1,0:T(8,128)(2,1)}, bf16[1024,768]{1,0:T(8,128)(2,1)S(1)}, u32[]{:S(2)}) copy-start(bf16[1024,768]{1,0:T(8,128)(2,1)S(1)} %fusion.22.refs_0_.kv_ref) | copy-start | bytes 4718596
  116.8 135.9 %all-gather.7.cloned.1.call-start = ((), (), s32[]{:S(2)}) async-start(), calls=%async_computation.4 | async-start | bytes 5308416 | tf_op jit(solution)/shard_map/all_gather | solution.py:1563
  117.5 484.5 %reduce-scatter.4.cloned.1.call-start = ((), (), s32[]{:S(2)}) async-start(), calls=%async_computation.5 | async-start | bytes 3244032 | tf_op jit(solution)/shard_map/reduce_scatter | solution.py:1732
  119.1 471.4 %copy-start.55 = (pred[4]{0:T(512)(128)(4,1)}, pred[4]{0:T(512)(128)(4,1)S(1)}, u32[]{:S(2)}) copy-start(pred[4]{0:T(512)(128)(4,1)S(1)} %iota_compare_fusion.1) | copy-start | bytes 16
  125.5 15.5 %copy-start.5 = (bf16[1024,384]{1,0:T(8,128)(2,1)}, bf16[1024,384]{1,0:T(8,128)(2,1)S(1)}, u32[]{:S(2)}) copy-start(bf16[1024,384]{1,0:T(8,128)(2,1)S(1)} %convolution_convert_fusion.11.q_ref) | copy-start | bytes 2359300
  125.9 15.1 %copy-start.3 = (s32[2560,128]{1,0:T(8,128)}, s32[2560,128]{1,0:T(8,128)S(1)}, u32[]{:S(2)}) copy-start(s32[2560,128]{1,0:T(8,128)S(1)} %broadcast_in_dim.105.kt_ref) | copy-start | bytes 3932164
  125.9 15.0 %copy-start.16 = (s32[8,1024]{1,0:T(8,128)}, s32[8,1024]{1,0:T(8,128)S(1)}, u32[]{:S(2)}) copy-start(s32[8,1024]{1,0:T(8,128)S(1)} %broadcast_in_dim.104.qt_ref) | copy-start | bytes 98308
  145.0 84.5 %copy-start.26 = (bf16[256,1536]{1,0:T(8,128)(2,1)S(1)}, bf16[256,1536]{1,0:T(8,128)(2,1)}, u32[]{:S(2)}) copy-start(bf16[256,1536]{1,0:T(8,128)(2,1)} %param.21) | copy-start | bytes 2359300
  235.4 10.5 %slice-start.6 = ((s8[4718592]{0:T(1024)(128)(4,1)}), s8[4194304]{0:T(1024)(128)(4,1)S(1)}, s32[]{:S(2)}) async-start(s8[4718592]{0:T(1024)(128)(4,1)} %bitcast.123), calls=%async_computation.15 | async-start | bytes 8388608
  238.6 7.2 slice-start.7
  239.1 6.8 copy-start
  239.1 6.8 copy-start.1
  239.8 6.1 copy-start.34
  252.7 94.9 %copy-start.31 = (bf16[256,1536]{1,0:T(8,128)(2,1)S(1)}, bf16[256,1536]{1,0:T(8,128)(2,1)}, u32[]{:S(2)}) copy-start(bf16[256,1536]{1,0:T(8,128)(2,1)} %param.25) | copy-start | bytes 2359300
  350.4 93.6 %copy-start.32 = (bf16[256,1536]{1,0:T(8,128)(2,1)}, bf16[256,1536]{1,0:T(8,128)(2,1)S(1)}, u32[]{:S(2)}) copy-start(bf16[256,1536]{1,0:T(8,128)(2,1)S(1)} %get-tuple-element.159) | copy-start | bytes 2359300
  450.2 9.2 %copy-start.35 = (bf16[256,1536]{1,0:T(8,128)(2,1)S(1)}, bf16[256,1536]{1,0:T(8,128)(2,1)}, u32[]{:S(2)}) copy-start(bf16[256,1536]{1,0:T(8,128)(2,1)} %copy-done.33) | copy-start | bytes 2359300
  450.2 12.9 %slice-start.4 = ((s8[4718592]{0:T(1024)(128)(4,1)}), s8[524288]{0:T(1024)(128)(4,1)S(1)}, s32[]{:S(2)}) async-start(s8[4718592]{0:T(1024)(128)(4,1)} %bitcast.120), calls=%async_computation.13 | async-start | bytes 1048576
  468.4 282.4 %reduce-scatter.6.cloned.1.call-start = ((), (), s32[]{:S(2)}) async-start(), calls=%async_computation.6 | async-start | bytes 2654208 | tf_op jit(solution)/shard_map/reduce_scatter | solution.py:1568
  470.1 6.8 copy-start.30
  470.1 6.8 copy-start.36
  470.1 6.8 copy-start.42
  559.1 27.7 %copy-start.12 = (bf16[1024,384]{1,0:T(8,128)(2,1)S(1)}, bf16[1024,384]{1,0:T(8,128)(2,1)}, u32[]{:S(2)}) copy-start(bf16[1024,384]{1,0:T(8,128)(2,1)} %copy-done.11) | copy-start | bytes 2359300
  584.0 55.7 %collective-permute-start = (bf16[1024,768]{1,0:T(8,128)(2,1)}, bf16[1024,768]{1,0:T(8,128)(2,1)}, u32[]{:S(2)}, u32[]{:S(2)}) collective-permute-start(bf16[1024,768]{1,0:T(8,128)(2,1)} %get-tuple-element.105), channel_id=1, source_target_pairs={{4,0},{8,4},{12,8},{16,12},{20,16},{24,20},{28,24},{5,1},{9,5},{13... | collective-permute-start | bytes 4718600 | tf_op jit(solution)/shard_map/ppermute | solution.py:1764
  585.3 54.4 %collective-permute-start.1 = (bf16[512,768]{1,0:T(8,128)(2,1)}, bf16[512,768]{1,0:T(8,128)(2,1)S(1)}, u32[]{:S(2)}, u32[]{:S(2)}) collective-permute-start(bf16[512,768]{1,0:T(8,128)(2,1)} %get-tuple-element.106), channel_id=1, source_target_pairs={{8,0},{12,4},{16,8},{20,12},{24,16},{28,20},{9,1},{13,5},{17,9},{2... | collective-permute-start | bytes 2359304 | tf_op jit(solution)/shard_map/ppermute | solution.py:1764
  641.4 149.9 %reduce-scatter.8.cloned.1.call-start = ((), (), s32[]{:S(2)}) async-start(), calls=%async_computation.7 | async-start | bytes 3981312 | tf_op jit(solution)/shard_map/reduce_scatter | solution.py:1568
  641.5 98.3 %copy-start.57 = (pred[4]{0:T(512)(128)(4,1)}, pred[4]{0:T(512)(128)(4,1)S(1)}, u32[]{:S(2)}) copy-start(pred[4]{0:T(512)(128)(4,1)S(1)} %iota_compare_fusion) | copy-start | bytes 16
  659.4 78.3 %copy-start.27 = (bf16[256,1536]{1,0:T(8,128)(2,1)S(1)}, bf16[256,1536]{1,0:T(8,128)(2,1)}, u32[]{:S(2)}) copy-start(bf16[256,1536]{1,0:T(8,128)(2,1)} %param.21) | copy-start | bytes 2359300
  750.8 35.7 %copy-start.56 = (pred[4]{0:T(512)(128)(4,1)S(1)}, pred[4]{0:T(512)(128)(4,1)}, u32[]{:S(2)}) copy-start(pred[4]{0:T(512)(128)(4,1)} %copy-done.55) | copy-start | bytes 16
  750.8 35.9 %copy-start.58 = (pred[4]{0:T(512)(128)(4,1)S(1)}, pred[4]{0:T(512)(128)(4,1)}, u32[]{:S(2)}) copy-start(pred[4]{0:T(512)(128)(4,1)} %copy-done.57) | copy-start | bytes 16
  (47 other events, 118.4 us)
Sparse Core Ops, SparseCore 0:
  13.2 69.0 all-gather.4
  116.9 89.4 all-gather.8
  208.3 44.3 all-gather.6
  468.5 133.4 reduce-scatter.3
  641.5 86.3 reduce-scatter.5
  731.7 56.6 reduce-scatter.7
